TPU v7x, 768 devices: a whole 4x8x12 slice. The times are simulated.
768 devices in a mesh: slab: 24 (over z_lo, x), angle: 32 (over z_hi, y, core).
Axes of the slice: x: 4, y: 8, z: 12 (z_hi: 2, z_lo: 6; z = z_hi * 6 + z_lo), core: 2. Of those that a mesh axis runs over, the one named last changes fastest.
Arguments:
- volume: bfloat16 [192, 128, 2048], P('slab', 'angle'), may hold values from -6 to 6
- measured: float32 [32, 192, 2048], P('angle', 'slab'), may hold values from -6 to 6
- ray_tiles: bfloat16 [32, 128, 2, 128, 128], P(None, 'angle'), may hold values from -0.03125 to 0.03125
- tile_offsets: int32 [32, 128], replicated, may hold values from -3 to 3
- band_counts: int32 [32, 128], replicated, may hold values from 1 to 2
Outputs:
- updated: float32 [192, 128, 2048], P('slab', 'angle')
- residual: float32 [32, 192, 2048], P('angle', 'slab')
All inputs are finite; a program needn't handle non-finite values.
Results may differ from a plain program's by a relative error of at most 0.00056.
Values may be sent and summed in bfloat16 or wider, within the bound.
No kernel may reach another device: no remote copies, remote signals or barrier semaphores. Data moves between devices by JAX's collectives and lax.ppermute only.
A program may use at most 64 MiB of HBM per device.

v0:
```python
from functools import partial

import jax
import jax.numpy as jnp
from jax import lax
from jax.sharding import PartitionSpec as P

OFFMAX = 3


step_size = 0.3
smooth_weight = 0.2
smooth_floor = 0.25


def padded_2(shard, sides, width):
    for axis, dim in sides:
        size, length = (lax.axis_size(axis), shard.shape[dim])
        up = [(i, (i + 1) % size) for i in range(size - 1)]
        down = [(j, i) for i, j in up]
        last = lax.slice_in_dim(shard, length - width, length, axis=dim)
        initial = lax.slice_in_dim(shard, 0, width, axis=dim)
        before = lax.ppermute(last, axis, up)
        after = lax.ppermute(initial, axis, down)
        shard = jnp.concatenate([before, shard, after], axis=dim)
    return shard


def shift_table(tile_offsets, band_counts, band):
    center = band // 2
    shifts = jnp.stack([tile_offsets + (k - center) for k in range(band)], axis=1)
    masks = jnp.stack([band_counts > k for k in range(band)], axis=1).astype(jnp.bfloat16)
    return (shifts, masks)


def project_angle(padded, shifts, masks, tiles, margin):
    tile_count = padded.shape[2] - 2 * margin
    summed = jnp.zeros((padded.shape[0], tile_count, padded.shape[3]), jnp.float32)
    for k in range(tiles.shape[1]):
        moved = jax.vmap(
            lambda block, offset: lax.dynamic_slice_in_dim(block, margin + offset, tile_count, 1),
            in_axes=(1, 0),
            out_axes=1,
        )(padded, shifts[k])
        moved = moved * masks[k][None, :, None, None]
        summed = summed + jnp.einsum(
            "zrtc,rcd->ztd", moved, tiles[:, k], preferred_element_type=jnp.float32
        )
    return summed.reshape(padded.shape[0], tile_count * padded.shape[3])


def spread_angle(view_pad, shifts, masks, tiles, margin):
    tile_count = view_pad.shape[1] - 2 * margin
    rows_here = shifts.shape[1]
    summed = jnp.zeros((view_pad.shape[0], rows_here, tile_count, view_pad.shape[2]), jnp.float32)
    for k in range(tiles.shape[1]):
        moved = jax.vmap(
            lambda offset: lax.dynamic_slice_in_dim(view_pad, margin - offset, tile_count, 1),
            out_axes=1,
        )(shifts[k])
        product = jnp.einsum(
            "zrtd,rcd->zrtc", moved, tiles[:, k], preferred_element_type=jnp.float32
        )
        summed = summed + product * masks[k].astype(jnp.float32)[None, :, None, None]
    return summed.reshape(view_pad.shape[0], rows_here, tile_count * view_pad.shape[2])


def divergence(field):
    base = field[:-1, :-1, :-1]
    step_z = field[1:, :-1, :-1] - base
    step_y = field[:-1, 1:, :-1] - base
    step_x = field[:-1, :-1, 1:] - base
    scale = jnp.sqrt(step_z * step_z + step_y * step_y + step_x * step_x + smooth_floor)
    flow_z = step_z / scale
    flow_y = step_y / scale
    flow_x = step_x / scale
    result = flow_z[1:, 1:, 1:] - flow_z[:-1, 1:, 1:]
    result = result + flow_y[1:, 1:, 1:] - flow_y[1:, :-1, 1:]
    return result + flow_x[1:, 1:, 1:] - flow_x[1:, 1:, :-1]


def per_device(volume, measured, ray_tiles, tile_offsets, band_counts):
    depth, row_count, width = volume.shape
    band = ray_tiles.shape[2]
    tile = ray_tiles.shape[3]
    margin = OFFMAX + band
    tile_count = width // tile
    angle_dev = measured.shape[0]
    first_angle = lax.axis_index("angle") * angle_dev
    first_row = lax.axis_index("angle") * row_count
    shifts, masks = shift_table(tile_offsets, band_counts, band)
    row_shifts = lax.dynamic_slice_in_dim(shifts, first_row, row_count, 2)
    row_masks = lax.dynamic_slice_in_dim(masks, first_row, row_count, 2)
    blocks = volume.reshape(depth, row_count, tile_count, tile)
    padded = jnp.pad(blocks, ((0, 0), (0, 0), (margin, margin), (0, 0)))
    sub_shift = row_shifts
    sub_mask = row_masks
    sub_tiles = ray_tiles
    full_views = lax.psum(
        jax.vmap(partial(project_angle, margin=margin), in_axes=(None, 0, 0, 0))(
            padded, sub_shift, sub_mask, sub_tiles
        ),
        "angle",
    )
    measured_all = lax.all_gather(measured, "angle", axis=0, tiled=True)
    residual_all = full_views - measured_all
    residual = lax.dynamic_slice_in_dim(residual_all, first_angle, angle_dev, 0)
    rounded_all = residual_all.astype(jnp.bfloat16)
    count = rounded_all.shape[0]
    sub_shift = row_shifts
    sub_mask = row_masks
    sub_tiles = ray_tiles
    view_blocks = rounded_all.reshape(count, rounded_all.shape[1], tile_count, tile)
    view_pad = jnp.pad(view_blocks, ((0, 0), (0, 0), (margin, margin), (0, 0)))
    spread = jax.vmap(partial(spread_angle, margin=margin))(
        view_pad, sub_shift, sub_mask, sub_tiles
    )
    gradient = jnp.sum(spread, axis=0)
    beside_all = padded_2(volume, (("slab", 0), ("angle", 1)), 1)
    field = jnp.pad(beside_all.astype(jnp.float32), ((0, 0), (0, 0), (1, 1)))
    updated = (
        volume.astype(jnp.float32)
        - step_size * gradient
        + step_size * smooth_weight * divergence(field)
    )
    return (updated, residual)


def solution(mesh):
    return jax.shard_map(
        per_device,
        mesh=mesh,
        in_specs=(
            P("slab", "angle", None),
            P("angle", "slab", None),
            P(None, "angle", None, None, None),
            P(),
            P(),
        ),
        out_specs=(P("slab", "angle", None), P("angle", "slab", None)),
        check_vma=False,
    )
```

profile of v0, /device:TPU:1, one launch (start us, length us, event | category | flops | bytes accessed | tf_op | source)
XLA Modules:
  0.0 612.4 jit_solution(13232436896485173337)
XLA Ops:
  7.2 0.7 add_bitcast_fusion
  7.9 0.8 dynamic-slice_add_fusion
  8.7 0.1 copy.138
  8.9 0.1 copy.116
  9.0 0.1 reshape.154
  9.1 1.0 reshape.176
  10.1 0.1 copy.109
  10.2 0.7 compare_bitcast_fusion.1
  11.0 0.1 fusion.40
  11.0 0.1 copy.117
  11.1 0.1 copy.118
  11.2 0.1 copy.111
  11.3 0.1 reshape.148
  11.5 3.8 gather_fusion.1
  15.3 3.8 gather_fusion
  19.1 0.1 copy.112
  19.2 0.1 copy.113
  19.3 4.9 fusion.4
  24.2 3.2 bitcast_add_fusion
  27.5 1.5 reshape.146
  29.1 0.7 all-gather.2.cloned.1.call-update
  29.8 3.9 collective-permute-start
  33.7 1.3 collective-permute-start.1
  35.1 3.1 collective-permute-done.1
  38.2 0.1 fusion.53
  38.4 5.2 collective-permute-start.2
  43.6 7.2 %collective-permute-start.3 = (bf16[10,1,2048]{2,1,0:T(2,128)(2,1)S(1)}, bf16[10,1,2048]{2,1,0:T(2,128)(2,1)S(1)}, u32[]{:S(2)}, u32[]{:S(2)}) collective-permute-start(bf16[10,1,2048]{2,1,0:T(2,128)(2,1)S(1)} %get-tuple-element.9), channel_id=1, source_target_pairs={{1,0},{2,1},{3,2},{4,3},{5,4},{6,5},{7,6},{8,7},{9,8},{10,9},{11,1... | collective-permute-start | bytes 122888 | tf_op jit(solution)/shard_map/ppermute | solution.py:24
  50.8 0.1 copy.125
  50.9 0.1 reshape.166
  51.0 0.1 copy.122
  51.1 0.1 reshape.160
  51.2 0.1 copy.124
  51.3 0.1 copy.127
  51.4 0.1 collective-permute-done.3
  51.5 0.5 fusion.34
  52.0 0.5 fusion.37
  52.5 1.1 fusion.38
  53.6 406.5 %all-reduce.5.cloned.1.call-done = f32[32,8,2048]{2,1,0:T(8,128)} async-done(((f32[32,8,2048]{2,1,0:T(8,128)}), f32[32,8,2048]{2,1,0:T(8,128)}) %all-reduce.5.cloned.1.call-update) | async-done | bytes 2097168 | tf_op jit(solution)/shard_map/psum | solution.py:99
  460.1 111.5 %all-gather.2.cloned.1.call-done = f32[32,8,2048]{2,1,0:T(8,128)} async-done(((f32[1,8,2048]{2,1,0:T(8,128)}), f32[32,8,2048]{2,1,0:T(8,128)}) %all-gather.2.cloned.1.call-update) | async-done | bytes 2097168 | tf_op jit(solution)/shard_map/all_gather | solution.py:105
  571.6 4.0 convert_bitcast_fusion
  575.6 0.3 copy.167
  575.9 0.2 pad.16
  576.1 3.9 gather_fusion.3
  580.0 9.7 %fusion = f32[32,4,8,16,128]{4,3,2,1,0:T(8,128)} fusion(bf16[32,4,8,16,128]{4,2,3,1,0:T(8,128)(2,1)} %bitcast.106, bf16[32,4,2,128,128]{4,3,2,1,0:T(8,128)(2,1)} %param.7), kind=kOutput, calls=%fused_computation.5 | convolution fusion | flops 536870912 | bytes 16777216 | tf_op jit(solution)/shard_map/vmap(zrtd,rcd->zrtc)/dot_general | solution.py:61
  589.7 3.9 gather_fusion.2
  593.6 9.0 %add_reduce_fusion = f32[4,8,16,128]{3,2,1,0:T(8,128)S(1)} fusion(f32[32,4,8,16,128]{4,3,2,1,0:T(8,128)} %fusion, f32[32,4]{1,0:T(8,128)S(1)} %copy.127, f32[32,4]{1,0:T(8,128)S(1)} %copy.124, bf16[32,4,2,128,128]{4,3,2,1,0:T(8,128)(2,1)} %param.7, bf16[32,4,8,16,128]{4,2,3,1,0:T(8,128)(2,1)} %bitcast.109), kind=kOutput, calls=%fused_computation.4 | convolution fusion | flops 545193984 | bytes 17040384 | tf_op jit(solution)/shard_map/vmap(zrtd,rcd->zrtc)/dot_general | solution.py:61
  602.6 1.5 constant_dynamic-slice_fusion
  604.1 1.5 fusion.36
  (24 shorter events, 0.4 us)
Async XLA Ops:
  7.2 453.0 %all-reduce.5.cloned.1.call-start = ((), (), s32[]{:S(2)}) async-start(), calls=%async_computation | async-start | bytes 4194304 | tf_op jit(solution)/shard_map/psum | solution.py:99
  19.3 4.9 copy-start
  27.5 2.3 copy-start.2
  29.0 542.5 %all-gather.2.cloned.1.call-start = ((), (), s32[]{:S(2)}) async-start(), calls=%async_computation.1 | async-start | bytes 2162688 | tf_op jit(solution)/shard_map/all_gather | solution.py:105
  29.8 5.2 collective-permute-start
  33.7 4.5 collective-permute-start.1
  38.4 13.0 %collective-permute-start.2 = (bf16[10,1,2048]{2,1,0:T(2,128)(2,1)S(1)}, bf16[10,1,2048]{2,1,0:T(2,128)(2,1)S(1)}, u32[]{:S(2)}, u32[]{:S(2)}) collective-permute-start(bf16[10,1,2048]{2,1,0:T(2,128)(2,1)S(1)} %get-tuple-element.8), channel_id=1, source_target_pairs={{0,1},{1,2},{2,3},{3,4},{4,5},{5,6},{6,7},{7,8},{8,9},{9,10},{10,1... | collective-permute-start | bytes 122888 | tf_op jit(solution)/shard_map/ppermute | solution.py:23
  43.6 7.9 %collective-permute-start.3 = (bf16[10,1,2048]{2,1,0:T(2,128)(2,1)S(1)}, bf16[10,1,2048]{2,1,0:T(2,128)(2,1)S(1)}, u32[]{:S(2)}, u32[]{:S(2)}) collective-permute-start(bf16[10,1,2048]{2,1,0:T(2,128)(2,1)S(1)} %get-tuple-element.9), channel_id=1, source_target_pairs={{1,0},{2,1},{3,2},{4,3},{5,4},{6,5},{7,6},{8,7},{9,8},{10,9},{11,1... | collective-permute-start | bytes 122888 | tf_op jit(solution)/shard_map/ppermute | solution.py:24
  593.6 10.5 %copy-start.1 = (f32[9,5,2049]{2,1,0:T(8,128)S(1)}, f32[9,5,2049]{2,1,0:T(8,128)}, u32[]{:S(2)}) copy-start(f32[9,5,2049]{2,1,0:T(8,128)} %get-tuple-element.7) | copy-start | bytes 1106464
Sparse Core Ops, SparseCore 0:
  29.2 430.9 all-reduce.4
  464.7 106.8 all-gather.1
where the time goes:
time: 613 us; the launch traced here: 612 us
  waiting for transfers between devices  522 us (85%)
  matrix products  26.9 us (4%)
  local copies, waits for them, and re-layouts  21.8 us (4%)
  starting transfers between devices  17.7 us (3%)
  between operations  14.3 us (2%)
  other arithmetic  9.95 us (2%)
    psum x1, waiting for transfers between devices, per_device(): lax.psum(jax.vmap(partial(project_angle, margin=margin), in_axes=(None, 0...  407 us
    all_gather x1, waiting for transfers between devices, per_device(): measured_all = lax.all_gather(measured, 'angle', axis=0, tiled=True)  111 us
    dot_general x2, matrix products, spread_angle(): jnp.einsum('zrtd,rcd->zrtc', moved, tiles[:, k], preferred_element_type=j...  18.7 us
  transfers between devices with their start and end apart: 6, of which 4 were waited for; matrix products, arithmetic and copies ran while one was open for 0% of the time, Pallas kernels for 0%

commit v1 on v0

v1 whole, which is shorter than its diff:
```python
from functools import partial

import jax
import jax.numpy as jnp
from jax import lax
from jax.experimental import pallas as pl
from jax.experimental.pallas import tpu as pltpu
from jax.sharding import Mesh, PartitionSpec as P

OFFMAX = 3

step_size = 0.3
smooth_weight = 0.2
smooth_floor = 0.25

ZHI, YS, CORES = 2, 8, 2
SLAB = ("zlo", "x")
ANGLE = ("zhi", "y", "core")

PAIR_SCALE = 2.0**6
PLANE_SCALE = 2.0**3


def padded_2(shard, sides, width):
    for axis, dim in sides:
        size, length = (lax.axis_size(axis), shard.shape[dim])
        up = [(i, (i + 1) % size) for i in range(size - 1)]
        down = [(j, i) for i, j in up]
        last = lax.slice_in_dim(shard, length - width, length, axis=dim)
        initial = lax.slice_in_dim(shard, 0, width, axis=dim)
        before = lax.ppermute(last, axis, up)
        after = lax.ppermute(initial, axis, down)
        shard = jnp.concatenate([before, shard, after], axis=dim)
    return shard


def divergence(field):
    base = field[:-1, :-1, :-1]
    step_z = field[1:, :-1, :-1] - base
    step_y = field[:-1, 1:, :-1] - base
    step_x = field[:-1, :-1, 1:] - base
    scale = jnp.sqrt(step_z * step_z + step_y * step_y + step_x * step_x + smooth_floor)
    flow_z = step_z / scale
    flow_y = step_y / scale
    flow_x = step_x / scale
    result = flow_z[1:, 1:, 1:] - flow_z[:-1, 1:, 1:]
    result = result + flow_y[1:, 1:, 1:] - flow_y[1:, :-1, 1:]
    return result + flow_x[1:, 1:, 1:] - flow_x[1:, 1:, :-1]


PAD = 4


def window_start(tile, copy_rows):
    return tile * 8 + (tile & 1) * (copy_rows - 8)


def band_windows(offset, count, sign, copy_rows):
    first = PAD + sign * (offset - 1)
    second = first + sign
    second_row = jnp.where(count > 1, window_start(second, copy_rows), 2 * copy_rows)
    return [pl.multiple_of(start, 16) for start in (window_start(first, copy_rows), second_row)]


def fill_windows(ref, index, block):
    rows = block.shape[0]
    wide = block.astype(jnp.float32)
    zero = lambda n: jnp.zeros((n, wide.shape[1]), jnp.float32)
    copy_rows = rows + 16 * PAD
    ref[index, :copy_rows] = jnp.concatenate([zero(8 * PAD), wide, zero(8 * PAD)], 0).astype(ref.dtype)
    ref[index, copy_rows : 2 * copy_rows] = jnp.concatenate(
        [zero(8 * (PAD - 1)), wide, zero(8 * (PAD + 1))], 0
    ).astype(ref.dtype)


def project_kernel(place, offsets, counts, volume, tiles, out, windows, *, scale):
    per_step = tiles.shape[1]
    rows, band = tiles.shape[3], tiles.shape[4]
    count = volume.shape[1]
    step = pl.program_id(0)

    @pl.when(step == 0)
    def _():
        for r in range(rows):
            fill_windows(windows, r, volume[r])
            windows[r, 2 * (count + 16 * PAD) :] = jnp.zeros((count, windows.shape[2]), windows.dtype)

    for i in range(per_step):
        for zh in range(ZHI):
            angle = (zh * YS + step * per_step + i) * CORES + place[0]
            pieces = []
            for r in range(rows):
                row = place[1] + r
                for start in band_windows(offsets[angle, row], counts[angle, row], 1, count + 16 * PAD):
                    pieces.append(windows[r, pl.ds(start, count), :])
            weights = tiles[zh, i, 0].reshape(rows * band * tiles.shape[5], tiles.shape[6])
            view = jnp.dot(jnp.concatenate(pieces, 1), weights, preferred_element_type=jnp.float32)
            out[i, zh] = (view * scale).astype(out.dtype)


def spread_kernel(place, offsets, counts, views, tiles, begin, out, windows):
    per_step = tiles.shape[1]
    rows = tiles.shape[3]
    count = views.shape[2]
    step = pl.program_id(0)

    @pl.when(step == 0)
    def _():
        for j in range(windows.shape[0]):
            windows[j, 2 * (count + 16 * PAD) :] = jnp.zeros((count, windows.shape[2]), windows.dtype)
        out[...] = begin[...]

    for i in range(per_step):
        for zh in range(ZHI):
            fill_windows(windows, i * ZHI + zh, views[i, zh])
    for r in range(rows):
        lhs, rhs = [], []
        for i in range(per_step):
            for zh in range(ZHI):
                angle = (zh * YS + step * per_step + i) * CORES + place[0]
                row = place[1] + r
                starts = band_windows(offsets[angle, row], counts[angle, row], -1, count + 16 * PAD)
                for k, start in enumerate(starts):
                    lhs.append(windows[i * ZHI + zh, pl.ds(start, count), :])
                    rhs.append(tiles[zh, i, 0, r, k])
        out[r] += lax.dot_general(
            jnp.concatenate(lhs, 1),
            jnp.concatenate(rhs, 1),
            (((1,), (1,)), ((), ())),
            preferred_element_type=jnp.float32,
        )


def tile_spec(tiles, per_step):
    return pl.BlockSpec(
        (ZHI, per_step, 1) + tiles.shape[3:], lambda i, place, offsets, counts: (0, i, place[0], 0, 0, 0, 0)
    )


def window_rows(count):
    return 3 * count + 32 * PAD


def project(place, offsets, counts, volume, tiles, dtype, scale, per_step=2):
    rows, count, lanes = volume.shape
    flops = 2 * ZHI * YS * count * lanes * tiles.shape[3] * tiles.shape[4] * lanes
    return pl.pallas_call(
        partial(project_kernel, scale=scale),
        grid_spec=pltpu.PrefetchScalarGridSpec(
            num_scalar_prefetch=3,
            grid=(YS // per_step,),
            in_specs=[
                pl.BlockSpec(volume.shape, lambda i, place, offsets, counts: (0, 0, 0)),
                tile_spec(tiles, per_step),
            ],
            out_specs=pl.BlockSpec((per_step, ZHI, count, lanes), lambda i, place, offsets, counts: (i, 0, 0, 0)),
            scratch_shapes=[pltpu.VMEM((rows, window_rows(count), lanes), jnp.bfloat16)],
        ),
        out_shape=jax.ShapeDtypeStruct((YS, ZHI, count, lanes), dtype),
        compiler_params=pltpu.CompilerParams(
            dimension_semantics=("arbitrary",), vmem_limit_bytes=16 << 20
        ),
        cost_estimate=pl.CostEstimate(flops=flops, bytes_accessed=tiles.size, transcendentals=0),
        name="project",
    )(place, offsets, counts, volume, tiles)


def spread(place, offsets, counts, views, tiles, begin, per_step=2):
    rows, count, lanes = begin.shape
    flops = 2 * ZHI * YS * count * lanes * tiles.shape[3] * tiles.shape[4] * lanes
    return pl.pallas_call(
        spread_kernel,
        grid_spec=pltpu.PrefetchScalarGridSpec(
            num_scalar_prefetch=3,
            grid=(YS // per_step,),
            in_specs=[
                pl.BlockSpec((per_step, ZHI, count, lanes), lambda i, place, offsets, counts: (i, 0, 0, 0)),
                tile_spec(tiles, per_step),
                pl.BlockSpec(begin.shape, lambda i, place, offsets, counts: (0, 0, 0)),
            ],
            out_specs=pl.BlockSpec(begin.shape, lambda i, place, offsets, counts: (0, 0, 0)),
            scratch_shapes=[pltpu.VMEM((per_step * ZHI, window_rows(count), lanes), jnp.bfloat16)],
        ),
        out_shape=jax.ShapeDtypeStruct(begin.shape, jnp.float32),
        compiler_params=pltpu.CompilerParams(
            dimension_semantics=("arbitrary",), vmem_limit_bytes=16 << 20
        ),
        cost_estimate=pl.CostEstimate(flops=flops, bytes_accessed=tiles.size, transcendentals=0),
        name="spread",
    )(place, offsets, counts, views, tiles, begin)


def swap(array, axis):
    return lax.ppermute(array, axis, [(0, 1), (1, 0)])


def per_device(volume, measured, ray_tiles, tile_offsets, band_counts):
    f32, f16, bf16 = jnp.float32, jnp.float16, jnp.bfloat16
    depth, row_count, width = volume.shape
    tile = ray_tiles.shape[3]
    tile_count = width // tile
    count = tile_count * depth
    zhi, core = lax.axis_index("zhi"), lax.axis_index("core")
    first_row = lax.axis_index(ANGLE) * row_count
    mine = jnp.stack([core, first_row])
    other = jnp.stack([1 - core, first_row])
    tiles = pltpu.with_memory_space_constraint(
        ray_tiles.reshape((ZHI, YS, CORES) + ray_tiles.shape[1:]), pltpu.HBM
    )
    by_row = (
        volume.reshape(depth, row_count, tile_count, tile).transpose(1, 2, 0, 3).reshape(row_count, count, tile)
    )

    away = project(other, tile_offsets, band_counts, by_row, tiles, f32, PAIR_SCALE)
    arrived = swap(away, "core")
    kept = project(mine, tile_offsets, band_counts, by_row, tiles, f32, PAIR_SCALE)
    pair = (kept + arrived).astype(f16)
    parts = lax.all_to_all(pair, "y", 0, 0, tiled=True)
    plane = jnp.sum(parts.astype(f32), axis=0) * (1 / PAIR_SCALE)
    seen = measured.reshape(depth, tile_count, tile).transpose(1, 0, 2).reshape(count, tile)
    is_mine = (lax.broadcasted_iota(jnp.int32, (ZHI, 1, 1), 0) == zhi)
    plane = plane - jnp.where(is_mine, seen[None], 0.0)
    far = swap((plane * PLANE_SCALE).astype(f16), "zhi")
    both = plane + far.astype(f32) * (1 / PLANE_SCALE)
    residual = jnp.where(zhi == 0, both[0], both[1])
    residual = residual.reshape(tile_count, depth, tile).transpose(1, 0, 2).reshape(1, depth, width)
    rounded = both.astype(bf16)
    views = lax.all_to_all(
        jnp.broadcast_to(rounded[None], (YS,) + rounded.shape), "y", 0, 0, tiled=True
    )
    views_other = swap(views, "core")
    gradient = spread(mine, tile_offsets, band_counts, views, tiles, jnp.zeros((row_count, count, tile), f32))
    gradient = spread(other, tile_offsets, band_counts, views_other, tiles, gradient)
    gradient = (
        gradient.reshape(row_count, tile_count, depth, tile).transpose(2, 0, 1, 3).reshape(depth, row_count, width)
    )

    beside_all = padded_2(volume, ((SLAB, 0), (ANGLE, 1)), 1)
    field = jnp.pad(beside_all.astype(f32), ((0, 0), (0, 0), (1, 1)))
    updated = volume.astype(f32) - step_size * gradient + step_size * smooth_weight * divergence(field)
    return (updated, residual)


def solution(mesh):
    slabs = mesh.shape["slab"]
    fine = Mesh(
        mesh.devices.reshape(slabs // 4, 4, ZHI, YS, CORES), SLAB + ANGLE
    )
    return jax.shard_map(
        per_device,
        mesh=fine,
        in_specs=(
            P(SLAB, ANGLE, None),
            P(ANGLE, SLAB, None),
            P(None, ANGLE, None, None, None),
            P(),
            P(),
        ),
        out_specs=(P(SLAB, ANGLE, None), P(ANGLE, SLAB, None)),
        check_vma=False,
    )
```

time: 613 us -> 103 us (0.17)
  waiting for transfers between devices: 522 us -> 32.2 us
  matrix products: 26.9 us -> 0 us
  starting transfers between devices: 17.7 us -> 38.8 us
  Pallas kernels: 0 us -> 20.4 us
  local copies, waits for them, and re-layouts: 21.8 us -> 3.82 us
  between operations: 14.3 us -> 0.96 us
    psum x1 -> x0, waiting for transfers between devices: 407 us -> none  [per_device(): lax.psum(jax.vmap(partial(project_angle, margin=margin), in_axes=(None, 0...]
    all_gather x1 -> x0, waiting for transfers between devices: 111 us -> none  [per_device(): measured_all = lax.all_gather(measured, 'angle', axis=0, tiled=True)]
    all_to_all x0 -> x2, waiting for transfers between devices: none -> 28.8 us  [the longest x1 16.9 us: per_device(): lax.all_to_all(jnp.broadcast_to(rounded[None], (YS,) + rounded.shape), 'y...]
    dot_general x4 -> x0, matrix products: 26.9 us -> none  [the longest x2 18.7 us: spread_angle(): jnp.einsum('zrtd,rcd->zrtc', moved, tiles[:, k], preferred_element_type=j...]
    ppermute x0 -> x3, starting transfers between devices: none -> 24.2 us  [swap(): return lax.ppermute(array, axis, [(0, 1), (1, 0)])]
    pallas_call x0 -> x4, Pallas kernels: none -> 20.4 us  [the longest x2 10.3 us: spread(): pl.pallas_call(spread_kernel, grid_spec=pltpu.PrefetchScalarGridSpec(num_...]
    gather x12 -> x0, local copies, waits for them, and re-layouts: 16.2 us -> none  [the longest x6 8.12 us: spread_angle(): lax.dynamic_slice_in_dim(view_pad, margin - offset, tile_count, 1)]
    all_to_all x0 -> x2, starting transfers between devices: none -> 7.37 us  [the longest x1 3.88 us: per_device(): lax.all_to_all(jnp.broadcast_to(rounded[None], (YS,) + rounded.shape), 'y...]
  transfers between devices with their start and end apart: 6 -> 9, of which waited for: 4 -> 3; matrix products, arithmetic and copies ran while one was open for 0% -> 4% of each run, Pallas kernels for 0% -> 10%
where the time goes in v1:
time: 103 us; the launch traced here: 102 us
  starting transfers between devices  38.8 us (38%)
  waiting for transfers between devices  32.2 us (31%)
  Pallas kernels  20.4 us (20%)
  other arithmetic  5.61 us (5%)
  local copies, waits for them, and re-layouts  3.82 us (4%)
    ppermute x3, starting transfers between devices, swap(): return lax.ppermute(array, axis, [(0, 1), (1, 0)])  24.2 us
    all_to_all x1, waiting for transfers between devices, per_device(): lax.all_to_all(jnp.broadcast_to(rounded[None], (YS,) + rounded.shape), 'y...  16.9 us
    all_to_all x1, waiting for transfers between devices, per_device(): parts = lax.all_to_all(pair, 'y', 0, 0, tiled=True)  11.8 us
    pallas_call x2, Pallas kernels, spread(): pl.pallas_call(spread_kernel, grid_spec=pltpu.PrefetchScalarGridSpec(num_...  10.3 us
    pallas_call x2, Pallas kernels, project(): pl.pallas_call(partial(project_kernel, scale=scale), grid_spec=pltpu.Pref...  10.1 us
    ppermute x2, starting transfers between devices, padded_2(): before = lax.ppermute(last, axis, up)  4.07 us
    all_to_all x1, starting transfers between devices, per_device(): lax.all_to_all(jnp.broadcast_to(rounded[None], (YS,) + rounded.shape), 'y...  3.88 us
    all_to_all x1, starting transfers between devices, per_device(): parts = lax.all_to_all(pair, 'y', 0, 0, tiled=True)  3.49 us
  transfers between devices with their start and end apart: 9, of which 3 were waited for; matrix products, arithmetic and copies ran while one was open for 4% of the time, Pallas kernels for 10%

profile of v1, /device:TPU:1, one launch (start us, length us, event | category | flops | bytes accessed | tf_op | source)
XLA Modules:
  0.0 101.8 jit_solution(3250993388234710453)
XLA Ops:
  0.6 0.0 copy-start.1
  0.6 1.0 reshape.37
  1.6 0.1 copy.10
  1.7 0.1 pad_add_fusion.place
  1.8 0.7 copy-done
  2.5 0.7 copy-done.2
  3.3 5.1 %project.3 = f32[8,2,128,128]{3,2,1,0:T(8,128)S(1)} custom-call(s32[2]{0:T(128)S(1)} %pad_add_fusion.place, s32[32,128]{1,0:T(8,128)S(1)} %copy-done, s32[32,128]{1,0:T(8,128)S(1)} %copy-done.2, bf16[4,128,128]{2,1,0:T(8,128)(2,1)S(1)} %bitcast.26, bf16[2,8,2,4,2,128,128]{6,5,4,3,2,1,0:T(8,128)(2,1)} %bitcast.28), custom_call_target="tpu_custom_call" | custom-call | flops 536870912 | bytes 4194304 | tf_op jit(solution)/shard_map/project/pallas_call | solution.py:147
  8.3 0.0 copy-start.5
  8.3 0.0 copy-start.6
  8.3 12.6 %collective-permute-start = (f32[8,2,128,128]{3,2,1,0:T(8,128)S(1)}, f32[8,2,128,128]{3,2,1,0:T(8,128)S(1)}, u32[]{:S(2)}, u32[]{:S(2)}) collective-permute-start(f32[8,2,128,128]{3,2,1,0:T(8,128)S(1)} %project.3), channel_id=1, source_target_pairs={{0,1},{1,0},{2,3},{3,2},{4,5},{5,4},{6,7},{7,6},{8,9},{9,8},{10,11... | collective-permute-start | bytes 3145736 | tf_op jit(solution)/shard_map/ppermute | solution.py:194
  20.9 0.1 pad_add_fusion.1.place
  21.0 0.0 copy-done.1
  21.0 5.1 %project.2 = f32[8,2,128,128]{3,2,1,0:T(8,128)S(1)} custom-call(s32[2]{0:T(128)S(1)} %pad_add_fusion.1.place, s32[32,128]{1,0:T(8,128)S(1)} %copy-done.1, s32[32,128]{1,0:T(8,128)S(1)} %copy-done.2, bf16[4,128,128]{2,1,0:T(8,128)(2,1)S(1)} %bitcast.27, bf16[2,8,2,4,2,128,128]{6,5,4,3,2,1,0:T(8,128)(2,1)} %bitcast.29), custom_call_target="tpu_custom_call" | custom-call | flops 536870912 | bytes 4194304 | tf_op jit(solution)/shard_map/project/pallas_call | solution.py:147
  26.1 0.0 copy-start.3
  26.1 0.0 collective-permute-done
  26.1 1.0 add_convert_fusion
  27.1 3.5 %all-to-all-start = ((f16[8,2,128,128]{3,2,1,0:T(8,128)(2,1)}), f16[8,2,128,128]{3,2,1,0:T(8,128)(2,1)S(1)}, u32[]{:S(2)}, u32[]{:S(2)}) async-start(f16[8,2,128,128]{3,2,1,0:T(8,128)(2,1)} %add_convert_fusion), calls=%async_computation | async-start | bytes 1048576 | tf_op jit(solution)/shard_map/all_to_all | solution.py:218
  30.6 0.0 copy-done.5
  30.6 1.3 %collective-permute-start.3 = (bf16[1,4,2048]{2,1,0:T(4,128)(2,1)S(1)}, bf16[1,4,2048]{2,1,0:T(4,128)(2,1)S(1)}, u32[]{:S(2)}, u32[]{:S(2)}) collective-permute-start(bf16[1,4,2048]{2,1,0:T(4,128)(2,1)S(1)} %get-tuple-element.11), channel_id=1, source_target_pairs={{0,32},{32,64},{64,96},{96,128},{128,160},{160,192},{192,224},{224... | collective-permute-start | bytes 49160 | tf_op jit(solution)/shard_map/ppermute | solution.py:31
  31.9 1.3 %collective-permute-start.4 = (bf16[1,4,2048]{2,1,0:T(4,128)(2,1)S(1)}, bf16[1,4,2048]{2,1,0:T(4,128)(2,1)S(1)}, u32[]{:S(2)}, u32[]{:S(2)}) collective-permute-start(bf16[1,4,2048]{2,1,0:T(4,128)(2,1)S(1)} %get-tuple-element.10), channel_id=1, source_target_pairs={{32,0},{64,32},{96,64},{128,96},{160,128},{192,160},{224,192},{256... | collective-permute-start | bytes 49160 | tf_op jit(solution)/shard_map/ppermute | solution.py:32
  33.2 0.0 collective-permute-done.3
  33.2 0.1 constant_dynamic-update-slice_fusion.1
  33.3 3.4 %collective-permute-done.4 = bf16[1,4,2048]{2,1,0:T(4,128)(2,1)S(1)} collective-permute-done((bf16[1,4,2048]{2,1,0:T(4,128)(2,1)S(1)}, bf16[1,4,2048]{2,1,0:T(4,128)(2,1)S(1)}, u32[]{:S(2)}, u32[]{:S(2)}) %collective-permute-start.4) | collective-permute-done | bytes 16416 | tf_op jit(solution)/shard_map/ppermute | solution.py:32
  36.7 11.8 %all-to-all-done = f16[8,2,128,128]{3,2,1,0:T(8,128)(2,1)S(1)} async-done(((f16[8,2,128,128]{3,2,1,0:T(8,128)(2,1)}), f16[8,2,128,128]{3,2,1,0:T(8,128)(2,1)S(1)}, u32[]{:S(2)}, u32[]{:S(2)}) %all-to-all-start) | async-done | bytes 524320 | tf_op jit(solution)/shard_map/all_to_all | solution.py:218
  48.5 0.1 convert_reduce_fusion
  48.6 0.1 multiply_convert_fusion
  48.7 9.2 %collective-permute-start.1 = (f16[2,128,128]{2,1,0:T(8,128)(2,1)S(1)}, f16[2,128,128]{2,1,0:T(8,128)(2,1)S(1)}, u32[]{:S(2)}, u32[]{:S(2)}) collective-permute-start(f16[2,128,128]{2,1,0:T(8,128)(2,1)S(1)} %multiply_convert_fusion), channel_id=1, source_target_pairs={{0,16},{16,0},{1,17},{17,1},{2,18},{18,2},{3,19},{19,3},{4,20},{20... | collective-permute-start | bytes 196616 | tf_op jit(solution)/shard_map/ppermute | solution.py:194
  57.9 0.1 fusion.14
  58.0 2.8 %collective-permute-start.5 = (bf16[10,1,2048]{2,1,0:T(2,128)(2,1)S(1)}, bf16[10,1,2048]{2,1,0:T(2,128)(2,1)S(1)}, u32[]{:S(2)}, u32[]{:S(2)}) collective-permute-start(bf16[10,1,2048]{2,1,0:T(2,128)(2,1)S(1)} %get-tuple-element.8), channel_id=1, source_target_pairs={{0,1},{1,2},{2,3},{3,4},{4,5},{5,6},{6,7},{7,8},{8,9},{9,10},{10,1... | collective-permute-start | bytes 122888 | tf_op jit(solution)/shard_map/ppermute | solution.py:31
  60.8 1.9 %collective-permute-start.6 = (bf16[10,1,2048]{2,1,0:T(2,128)(2,1)S(1)}, bf16[10,1,2048]{2,1,0:T(2,128)(2,1)S(1)}, u32[]{:S(2)}, u32[]{:S(2)}) collective-permute-start(bf16[10,1,2048]{2,1,0:T(2,128)(2,1)S(1)} %get-tuple-element.9), channel_id=1, source_target_pairs={{1,0},{2,1},{3,2},{4,3},{5,4},{6,5},{7,6},{8,7},{9,8},{10,9},{11,1... | collective-permute-start | bytes 122888 | tf_op jit(solution)/shard_map/ppermute | solution.py:32
  62.8 0.0 collective-permute-done.1
  62.8 0.1 fusion.13
  62.9 0.9 broadcast_in_dim.35
  63.8 3.9 %all-to-all-start.1 = ((bf16[8,2,128,128]{3,2,1,0:T(8,128)(2,1)}), bf16[8,2,128,128]{3,2,1,0:T(8,128)(2,1)S(1)}, u32[]{:S(2)}, u32[]{:S(2)}) async-start(bf16[8,2,128,128]{3,2,1,0:T(8,128)(2,1)} %broadcast_in_dim.35), calls=%async_computation.1 | async-start | bytes 1048576 | tf_op jit(solution)/shard_map/all_to_all | solution.py:228
  67.6 0.0 collective-permute-done.5
  67.7 0.0 collective-permute-done.6
  67.7 0.5 fusion.6
  68.2 0.5 fusion.9
  68.7 16.9 %all-to-all-done.1.views = bf16[8,2,128,128]{3,2,1,0:T(8,128)(2,1)S(1)} async-done(((bf16[8,2,128,128]{3,2,1,0:T(8,128)(2,1)}), bf16[8,2,128,128]{3,2,1,0:T(8,128)(2,1)S(1)}, u32[]{:S(2)}, u32[]{:S(2)}) %all-to-all-start.1) | async-done | bytes 524320 | tf_op jit(solution)/shard_map/all_to_all | solution.py:228
  85.6 2.4 %collective-permute-start.2 = (bf16[8,2,128,128]{3,2,1,0:T(8,128)(2,1)S(1)}, bf16[8,2,128,128]{3,2,1,0:T(8,128)(2,1)S(1)}, u32[]{:S(2)}, u32[]{:S(2)}) collective-permute-start(bf16[8,2,128,128]{3,2,1,0:T(8,128)(2,1)S(1)} %all-to-all-done.1.views), channel_id=1, source_target_pairs={{0,1},{1,0},{2,3},{3,2},{4,5},{5,4},{6,7},{7,6},{8,9},{9,8},{10,11... | collective-permute-start | bytes 1572872 | tf_op jit(solution)/shard_map/ppermute | solution.py:194
  88.0 1.1 %fusion.10 = (f32[9,5,2049]{2,1,0:T(8,128)S(1)}, f32[9,5,2049]{2,1,0:T(8,128)}) fusion(f32[9,5,2049]{2,1,0:T(8,128)S(1)} %get-tuple-element.5, f32[10,6,2050]{2,1,0:T(8,128)S(1)} %fusion.6), kind=kLoop, calls=%fused_computation.24 | loop fusion | flops 368820 | bytes 2212920 | tf_op jit(solution)/shard_map/div | solution.py:44
  89.1 0.6 fusion.12
  89.8 5.2 %spread.2.begin = f32[4,128,128]{2,1,0:T(8,128)S(1)} custom-call(s32[2]{0:T(128)S(1)} %pad_add_fusion.1.place, s32[32,128]{1,0:T(8,128)S(1)} %copy-done.1, s32[32,128]{1,0:T(8,128)S(1)} %copy-done.3, bf16[8,2,128,128]{3,2,1,0:T(8,128)(2,1)S(1)} %all-to-all-done.1.views, bf16[2,8,2,4,2,128,128]{6,5,4,3,2,1,0:T(8,128)(2,1)} %bitcast.30, ...), custom_call_target="tpu_custom_call" | custom-call | flops 536870912 | bytes 4194304 | tf_op jit(solution)/shard_map/spread/pallas_call | solution.py:171
  95.0 0.0 collective-permute-done.2.views
  95.0 5.2 %spread.3 = f32[4,128,128]{2,1,0:T(8,128)S(1)} custom-call(s32[2]{0:T(128)S(1)} %pad_add_fusion.place, s32[32,128]{1,0:T(8,128)S(1)} %copy-done.1, s32[32,128]{1,0:T(8,128)S(1)} %copy-done.3, bf16[8,2,128,128]{3,2,1,0:T(8,128)(2,1)S(1)} %collective-permute-done.2.views, bf16[2,8,2,4,2,128,128]{6,5,4,3,2,1,0:T(8,128)(2,1)} %bitcast.31, ...), custom_call_target="tpu_custom_call" | custom-call | flops 536870912 | bytes 4194304 | tf_op jit(solution)/shard_map/spread/pallas_call | solution.py:171
  100.2 0.1 copy.8
  100.2 0.1 mul.70
  100.3 1.5 %fusion.8 = f32[8,4,2048]{2,1,0:T(4,128)} fusion(f32[9,5,2049]{2,1,0:T(8,128)S(1)} %copy-done.4, f32[9,5,2049]{2,1,0:T(8,128)S(1)} %get-tuple-element.6, f32[9,5,2049]{2,1,0:T(8,128)S(1)} %get-tuple-element.4, f32[8,4,2048]{2,1,0:T(4,128)S(1)} %mul.70, bf16[8,4,2048]{2,1,0:T(4,128)(2,1)S(1)} %copy-done.5), kind=kLoop, calls=%fused_computation.17 | loop fusion | flops 589824 | bytes 2228224 | tf_op jit(solution)/shard_map/add | solution.py:240
  (12 shorter events, 0.1 us)
Async XLA Ops:
  0.6 20.4 %copy-start.1 = (s32[32,128]{1,0:T(8,128)S(1)}, s32[32,128]{1,0:T(8,128)}, u32[]{:S(2)}) copy-start(s32[32,128]{1,0:T(8,128)} %offsets.7) | copy-start | bytes 49156
  1.8 0.7 copy-start
  2.5 0.7 copy-start.2
  8.3 22.2 %copy-start.5 = (bf16[8,4,2048]{2,1,0:T(4,128)(2,1)S(1)}, bf16[8,4,2048]{2,1,0:T(4,128)(2,1)}, u32[]{:S(2)}) copy-start(bf16[8,4,2048]{2,1,0:T(4,128)(2,1)} %param.5) | copy-start | bytes 393220
  8.3 40.3 %copy-start.6 = (f32[1,8,2048]{2,1,0:T(8,128)S(1)}, f32[1,8,2048]{2,1,0:T(8,128)}, u32[]{:S(2)}) copy-start(f32[1,8,2048]{2,1,0:T(8,128)} %param.6) | copy-start | bytes 196612
  8.3 17.7 %collective-permute-start = (f32[8,2,128,128]{3,2,1,0:T(8,128)S(1)}, f32[8,2,128,128]{3,2,1,0:T(8,128)S(1)}, u32[]{:S(2)}, u32[]{:S(2)}) collective-permute-start(f32[8,2,128,128]{3,2,1,0:T(8,128)S(1)} %project.3), channel_id=1, source_target_pairs={{0,1},{1,0},{2,3},{3,2},{4,5},{5,4},{6,7},{7,6},{8,9},{9,8},{10,11... | collective-permute-start | bytes 3145736 | tf_op jit(solution)/shard_map/ppermute | solution.py:194
  26.1 63.7 %copy-start.3 = (s32[32,128]{1,0:T(8,128)S(1)}, s32[32,128]{1,0:T(8,128)}, u32[]{:S(2)}) copy-start(s32[32,128]{1,0:T(8,128)} %counts.7) | copy-start | bytes 49156
  27.1 21.5 %all-to-all-start = ((f16[8,2,128,128]{3,2,1,0:T(8,128)(2,1)}), f16[8,2,128,128]{3,2,1,0:T(8,128)(2,1)S(1)}, u32[]{:S(2)}, u32[]{:S(2)}) async-start(f16[8,2,128,128]{3,2,1,0:T(8,128)(2,1)} %add_convert_fusion), calls=%async_computation | async-start | bytes 1048576 | tf_op jit(solution)/shard_map/all_to_all | solution.py:218
  30.6 2.6 %collective-permute-start.3 = (bf16[1,4,2048]{2,1,0:T(4,128)(2,1)S(1)}, bf16[1,4,2048]{2,1,0:T(4,128)(2,1)S(1)}, u32[]{:S(2)}, u32[]{:S(2)}) collective-permute-start(bf16[1,4,2048]{2,1,0:T(4,128)(2,1)S(1)} %get-tuple-element.11), channel_id=1, source_target_pairs={{0,32},{32,64},{64,96},{96,128},{128,160},{160,192},{192,224},{224... | collective-permute-start | bytes 49160 | tf_op jit(solution)/shard_map/ppermute | solution.py:31
  31.9 4.8 %collective-permute-start.4 = (bf16[1,4,2048]{2,1,0:T(4,128)(2,1)S(1)}, bf16[1,4,2048]{2,1,0:T(4,128)(2,1)S(1)}, u32[]{:S(2)}, u32[]{:S(2)}) collective-permute-start(bf16[1,4,2048]{2,1,0:T(4,128)(2,1)S(1)} %get-tuple-element.10), channel_id=1, source_target_pairs={{32,0},{64,32},{96,64},{128,96},{160,128},{192,160},{224,192},{256... | collective-permute-start | bytes 49160 | tf_op jit(solution)/shard_map/ppermute | solution.py:32
  48.7 14.1 %collective-permute-start.1 = (f16[2,128,128]{2,1,0:T(8,128)(2,1)S(1)}, f16[2,128,128]{2,1,0:T(8,128)(2,1)S(1)}, u32[]{:S(2)}, u32[]{:S(2)}) collective-permute-start(f16[2,128,128]{2,1,0:T(8,128)(2,1)S(1)} %multiply_convert_fusion), channel_id=1, source_target_pairs={{0,16},{16,0},{1,17},{17,1},{2,18},{18,2},{3,19},{19,3},{4,20},{20... | collective-permute-start | bytes 196616 | tf_op jit(solution)/shard_map/ppermute | solution.py:194
  58.0 9.6 %collective-permute-start.5 = (bf16[10,1,2048]{2,1,0:T(2,128)(2,1)S(1)}, bf16[10,1,2048]{2,1,0:T(2,128)(2,1)S(1)}, u32[]{:S(2)}, u32[]{:S(2)}) collective-permute-start(bf16[10,1,2048]{2,1,0:T(2,128)(2,1)S(1)} %get-tuple-element.8), channel_id=1, source_target_pairs={{0,1},{1,2},{2,3},{3,4},{4,5},{5,6},{6,7},{7,8},{8,9},{9,10},{10,1... | collective-permute-start | bytes 122888 | tf_op jit(solution)/shard_map/ppermute | solution.py:31
  60.8 6.8 %collective-permute-start.6 = (bf16[10,1,2048]{2,1,0:T(2,128)(2,1)S(1)}, bf16[10,1,2048]{2,1,0:T(2,128)(2,1)S(1)}, u32[]{:S(2)}, u32[]{:S(2)}) collective-permute-start(bf16[10,1,2048]{2,1,0:T(2,128)(2,1)S(1)} %get-tuple-element.9), channel_id=1, source_target_pairs={{1,0},{2,1},{3,2},{4,3},{5,4},{6,5},{7,6},{8,7},{9,8},{10,9},{11,1... | collective-permute-start | bytes 122888 | tf_op jit(solution)/shard_map/ppermute | solution.py:32
  63.8 21.8 %all-to-all-start.1 = ((bf16[8,2,128,128]{3,2,1,0:T(8,128)(2,1)}), bf16[8,2,128,128]{3,2,1,0:T(8,128)(2,1)S(1)}, u32[]{:S(2)}, u32[]{:S(2)}) async-start(bf16[8,2,128,128]{3,2,1,0:T(8,128)(2,1)} %broadcast_in_dim.35), calls=%async_computation.1 | async-start | bytes 1048576 | tf_op jit(solution)/shard_map/all_to_all | solution.py:228
  85.6 9.4 %collective-permute-start.2 = (bf16[8,2,128,128]{3,2,1,0:T(8,128)(2,1)S(1)}, bf16[8,2,128,128]{3,2,1,0:T(8,128)(2,1)S(1)}, u32[]{:S(2)}, u32[]{:S(2)}) collective-permute-start(bf16[8,2,128,128]{3,2,1,0:T(8,128)(2,1)S(1)} %all-to-all-done.1.views), channel_id=1, source_target_pairs={{0,1},{1,0},{2,3},{3,2},{4,5},{5,4},{6,7},{7,6},{8,9},{9,8},{10,11... | collective-permute-start | bytes 1572872 | tf_op jit(solution)/shard_map/ppermute | solution.py:194
  89.8 10.5 %copy-start.4 = (f32[9,5,2049]{2,1,0:T(8,128)S(1)}, f32[9,5,2049]{2,1,0:T(8,128)}, u32[]{:S(2)}) copy-start(f32[9,5,2049]{2,1,0:T(8,128)} %get-tuple-element.7) | copy-start | bytes 1106464

commit v2 on v1

v2 whole, which is shorter than its diff:
```python
from functools import partial

import jax
import jax.numpy as jnp
from jax import lax
from jax.experimental import pallas as pl
from jax.experimental.pallas import tpu as pltpu
from jax.sharding import Mesh, PartitionSpec as P

OFFMAX = 3

step_size = 0.3
smooth_weight = 0.2
smooth_floor = 0.25

ZHI, YS, CORES = 2, 8, 2
SLAB = ("zlo", "x")
ANGLE = ("zhi", "y", "core")

PAIR_SCALE = 2.0**6
PLANE_SCALE = 2.0**3


def shifts_of(size, gap=None):
    up = [(i, i + 1) for i in range(size - 1) if i != gap]
    return up, [(j, i) for i, j in up]


def edges(shard, dim):
    length = shard.shape[dim]
    return lax.slice_in_dim(shard, length - 1, length, axis=dim), lax.slice_in_dim(shard, 0, 1, axis=dim)


def with_row_neighbours(shard, ends_plane, begins_plane):
    size = lax.axis_size(ANGLE)
    gap = size // ZHI - 1
    up, down = shifts_of(size, gap)
    last, first = edges(shard, 1)
    before, after = lax.ppermute(last, ANGLE, up), lax.ppermute(first, ANGLE, down)
    across = lax.ppermute(jnp.where(ends_plane, last, first), ANGLE, [(gap, gap + 1), (gap + 1, gap)])
    before = jnp.where(begins_plane, across, before)
    after = jnp.where(ends_plane, across, after)
    return jnp.concatenate([before, shard, after], axis=1)


def with_slab_neighbours(shard):
    up, down = shifts_of(lax.axis_size(SLAB))
    last, first = edges(shard, 0)
    return jnp.concatenate([lax.ppermute(last, SLAB, up), shard, lax.ppermute(first, SLAB, down)], axis=0)


def divergence(field):
    base = field[:-1, :-1, :-1]
    step_z = field[1:, :-1, :-1] - base
    step_y = field[:-1, 1:, :-1] - base
    step_x = field[:-1, :-1, 1:] - base
    scale = jnp.sqrt(step_z * step_z + step_y * step_y + step_x * step_x + smooth_floor)
    flow_z = step_z / scale
    flow_y = step_y / scale
    flow_x = step_x / scale
    result = flow_z[1:, 1:, 1:] - flow_z[:-1, 1:, 1:]
    result = result + flow_y[1:, 1:, 1:] - flow_y[1:, :-1, 1:]
    return result + flow_x[1:, 1:, 1:] - flow_x[1:, 1:, :-1]


PAD = 4
GROUP = 4


def copy_rows(count):
    return count + 16 * PAD


def window_rows(bands, count):
    return bands * 2 * copy_rows(count) + count


def band_windows(offset, used, sign, band, bands, count):
    base = band * 2 * copy_rows(count)

    def start(tile):
        return base + tile * 8 + (tile & 1) * (copy_rows(count) - 8)

    first = PAD + sign * (offset - 1)
    second = jnp.where(used > 1, start(first + sign), bands * 2 * copy_rows(count))
    return pl.multiple_of(start(first), 16), pl.multiple_of(second, 16)


def fill_windows(ref, band, wide):
    count, lanes = wide.shape
    rows = copy_rows(count)
    zero = lambda n: jnp.zeros((n, lanes), wide.dtype)
    base = band * 2 * rows
    ref[base : base + rows] = jnp.concatenate([zero(8 * PAD), wide, zero(8 * PAD)], 0).astype(ref.dtype)
    ref[base + rows : base + 2 * rows] = jnp.concatenate(
        [zero(8 * (PAD - 1)), wide, zero(8 * (PAD + 1))], 0
    ).astype(ref.dtype)


def fill_zeros(ref, bands, count):
    base = bands * 2 * copy_rows(count)
    ref[base : base + count] = jnp.zeros((count, ref.shape[1]), ref.dtype)


def angle_of(j, core):
    return ((j % ZHI) * YS + j // ZHI) * CORES + core


def project_one(j, core, first_row, offsets, counts, windows, tiles, out, scale):
    rows = tiles.shape[1]
    count, lanes = out.shape[2:]
    angle = angle_of(j, core)
    pieces = []
    for r in range(rows):
        row = first_row + r
        for start in band_windows(offsets[angle, row], counts[angle, row], 1, r, rows, count):
            pieces.append(windows[pl.ds(start, count), :])
    weights = tiles[angle].reshape(len(pieces) * lanes, lanes)
    view = jnp.dot(jnp.concatenate(pieces, 1), weights, preferred_element_type=jnp.float32)
    out[j // ZHI, j % ZHI] = view * scale


def load_project_kernel(
    place, offsets_hbm, counts_hbm, volume_hbm, tiles_hbm, out, tiles, windows, offsets, counts, volume, tile_sems, sems,
    *, scale
):
    core, first_row = place[0], place[1]
    blocks, rows = ZHI * YS, tiles.shape[1]
    count, lanes = out.shape[2:]
    small = [
        pltpu.make_async_copy(source, target, sems.at[i])
        for i, (source, target) in enumerate(
            ((volume_hbm, volume), (offsets_hbm, offsets), (counts_hbm, counts))
        )
    ]
    copies = tile_copies(tiles_hbm, tiles, tile_sems, 1 - core)
    for copy in small + copies[:blocks]:
        copy.start()
    small[0].wait()
    for r in range(rows):
        line = volume[:, r, :].astype(jnp.float32)
        fill_windows(
            windows, r, jnp.concatenate([line[:, t * lanes : (t + 1) * lanes] for t in range(line.shape[1] // lanes)], 0)
        )
    fill_zeros(windows, rows, count)
    small[1].wait()
    small[2].wait()
    for first in range(0, blocks, GROUP):
        wait_group(copies, first)
        for j in range(first, first + GROUP):
            project_one(j, 1 - core, first_row, offsets, counts, windows, tiles, out, scale)
    for copy in copies[blocks:]:
        copy.wait()


def project_kernel(place, offsets, counts, windows, tiles, out, *, scale):
    for j in range(ZHI * YS):
        project_one(j, place[0], place[1], offsets, counts, windows, tiles, out, scale)


def tile_copies(tiles_hbm, tiles, sems, first_core):
    blocks = ZHI * YS
    order = [angle_of(j, first_core) for j in range(blocks)] + [angle_of(j, 1 - first_core) for j in range(blocks)]
    return [pltpu.make_async_copy(tiles_hbm.at[a], tiles.at[a], sems.at[i]) for i, a in enumerate(order)]


def wait_group(copies, first):
    blocks = ZHI * YS
    for copy in copies[first : first + GROUP]:
        copy.wait()
    if first == 0:
        for copy in copies[blocks:]:
            copy.start()


def spread_group(first, core, first_row, offsets, counts, windows, tiles, begin, out):
    blocks, rows = ZHI * YS, tiles.shape[1]
    count = out.shape[1]
    for r in range(rows):
        row = first_row + r
        lhs, rhs = [], []
        for j in range(first, first + GROUP):
            angle = angle_of(j, core)
            starts = band_windows(offsets[angle, row], counts[angle, row], -1, j, blocks, count)
            for k, start in enumerate(starts):
                lhs.append(windows[pl.ds(start, count), :])
                rhs.append(tiles[angle, r, k])
        part = lax.dot_general(
            jnp.concatenate(lhs, 1),
            jnp.concatenate(rhs, 1),
            (((1,), (1,)), ((), ())),
            preferred_element_type=jnp.float32,
        )
        if first > 0:
            out[r] += part
        elif begin is None:
            out[r] = part
        else:
            out[r] = begin[r] + part


def fill_views(windows, views):
    blocks = ZHI * YS
    for j in range(blocks):
        fill_windows(windows, j, views[j // ZHI, j % ZHI].astype(jnp.float32))
    fill_zeros(windows, blocks, views.shape[2])


def load_spread_kernel(place, offsets, counts, views, tiles_hbm, out, tiles, windows, sems):
    copies = tile_copies(tiles_hbm, tiles, sems, place[0])
    for copy in copies[: ZHI * YS]:
        copy.start()
    fill_views(windows, views)
    for first in range(0, ZHI * YS, GROUP):
        wait_group(copies, first)
        spread_group(first, place[0], place[1], offsets, counts, windows, tiles, None, out)
    for copy in copies[ZHI * YS :]:
        copy.wait()


def spread_kernel(place, offsets, counts, views, tiles, begin, out, windows):
    fill_views(windows, views)
    for first in range(0, ZHI * YS, GROUP):
        spread_group(first, 1 - place[0], place[1], offsets, counts, windows, tiles, begin, out)


ANY = pl.BlockSpec(memory_space=pl.ANY)
VMEM = pl.BlockSpec(memory_space=pltpu.VMEM)
SMEM = pl.BlockSpec(memory_space=pltpu.SMEM)


def params():
    return pltpu.CompilerParams(vmem_limit_bytes=16 << 20)


def cost(tiles, share):
    return pl.CostEstimate(
        flops=256 * tiles.size // share, bytes_accessed=2 * tiles.size // share, transcendentals=0
    )


def in_hbm(array):
    return pltpu.with_memory_space_constraint(array, pltpu.HBM)


def load_project(place, offsets, counts, volume, tiles, scale):
    depth, rows, width = volume.shape
    lanes = tiles.shape[-1]
    count = depth * width // lanes
    return pl.pallas_call(
        partial(load_project_kernel, scale=scale),
        in_specs=[SMEM, ANY, ANY, ANY, ANY],
        out_specs=[VMEM, VMEM, VMEM, SMEM, SMEM],
        out_shape=[
            pltpu.VMEM((YS, ZHI, count, lanes), jnp.float32),
            pltpu.VMEM(tiles.shape, tiles.dtype),
            pltpu.VMEM((window_rows(rows, count), lanes), volume.dtype),
            pltpu.SMEM(offsets.shape, offsets.dtype),
            pltpu.SMEM(counts.shape, counts.dtype),
        ],
        scratch_shapes=[
            pltpu.VMEM(volume.shape, volume.dtype),
            pltpu.SemaphoreType.DMA((tiles.shape[0],)),
            pltpu.SemaphoreType.DMA((3,)),
        ],
        compiler_params=params(),
        cost_estimate=cost(tiles, 2),
        name="load_project",
    )(place, in_hbm(offsets), in_hbm(counts), in_hbm(volume), in_hbm(tiles))


def project(place, offsets, counts, windows, tiles, like, scale):
    return pl.pallas_call(
        partial(project_kernel, scale=scale),
        in_specs=[SMEM, SMEM, SMEM, VMEM, VMEM],
        out_specs=VMEM,
        out_shape=pltpu.VMEM(like.shape, jnp.float32),
        compiler_params=params(),
        cost_estimate=cost(tiles, 2),
        name="project",
    )(place, offsets, counts, windows, tiles)


def load_spread(place, offsets, counts, views, tiles):
    count, lanes = views.shape[2:]
    return pl.pallas_call(
        load_spread_kernel,
        in_specs=[SMEM, SMEM, SMEM, VMEM, ANY],
        out_specs=[VMEM, VMEM],
        out_shape=[
            pltpu.VMEM((tiles.shape[1], count, lanes), jnp.float32),
            pltpu.VMEM(tiles.shape, tiles.dtype),
        ],
        scratch_shapes=[
            pltpu.VMEM((window_rows(ZHI * YS, count), lanes), jnp.bfloat16),
            pltpu.SemaphoreType.DMA((tiles.shape[0],)),
        ],
        compiler_params=params(),
        cost_estimate=cost(tiles, 2),
        name="load_spread",
    )(place, offsets, counts, views, in_hbm(tiles))


def spread(place, offsets, counts, views, tiles, begin):
    count, lanes = views.shape[2:]
    return pl.pallas_call(
        spread_kernel,
        in_specs=[SMEM, SMEM, SMEM, VMEM, VMEM, VMEM],
        out_specs=VMEM,
        out_shape=pltpu.VMEM((tiles.shape[1], count, lanes), jnp.float32),
        scratch_shapes=[pltpu.VMEM((window_rows(ZHI * YS, count), lanes), jnp.bfloat16)],
        compiler_params=params(),
        cost_estimate=cost(tiles, 2),
        name="spread",
    )(place, offsets, counts, views, tiles, begin)


def swap(array, axis):
    return lax.ppermute(array, axis, [(0, 1), (1, 0)])


def per_device(volume, measured, ray_tiles, tile_offsets, band_counts):
    f32, f16, bf16 = jnp.float32, jnp.float16, jnp.bfloat16
    depth, row_count, width = volume.shape
    tile = ray_tiles.shape[3]
    tile_count = width // tile
    count = tile_count * depth
    zhi, core = lax.axis_index("zhi"), lax.axis_index("core")
    me = lax.axis_index(ANGLE)
    first_row = me * row_count
    gap = lax.axis_size(ANGLE) // ZHI - 1
    is_mine = lax.broadcasted_iota(jnp.int32, (ZHI, 1, 1), 0) == zhi
    place, is_mine, low_plane, ends_plane, begins_plane = lax.optimization_barrier(
        (jnp.stack([core, first_row]), is_mine, zhi == 0, me == gap, me == gap + 1)
    )

    away, tiles, windows, offsets, counts = load_project(
        place, tile_offsets, band_counts, volume, ray_tiles, PAIR_SCALE
    )
    arrived = swap(away, "core")
    kept = project(place, offsets, counts, windows, tiles, away, PAIR_SCALE)
    pair = (kept + arrived).astype(f16)
    parts = lax.all_to_all(pair, "y", 0, 0, tiled=True)
    plane = jnp.sum(parts.astype(f32), axis=0) * (1 / PAIR_SCALE)
    seen = measured.reshape(depth, tile_count, tile).transpose(1, 0, 2).reshape(count, tile)
    plane = plane - jnp.where(is_mine, seen[None], 0.0)
    far = swap((plane * PLANE_SCALE).astype(f16), "zhi")
    both = plane + far.astype(f32) * (1 / PLANE_SCALE)
    residual = jnp.where(low_plane, both[0], both[1])
    residual = residual.reshape(tile_count, depth, tile).transpose(1, 0, 2).reshape(1, depth, width)
    rounded = both.astype(bf16)
    views = lax.all_to_all(
        jnp.broadcast_to(rounded[None], (YS,) + rounded.shape), "y", 0, 0, tiled=True
    )
    views_other = swap(views, "core")
    gradient, tiles = load_spread(place, offsets, counts, views, ray_tiles)
    gradient = spread(place, offsets, counts, views_other, tiles, gradient)
    gradient = (
        gradient.reshape(row_count, tile_count, depth, tile).transpose(2, 0, 1, 3).reshape(depth, row_count, width)
    )

    beside_all = with_slab_neighbours(with_row_neighbours(volume, ends_plane, begins_plane))
    field = jnp.pad(beside_all.astype(f32), ((0, 0), (0, 0), (1, 1)))
    updated = volume.astype(f32) - step_size * gradient + step_size * smooth_weight * divergence(field)
    return (updated, residual)


def solution(mesh):
    slabs = mesh.shape["slab"]
    fine = Mesh(
        mesh.devices.reshape(slabs // 4, 4, ZHI, YS, CORES), SLAB + ANGLE
    )
    return jax.shard_map(
        per_device,
        mesh=fine,
        in_specs=(
            P(SLAB, ANGLE, None),
            P(ANGLE, SLAB, None),
            P(None, ANGLE, None, None, None),
            P(),
            P(),
        ),
        out_specs=(P(SLAB, ANGLE, None), P(ANGLE, SLAB, None)),
        check_vma=False,
    )
```

time: 103 us -> 92.5 us (0.90)
  Pallas kernels: 20.4 us -> 12.8 us
  waiting for transfers between devices: 32.2 us -> 27.2 us
  starting transfers between devices: 38.8 us -> 43 us
  local copies, waits for them, and re-layouts: 3.82 us -> 1.05 us
    all_to_all x1, waiting for transfers between devices: 11.8 us -> 3.3 us  [per_device(): parts = lax.all_to_all(pair, 'y', 0, 0, tiled=True)]
    pallas_call x4, Pallas kernels: 20.4 us -> 12.8 us  [the longest x1 4.5 us: load_project(): pl.pallas_call(partial(load_project_kernel, scale=scale), in_specs=[SMEM,...]
    ppermute x4 -> x5, waiting for transfers between devices: 3.37 us -> 7.86 us  [the longest x1 4.65 us: with_row_neighbours(): lax.ppermute(last, ANGLE, up)]
    ppermute x4 -> x5, starting transfers between devices: 7.28 us -> 10.8 us  [the longest x1 3.79 us: with_row_neighbours(): lax.ppermute(last, ANGLE, up)]
    unnamed x16 -> x6, local copies, waits for them, and re-layouts: 1.54 us -> 0.02 us
    all_to_all x1, waiting for transfers between devices: 16.9 us -> 15.7 us  [per_device(): lax.all_to_all(jnp.broadcast_to(rounded[None], (YS,) + rounded.shape), 'y...]
    reshape x2 -> x0, local copies, waits for them, and re-layouts: 1.08 us -> none  [per_device(): volume.reshape(depth, row_count, tile_count, tile).transpose(1, 2, 0, 3)]
  transfers between devices with their start and end apart: 9 -> 10, of which waited for: 3 -> 5; matrix products, arithmetic and copies ran while one was open for 4% -> 4% of each run, Pallas kernels for 10% -> 7%
where the time goes in v2:
time: 92.5 us; the launch traced here: 90.8 us
  starting transfers between devices  43 us (46%)
  waiting for transfers between devices  27.2 us (29%)
  Pallas kernels  12.8 us (14%)
  other arithmetic  5.82 us (6%)
  local copies, waits for them, and re-layouts  1.05 us (1%)
    ppermute x3, starting transfers between devices, swap(): return lax.ppermute(array, axis, [(0, 1), (1, 0)])  25.2 us
    all_to_all x1, waiting for transfers between devices, per_device(): lax.all_to_all(jnp.broadcast_to(rounded[None], (YS,) + rounded.shape), 'y...  15.7 us
    ppermute x1, waiting for transfers between devices, with_row_neighbours(): lax.ppermute(last, ANGLE, up)  4.65 us
    pallas_call x1, Pallas kernels, load_project(): pl.pallas_call(partial(load_project_kernel, scale=scale), in_specs=[SMEM,...  4.5 us
    pallas_call x1, Pallas kernels, load_spread(): pl.pallas_call(load_spread_kernel, in_specs=[SMEM, SMEM, SMEM, VMEM, ANY]...  4.41 us
    ppermute x1, starting transfers between devices, with_row_neighbours(): lax.ppermute(last, ANGLE, up)  3.79 us
    all_to_all x1, starting transfers between devices, per_device(): parts = lax.all_to_all(pair, 'y', 0, 0, tiled=True)  3.49 us
    all_to_all x1, starting transfers between devices, per_device(): lax.all_to_all(jnp.broadcast_to(rounded[None], (YS,) + rounded.shape), 'y...  3.49 us
  transfers between devices with their start and end apart: 10, of which 5 were waited for; matrix products, arithmetic and copies ran while one was open for 4% of the time, Pallas kernels for 7%

profile of v2, /device:TPU:1, one launch (start us, length us, event | category | flops | bytes accessed | tf_op | source)
XLA Modules:
  0.0 90.8 jit_solution(13848290327744161539)
XLA Ops:
  0.7 0.1 pad_add_fusion.place
  0.7 4.5 %load_project.1 = (f32[8,2,128,128]{3,2,1,0:T(8,128)S(1)}, bf16[32,4,2,128,128]{4,3,2,1,0:T(8,128)(2,1)S(1)}, bf16[1664,128]{1,0:T(8,128)(2,1)S(1)}, s32[32,128]{1,0:T(8,128)S(4)}, s32[32,128]{1,0:T(8,128)S(4)}) custom-call(s32[2]{0:T(128)S(1)} %pad_add_fusion.place, s32[32,128]{1,0:T(8,128)} %offsets_hbm.1, s32[32,128]{1,0:T(8,128)} %counts_hbm.1, ...), custom_call_target="tpu_custom_call" | custom-call | flops 536870912 | bytes 4194304 | tf_op jit(solution)/shard_map/load_project/pallas_call | solution.py:250
  5.3 0.0 copy-start
  5.3 0.0 copy-start.2
  5.3 12.6 %collective-permute-start = (f32[8,2,128,128]{3,2,1,0:T(8,128)S(1)}, f32[8,2,128,128]{3,2,1,0:T(8,128)S(1)}, u32[]{:S(2)}, u32[]{:S(2)}) collective-permute-start(f32[8,2,128,128]{3,2,1,0:T(8,128)S(1)} %get-tuple-element.19), channel_id=1, source_target_pairs={{0,1},{1,0},{2,3},{3,2},{4,5},{5,4},{6,7},{7,6},{8,9},{9,8},{10,11... | collective-permute-start | bytes 3145736 | tf_op jit(solution)/shard_map/ppermute | solution.py:319
  17.8 1.9 %project.1 = f32[8,2,128,128]{3,2,1,0:T(8,128)S(1)} custom-call(s32[2]{0:T(128)S(1)} %pad_add_fusion.place, s32[32,128]{1,0:T(8,128)S(4)} %get-tuple-element.15.offsets, s32[32,128]{1,0:T(8,128)S(4)} %get-tuple-element.16.counts, bf16[1664,128]{1,0:T(8,128)(2,1)S(1)} %get-tuple-element.17.windows, bf16[32,4,2,128,128]{4,3,2,1,0:T(8,128)(2,1)S(1)} %get-tuple-element.18.tiles), custom_call_target="tpu_custom_call" | custom-call | flops 536870912 | bytes 4194304 | tf_op jit(solution)/shard_map/project/pallas_call | solution.py:273
  19.8 0.3 collective-permute-done
  20.1 0.9 %add_convert_fusion = f16[8,2,128,128]{3,2,1,0:T(8,128)(2,1)} fusion(f32[8,2,128,128]{3,2,1,0:T(8,128)S(1)} %project.1, f32[8,2,128,128]{3,2,1,0:T(8,128)S(1)} %collective-permute-done), kind=kLoop, calls=%fused_computation.1 | loop fusion | flops 524288 | bytes 2621440 | tf_op jit(solution)/shard_map/convert_element_type | solution.py:342
  21.0 3.5 %all-to-all-start = ((f16[8,2,128,128]{3,2,1,0:T(8,128)(2,1)}), f16[8,2,128,128]{3,2,1,0:T(8,128)(2,1)S(1)}, u32[]{:S(2)}, u32[]{:S(2)}) async-start(f16[8,2,128,128]{3,2,1,0:T(8,128)(2,1)} %add_convert_fusion), calls=%async_computation | async-start | bytes 1048576 | tf_op jit(solution)/shard_map/all_to_all | solution.py:343
  24.5 0.0 copy-done
  24.5 0.2 fusion.14
  24.7 0.7 collective-permute-start.3
  25.4 3.8 %collective-permute-start.4 = (bf16[8,1,2048]{2,1,0:T(2,128)(2,1)S(1)}, bf16[8,1,2048]{2,1,0:T(2,128)(2,1)S(1)}, u32[]{:S(2)}, u32[]{:S(2)}) collective-permute-start(bf16[8,1,2048]{2,1,0:T(2,128)(2,1)S(1)} %get-tuple-element.34), channel_id=1, source_target_pairs={{0,1},{1,2},{2,3},{3,4},{4,5},{5,6},{6,7},{7,8},{8,9},{9,10},{10,1... | collective-permute-start | bytes 98312 | tf_op jit(solution)/shard_map/ppermute | solution.py:39
  29.2 1.9 %collective-permute-start.5 = (bf16[8,1,2048]{2,1,0:T(2,128)(2,1)S(1)}, bf16[8,1,2048]{2,1,0:T(2,128)(2,1)S(1)}, u32[]{:S(2)}, u32[]{:S(2)}) collective-permute-start(bf16[8,1,2048]{2,1,0:T(2,128)(2,1)S(1)} %get-tuple-element.36), channel_id=1, source_target_pairs={{1,0},{2,1},{3,2},{4,3},{5,4},{6,5},{7,6},{8,7},{9,8},{10,9},{11,1... | collective-permute-start | bytes 98312 | tf_op jit(solution)/shard_map/ppermute | solution.py:39
  31.1 0.0 collective-permute-done.3
  31.1 4.7 %collective-permute-done.4 = bf16[8,1,2048]{2,1,0:T(2,128)(2,1)S(1)} collective-permute-done((bf16[8,1,2048]{2,1,0:T(2,128)(2,1)S(1)}, bf16[8,1,2048]{2,1,0:T(2,128)(2,1)S(1)}, u32[]{:S(2)}, u32[]{:S(2)}) %collective-permute-start.4) | collective-permute-done | bytes 32800 | tf_op jit(solution)/shard_map/ppermute | solution.py:39
  35.8 3.2 %collective-permute-done.5 = bf16[8,1,2048]{2,1,0:T(2,128)(2,1)S(1)} collective-permute-done((bf16[8,1,2048]{2,1,0:T(2,128)(2,1)S(1)}, bf16[8,1,2048]{2,1,0:T(2,128)(2,1)S(1)}, u32[]{:S(2)}, u32[]{:S(2)}) %collective-permute-start.5) | collective-permute-done | bytes 32800 | tf_op jit(solution)/shard_map/ppermute | solution.py:39
  39.0 0.2 broadcast_select_fusion.2
  39.2 3.3 %all-to-all-done = f16[8,2,128,128]{3,2,1,0:T(8,128)(2,1)S(1)} async-done(((f16[8,2,128,128]{3,2,1,0:T(8,128)(2,1)}), f16[8,2,128,128]{3,2,1,0:T(8,128)(2,1)S(1)}, u32[]{:S(2)}, u32[]{:S(2)}) %all-to-all-start) | async-done | bytes 524320 | tf_op jit(solution)/shard_map/all_to_all | solution.py:343
  42.5 0.1 convert_reduce_fusion
  42.5 0.0 copy-done.2
  42.6 0.1 multiply_convert_fusion
  42.7 9.0 %collective-permute-start.1 = (f16[2,128,128]{2,1,0:T(8,128)(2,1)S(1)}, f16[2,128,128]{2,1,0:T(8,128)(2,1)S(1)}, u32[]{:S(2)}, u32[]{:S(2)}) collective-permute-start(f16[2,128,128]{2,1,0:T(8,128)(2,1)S(1)} %multiply_convert_fusion), channel_id=1, source_target_pairs={{0,16},{16,0},{1,17},{17,1},{2,18},{18,2},{3,19},{19,3},{4,20},{20... | collective-permute-start | bytes 196616 | tf_op jit(solution)/shard_map/ppermute | solution.py:319
  51.7 0.1 pad_maximum_fusion.2
  51.8 3.1 %collective-permute-start.6 = (bf16[1,6,2048]{2,1,0:T(8,128)(2,1)S(1)}, bf16[1,6,2048]{2,1,0:T(8,128)(2,1)S(1)}, u32[]{:S(2)}, u32[]{:S(2)}) collective-permute-start(bf16[1,6,2048]{2,1,0:T(8,128)(2,1)S(1)} %get-tuple-element.32), channel_id=1, source_target_pairs={{0,32},{32,64},{64,96},{96,128},{128,160},{160,192},{192,224},{224... | collective-permute-start | bytes 73736 | tf_op jit(solution)/shard_map/ppermute | solution.py:49
  54.9 1.3 %collective-permute-start.7 = (bf16[1,6,2048]{2,1,0:T(8,128)(2,1)S(1)}, bf16[1,6,2048]{2,1,0:T(8,128)(2,1)S(1)}, u32[]{:S(2)}, u32[]{:S(2)}) collective-permute-start(bf16[1,6,2048]{2,1,0:T(8,128)(2,1)S(1)} %get-tuple-element.33), channel_id=1, source_target_pairs={{32,0},{64,32},{96,64},{128,96},{160,128},{192,160},{224,192},{256... | collective-permute-start | bytes 73736 | tf_op jit(solution)/shard_map/ppermute | solution.py:49
  56.2 0.0 collective-permute-done.1
  56.2 0.1 fusion.13
  56.3 0.9 broadcast_in_dim.35
  57.2 3.5 %all-to-all-start.1 = ((bf16[8,2,128,128]{3,2,1,0:T(8,128)(2,1)}), bf16[8,2,128,128]{3,2,1,0:T(8,128)(2,1)S(1)}, u32[]{:S(2)}, u32[]{:S(2)}) async-start(bf16[8,2,128,128]{3,2,1,0:T(8,128)(2,1)} %broadcast_in_dim.35), calls=%async_computation.1 | async-start | bytes 1048576 | tf_op jit(solution)/shard_map/all_to_all | solution.py:352
  60.7 0.0 collective-permute-done.6
  60.7 0.0 collective-permute-done.7
  60.7 0.5 fusion.1
  61.1 0.5 fusion.9
  61.6 15.7 %all-to-all-done.1.views = bf16[8,2,128,128]{3,2,1,0:T(8,128)(2,1)S(1)} async-done(((bf16[8,2,128,128]{3,2,1,0:T(8,128)(2,1)}), bf16[8,2,128,128]{3,2,1,0:T(8,128)(2,1)S(1)}, u32[]{:S(2)}, u32[]{:S(2)}) %all-to-all-start.1) | async-done | bytes 524320 | tf_op jit(solution)/shard_map/all_to_all | solution.py:352
  77.3 3.6 %collective-permute-start.2 = (bf16[8,2,128,128]{3,2,1,0:T(8,128)(2,1)S(1)}, bf16[8,2,128,128]{3,2,1,0:T(8,128)(2,1)S(1)}, u32[]{:S(2)}, u32[]{:S(2)}) collective-permute-start(bf16[8,2,128,128]{3,2,1,0:T(8,128)(2,1)S(1)} %all-to-all-done.1.views), channel_id=1, source_target_pairs={{0,1},{1,0},{2,3},{3,2},{4,5},{5,4},{6,7},{7,6},{8,9},{9,8},{10,11... | collective-permute-start | bytes 1572872 | tf_op jit(solution)/shard_map/ppermute | solution.py:319
  80.9 1.1 %fusion.10 = (f32[9,5,2049]{2,1,0:T(8,128)S(1)}, f32[9,5,2049]{2,1,0:T(8,128)}) fusion(f32[9,5,2049]{2,1,0:T(8,128)S(1)} %get-tuple-element.29, f32[10,6,2050]{2,1,0:T(8,128)S(1)} %fusion.1), kind=kLoop, calls=%fused_computation.26 | loop fusion | flops 368820 | bytes 2212920 | tf_op jit(solution)/shard_map/div | solution.py:59
  82.1 0.6 fusion.12
  82.7 0.0 copy-start.1
  82.7 4.4 %load_spread.1 = (f32[4,128,128]{2,1,0:T(8,128)S(1)}, bf16[32,4,2,128,128]{4,3,2,1,0:T(8,128)(2,1)S(1)}) custom-call(s32[2]{0:T(128)S(1)} %pad_add_fusion.place, s32[32,128]{1,0:T(8,128)S(4)} %get-tuple-element.15.offsets, s32[32,128]{1,0:T(8,128)S(4)} %get-tuple-element.16.counts, bf16[8,2,128,128]{3,2,1,0:T(8,128)(2,1)S(1)} %all-to-all-done.1.views, ...), custom_call_target="tpu_custom_call" | custom-call | flops 536870912 | bytes 4194304 | tf_op jit(solution)/shard_map/load_spread/pallas_call | solution.py:286
  87.1 0.0 collective-permute-done.2.views
  87.1 2.0 %spread.1 = f32[4,128,128]{2,1,0:T(8,128)S(1)} custom-call(s32[2]{0:T(128)S(1)} %pad_add_fusion.place, s32[32,128]{1,0:T(8,128)S(4)} %get-tuple-element.15.offsets, s32[32,128]{1,0:T(8,128)S(4)} %get-tuple-element.16.counts, bf16[8,2,128,128]{3,2,1,0:T(8,128)(2,1)S(1)} %collective-permute-done.2.views, ...), custom_call_target="tpu_custom_call" | custom-call | flops 536870912 | bytes 4194304 | tf_op jit(solution)/shard_map/spread/pallas_call | solution.py:306
  89.1 0.1 copy.7
  89.2 0.1 mul.70
  89.3 0.0 copy-done.1
  89.3 1.5 %fusion.8 = f32[8,4,2048]{2,1,0:T(4,128)} fusion(f32[9,5,2049]{2,1,0:T(8,128)S(1)} %copy-done.1, f32[9,5,2049]{2,1,0:T(8,128)S(1)} %get-tuple-element.30, f32[9,5,2049]{2,1,0:T(8,128)S(1)} %get-tuple-element.28, f32[8,4,2048]{2,1,0:T(4,128)S(1)} %mul.70, bf16[8,4,2048]{2,1,0:T(4,128)(2,1)S(1)} %copy-done), kind=kLoop, calls=%fused_computation.19 | loop fusion | flops 589824 | bytes 2228224 | tf_op jit(solution)/shard_map/add | solution.py:364
  (2 shorter events, 0.0 us)
Async XLA Ops:
  5.3 19.3 %copy-start = (bf16[8,4,2048]{2,1,0:T(4,128)(2,1)S(1)}, bf16[8,4,2048]{2,1,0:T(4,128)(2,1)}, u32[]{:S(2)}) copy-start(bf16[8,4,2048]{2,1,0:T(4,128)(2,1)} %volume_hbm.1) | copy-start | bytes 393220
  5.3 37.3 %copy-start.2 = (f32[1,8,2048]{2,1,0:T(8,128)S(1)}, f32[1,8,2048]{2,1,0:T(8,128)}, u32[]{:S(2)}) copy-start(f32[1,8,2048]{2,1,0:T(8,128)} %param.6) | copy-start | bytes 196612
  5.3 14.8 %collective-permute-start = (f32[8,2,128,128]{3,2,1,0:T(8,128)S(1)}, f32[8,2,128,128]{3,2,1,0:T(8,128)S(1)}, u32[]{:S(2)}, u32[]{:S(2)}) collective-permute-start(f32[8,2,128,128]{3,2,1,0:T(8,128)S(1)} %get-tuple-element.19), channel_id=1, source_target_pairs={{0,1},{1,0},{2,3},{3,2},{4,5},{5,4},{6,7},{7,6},{8,9},{9,8},{10,11... | collective-permute-start | bytes 3145736 | tf_op jit(solution)/shard_map/ppermute | solution.py:319
  21.0 21.4 %all-to-all-start = ((f16[8,2,128,128]{3,2,1,0:T(8,128)(2,1)}), f16[8,2,128,128]{3,2,1,0:T(8,128)(2,1)S(1)}, u32[]{:S(2)}, u32[]{:S(2)}) async-start(f16[8,2,128,128]{3,2,1,0:T(8,128)(2,1)} %add_convert_fusion), calls=%async_computation | async-start | bytes 1048576 | tf_op jit(solution)/shard_map/all_to_all | solution.py:343
  24.7 6.4 %collective-permute-start.3 = (bf16[8,1,2048]{2,1,0:T(2,128)(2,1)S(1)}, bf16[8,1,2048]{2,1,0:T(2,128)(2,1)S(1)}, u32[]{:S(2)}, u32[]{:S(2)}) collective-permute-start(bf16[8,1,2048]{2,1,0:T(2,128)(2,1)S(1)} %get-tuple-element.35), channel_id=1, source_target_pairs={{15,16},{16,15},{47,48},{48,47},{79,80},{80,79},{111,112},{112,111... | collective-permute-start | bytes 98312 | tf_op jit(solution)/shard_map/ppermute | solution.py:40
  25.4 10.4 %collective-permute-start.4 = (bf16[8,1,2048]{2,1,0:T(2,128)(2,1)S(1)}, bf16[8,1,2048]{2,1,0:T(2,128)(2,1)S(1)}, u32[]{:S(2)}, u32[]{:S(2)}) collective-permute-start(bf16[8,1,2048]{2,1,0:T(2,128)(2,1)S(1)} %get-tuple-element.34), channel_id=1, source_target_pairs={{0,1},{1,2},{2,3},{3,4},{4,5},{5,6},{6,7},{7,8},{8,9},{9,10},{10,1... | collective-permute-start | bytes 98312 | tf_op jit(solution)/shard_map/ppermute | solution.py:39
  29.2 9.8 %collective-permute-start.5 = (bf16[8,1,2048]{2,1,0:T(2,128)(2,1)S(1)}, bf16[8,1,2048]{2,1,0:T(2,128)(2,1)S(1)}, u32[]{:S(2)}, u32[]{:S(2)}) collective-permute-start(bf16[8,1,2048]{2,1,0:T(2,128)(2,1)S(1)} %get-tuple-element.36), channel_id=1, source_target_pairs={{1,0},{2,1},{3,2},{4,3},{5,4},{6,5},{7,6},{8,7},{9,8},{10,9},{11,1... | collective-permute-start | bytes 98312 | tf_op jit(solution)/shard_map/ppermute | solution.py:39
  42.7 13.5 %collective-permute-start.1 = (f16[2,128,128]{2,1,0:T(8,128)(2,1)S(1)}, f16[2,128,128]{2,1,0:T(8,128)(2,1)S(1)}, u32[]{:S(2)}, u32[]{:S(2)}) collective-permute-start(f16[2,128,128]{2,1,0:T(8,128)(2,1)S(1)} %multiply_convert_fusion), channel_id=1, source_target_pairs={{0,16},{16,0},{1,17},{17,1},{2,18},{18,2},{3,19},{19,3},{4,20},{20... | collective-permute-start | bytes 196616 | tf_op jit(solution)/shard_map/ppermute | solution.py:319
  51.8 8.9 %collective-permute-start.6 = (bf16[1,6,2048]{2,1,0:T(8,128)(2,1)S(1)}, bf16[1,6,2048]{2,1,0:T(8,128)(2,1)S(1)}, u32[]{:S(2)}, u32[]{:S(2)}) collective-permute-start(bf16[1,6,2048]{2,1,0:T(8,128)(2,1)S(1)} %get-tuple-element.32), channel_id=1, source_target_pairs={{0,32},{32,64},{64,96},{96,128},{128,160},{160,192},{192,224},{224... | collective-permute-start | bytes 73736 | tf_op jit(solution)/shard_map/ppermute | solution.py:49
  54.9 5.8 %collective-permute-start.7 = (bf16[1,6,2048]{2,1,0:T(8,128)(2,1)S(1)}, bf16[1,6,2048]{2,1,0:T(8,128)(2,1)S(1)}, u32[]{:S(2)}, u32[]{:S(2)}) collective-permute-start(bf16[1,6,2048]{2,1,0:T(8,128)(2,1)S(1)} %get-tuple-element.33), channel_id=1, source_target_pairs={{32,0},{64,32},{96,64},{128,96},{160,128},{192,160},{224,192},{256... | collective-permute-start | bytes 73736 | tf_op jit(solution)/shard_map/ppermute | solution.py:49
  57.2 20.2 %all-to-all-start.1 = ((bf16[8,2,128,128]{3,2,1,0:T(8,128)(2,1)}), bf16[8,2,128,128]{3,2,1,0:T(8,128)(2,1)S(1)}, u32[]{:S(2)}, u32[]{:S(2)}) async-start(bf16[8,2,128,128]{3,2,1,0:T(8,128)(2,1)} %broadcast_in_dim.35), calls=%async_computation.1 | async-start | bytes 1048576 | tf_op jit(solution)/shard_map/all_to_all | solution.py:352
  77.3 9.8 %collective-permute-start.2 = (bf16[8,2,128,128]{3,2,1,0:T(8,128)(2,1)S(1)}, bf16[8,2,128,128]{3,2,1,0:T(8,128)(2,1)S(1)}, u32[]{:S(2)}, u32[]{:S(2)}) collective-permute-start(bf16[8,2,128,128]{3,2,1,0:T(8,128)(2,1)S(1)} %all-to-all-done.1.views), channel_id=1, source_target_pairs={{0,1},{1,0},{2,3},{3,2},{4,5},{5,4},{6,7},{7,6},{8,9},{9,8},{10,11... | collective-permute-start | bytes 1572872 | tf_op jit(solution)/shard_map/ppermute | solution.py:319
  82.7 6.6 %copy-start.1 = (f32[9,5,2049]{2,1,0:T(8,128)S(1)}, f32[9,5,2049]{2,1,0:T(8,128)}, u32[]{:S(2)}) copy-start(f32[9,5,2049]{2,1,0:T(8,128)} %get-tuple-element.31) | copy-start | bytes 1106464

commit v3 on v2

--- a/solution.py
+++ b/solution.py
@@ -218,10 +218,16 @@
         copy.wait()
 
 
-def spread_kernel(place, offsets, counts, views, tiles, begin, out, windows):
+def spread_kernel(place, offsets, counts, views, tiles, begin, base, out, total, windows):
     fill_views(windows, views)
     for first in range(0, ZHI * YS, GROUP):
-        spread_group(first, 1 - place[0], place[1], offsets, counts, windows, tiles, begin, out)
+        spread_group(first, 1 - place[0], place[1], offsets, counts, windows, tiles, begin, total)
+    depth, rows, width = out.shape
+    lanes = total.shape[2]
+    for r in range(rows):
+        for t in range(width // lanes):
+            here = slice(t * lanes, (t + 1) * lanes)
+            out[:, r, here] = base[:, r, here] - step_size * total[r, t * depth : (t + 1) * depth, :]
 
 
 ANY = pl.BlockSpec(memory_space=pl.ANY)
@@ -301,18 +307,39 @@
     )(place, offsets, counts, views, in_hbm(tiles))
 
 
-def spread(place, offsets, counts, views, tiles, begin):
+def spread(place, offsets, counts, views, tiles, begin, base):
     count, lanes = views.shape[2:]
     return pl.pallas_call(
         spread_kernel,
-        in_specs=[SMEM, SMEM, SMEM, VMEM, VMEM, VMEM],
+        in_specs=[SMEM, SMEM, SMEM] + [VMEM] * 4,
         out_specs=VMEM,
-        out_shape=pltpu.VMEM((tiles.shape[1], count, lanes), jnp.float32),
-        scratch_shapes=[pltpu.VMEM((window_rows(ZHI * YS, count), lanes), jnp.bfloat16)],
+        out_shape=jax.ShapeDtypeStruct(base.shape, base.dtype),
+        scratch_shapes=[
+            pltpu.VMEM(begin.shape, begin.dtype),
+            pltpu.VMEM((window_rows(ZHI * YS, count), lanes), jnp.bfloat16),
+        ],
         compiler_params=params(),
         cost_estimate=cost(tiles, 2),
         name="spread",
-    )(place, offsets, counts, views, tiles, begin)
+    )(place, offsets, counts, views, tiles, begin, base)
+
+
+def own_view_kernel(place, both, out):
+    depth, lanes = out.shape[1], both.shape[2]
+    for t in range(out.shape[2] // lanes):
+        out[0, :, t * lanes : (t + 1) * lanes] = both[place[2], t * depth : (t + 1) * depth, :]
+
+
+def own_view(place, both, like):
+    return pl.pallas_call(
+        own_view_kernel,
+        in_specs=[SMEM, VMEM],
+        out_specs=VMEM,
+        out_shape=jax.ShapeDtypeStruct(like.shape, like.dtype),
+        compiler_params=params(),
+        cost_estimate=pl.CostEstimate(flops=0, bytes_accessed=8 * like.size, transcendentals=0),
+        name="own_view",
+    )(place, both)
 
 
 def swap(array, axis):
@@ -330,8 +357,8 @@
     first_row = me * row_count
     gap = lax.axis_size(ANGLE) // ZHI - 1
     is_mine = lax.broadcasted_iota(jnp.int32, (ZHI, 1, 1), 0) == zhi
-    place, is_mine, low_plane, ends_plane, begins_plane = lax.optimization_barrier(
-        (jnp.stack([core, first_row]), is_mine, zhi == 0, me == gap, me == gap + 1)
+    place, is_mine, ends_plane, begins_plane = lax.optimization_barrier(
+        (jnp.stack([core, first_row, zhi]), is_mine, me == gap, me == gap + 1)
     )
 
     away, tiles, windows, offsets, counts = load_project(
@@ -346,22 +373,16 @@
     plane = plane - jnp.where(is_mine, seen[None], 0.0)
     far = swap((plane * PLANE_SCALE).astype(f16), "zhi")
     both = plane + far.astype(f32) * (1 / PLANE_SCALE)
-    residual = jnp.where(low_plane, both[0], both[1])
-    residual = residual.reshape(tile_count, depth, tile).transpose(1, 0, 2).reshape(1, depth, width)
-    rounded = both.astype(bf16)
-    views = lax.all_to_all(
-        jnp.broadcast_to(rounded[None], (YS,) + rounded.shape), "y", 0, 0, tiled=True
-    )
+    residual = own_view(place, both, measured)
+    copies = jnp.broadcast_to(both.astype(bf16)[None], (YS,) + both.shape)
+    with_rows = with_row_neighbours(volume, ends_plane, begins_plane)
+    views = lax.all_to_all(copies, "y", 0, 0, tiled=True)
+    field = jnp.pad(with_slab_neighbours(with_rows).astype(f32), ((0, 0), (0, 0), (1, 1)))
+    base = volume.astype(f32) + step_size * smooth_weight * divergence(field)
+    views, base, residual = lax.optimization_barrier((views, base, residual))
     views_other = swap(views, "core")
     gradient, tiles = load_spread(place, offsets, counts, views, ray_tiles)
-    gradient = spread(place, offsets, counts, views_other, tiles, gradient)
-    gradient = (
-        gradient.reshape(row_count, tile_count, depth, tile).transpose(2, 0, 1, 3).reshape(depth, row_count, width)
-    )
-
-    beside_all = with_slab_neighbours(with_row_neighbours(volume, ends_plane, begins_plane))
-    field = jnp.pad(beside_all.astype(f32), ((0, 0), (0, 0), (1, 1)))
-    updated = volume.astype(f32) - step_size * gradient + step_size * smooth_weight * divergence(field)
+    updated = spread(place, offsets, counts, views_other, tiles, gradient, base)
     return (updated, residual)
 
 

time: 92.5 us -> 96.9 us (1.048); the launches traced: 90.8 us -> 96.4 us
  waiting for transfers between devices: 27.2 us -> 34.6 us
  other arithmetic: 5.82 us -> 3.62 us
  Pallas kernels: 12.8 us -> 14.9 us
  starting transfers between devices: 43 us -> 41.5 us
    ppermute x3, waiting for transfers between devices: 0.35 us -> 9.08 us  [swap(): return lax.ppermute(array, axis, [(0, 1), (1, 0)])]
    all_to_all x1, waiting for transfers between devices: 3.3 us -> 11 us  [per_device(): parts = lax.all_to_all(pair, 'y', 0, 0, tiled=True)]
    ppermute x3, starting transfers between devices: 25.2 us -> 19 us  [swap(): return lax.ppermute(array, axis, [(0, 1), (1, 0)])]
    all_to_all x1, starting transfers between devices: 3.49 us -> 8.75 us  [per_device(): parts = lax.all_to_all(pair, 'y', 0, 0, tiled=True)]
    ppermute x1, waiting for transfers between devices: 4.65 us -> 0.01 us  [with_row_neighbours(): lax.ppermute(last, ANGLE, up)]
    ppermute x1, waiting for transfers between devices: 3.2 us -> 0.01 us  [with_row_neighbours(): lax.ppermute(first, ANGLE, down)]
    all_to_all x1, waiting for transfers between devices: 15.7 us -> 13.5 us  [per_device(): views = lax.all_to_all(copies, 'y', 0, 0, tiled=True)]
    pallas_call x1 -> x2, Pallas kernels: 1.97 us -> 4.02 us  [the longest x1 2.84 us: spread(): pl.pallas_call(spread_kernel, in_specs=[SMEM, SMEM, SMEM] + [VMEM] * 4, o...]
  transfers between devices with their start and end apart: 10 -> 10, of which waited for: 5 -> 4; matrix products, arithmetic and copies ran while one was open for 4% -> 3% of each run, Pallas kernels for 7% -> 8%
where the time goes in v3:
time: 96.9 us; the launch traced here: 96.4 us
  starting transfers between devices  41.5 us (43%)
  waiting for transfers between devices  34.6 us (36%)
  Pallas kernels  14.9 us (15%)
  other arithmetic  3.62 us (4%)
    ppermute x3, starting transfers between devices, swap(): return lax.ppermute(array, axis, [(0, 1), (1, 0)])  19 us
    all_to_all x1, waiting for transfers between devices, per_device(): views = lax.all_to_all(copies, 'y', 0, 0, tiled=True)  13.5 us
    all_to_all x1, waiting for transfers between devices, per_device(): parts = lax.all_to_all(pair, 'y', 0, 0, tiled=True)  11 us
    ppermute x3, waiting for transfers between devices, swap(): return lax.ppermute(array, axis, [(0, 1), (1, 0)])  9.08 us
    all_to_all x1, starting transfers between devices, per_device(): parts = lax.all_to_all(pair, 'y', 0, 0, tiled=True)  8.75 us
    pallas_call x1, Pallas kernels, load_project(): pl.pallas_call(partial(load_project_kernel, scale=scale), in_specs=[SMEM,...  4.5 us
    pallas_call x1, Pallas kernels, load_spread(): pl.pallas_call(load_spread_kernel, in_specs=[SMEM, SMEM, SMEM, VMEM, ANY]...  4.42 us
    ppermute x1, starting transfers between devices, with_slab_neighbours(): lax.ppermute(last, SLAB, up)  3.99 us
  transfers between devices with their start and end apart: 10, of which 4 were waited for; matrix products, arithmetic and copies ran while one was open for 3% of the time, Pallas kernels for 8%

profile of v3, /device:TPU:1, one launch (start us, length us, event | category | flops | bytes accessed | tf_op | source)
XLA Modules:
  0.0 96.4 jit_solution(1699792704541646725)
XLA Ops:
  0.6 0.0 copy-start
  0.7 0.1 pad_add_fusion.place
  0.8 4.5 %load_project.1 = (f32[8,2,128,128]{3,2,1,0:T(8,128)S(1)}, bf16[32,4,2,128,128]{4,3,2,1,0:T(8,128)(2,1)S(1)}, bf16[1664,128]{1,0:T(8,128)(2,1)S(1)}, s32[32,128]{1,0:T(8,128)S(4)}, s32[32,128]{1,0:T(8,128)S(4)}) custom-call(s32[3]{0:T(128)S(1)} %pad_add_fusion.place, s32[32,128]{1,0:T(8,128)} %offsets_hbm.1, s32[32,128]{1,0:T(8,128)} %counts_hbm.1, ...), custom_call_target="tpu_custom_call" | custom-call | flops 536870912 | bytes 4194304 | tf_op jit(solution)/shard_map/load_project/pallas_call | solution.py:256
  5.3 0.0 copy-start.1
  5.3 12.6 %collective-permute-start = (f32[8,2,128,128]{3,2,1,0:T(8,128)S(1)}, f32[8,2,128,128]{3,2,1,0:T(8,128)S(1)}, u32[]{:S(2)}, u32[]{:S(2)}) collective-permute-start(f32[8,2,128,128]{3,2,1,0:T(8,128)S(1)} %get-tuple-element.21), channel_id=1, source_target_pairs={{0,1},{1,0},{2,3},{3,2},{4,5},{5,4},{6,7},{7,6},{8,9},{9,8},{10,11... | collective-permute-start | bytes 3145736 | tf_op jit(solution)/shard_map/ppermute | solution.py:346
  17.8 0.0 copy-done
  17.9 0.2 fusion.13
  18.0 0.7 collective-permute-start.2
  18.7 1.9 %collective-permute-start.3 = (bf16[8,1,2048]{2,1,0:T(2,128)(2,1)S(1)}, bf16[8,1,2048]{2,1,0:T(2,128)(2,1)S(1)}, u32[]{:S(2)}, u32[]{:S(2)}) collective-permute-start(bf16[8,1,2048]{2,1,0:T(2,128)(2,1)S(1)} %get-tuple-element.38), channel_id=1, source_target_pairs={{0,1},{1,2},{2,3},{3,4},{4,5},{5,6},{6,7},{7,8},{8,9},{9,10},{10,1... | collective-permute-start | bytes 98312 | tf_op jit(solution)/shard_map/ppermute | solution.py:39
  20.6 2.4 %collective-permute-start.4 = (bf16[8,1,2048]{2,1,0:T(2,128)(2,1)S(1)}, bf16[8,1,2048]{2,1,0:T(2,128)(2,1)S(1)}, u32[]{:S(2)}, u32[]{:S(2)}) collective-permute-start(bf16[8,1,2048]{2,1,0:T(2,128)(2,1)S(1)} %get-tuple-element.40), channel_id=1, source_target_pairs={{1,0},{2,1},{3,2},{4,3},{5,4},{6,5},{7,6},{8,7},{9,8},{10,9},{11,1... | collective-permute-start | bytes 98312 | tf_op jit(solution)/shard_map/ppermute | solution.py:39
  23.0 1.9 %project.1 = f32[8,2,128,128]{3,2,1,0:T(8,128)S(1)} custom-call(s32[3]{0:T(128)S(1)} %pad_add_fusion.place, s32[32,128]{1,0:T(8,128)S(4)} %get-tuple-element.17.offsets, s32[32,128]{1,0:T(8,128)S(4)} %get-tuple-element.18.counts, bf16[1664,128]{1,0:T(8,128)(2,1)S(1)} %get-tuple-element.19.windows, bf16[32,4,2,128,128]{4,3,2,1,0:T(8,128)(2,1)S(1)} %get-tuple-element.20.tiles), custom_call_target="tpu_custom_call" | custom-call | flops 536870912 | bytes 4194304 | tf_op jit(solution)/shard_map/project/pallas_call | solution.py:279
  25.0 0.0 collective-permute-done
  25.0 0.9 add_convert_fusion
  25.9 8.7 %all-to-all-start = ((f16[8,2,128,128]{3,2,1,0:T(8,128)(2,1)}), f16[8,2,128,128]{3,2,1,0:T(8,128)(2,1)S(1)}, u32[]{:S(2)}, u32[]{:S(2)}) async-start(f16[8,2,128,128]{3,2,1,0:T(8,128)(2,1)} %add_convert_fusion), calls=%async_computation | async-start | bytes 1048576 | tf_op jit(solution)/shard_map/all_to_all | solution.py:370
  34.7 0.0 collective-permute-done.2
  34.7 0.0 collective-permute-done.3
  34.7 0.0 collective-permute-done.4
  34.7 0.2 broadcast_select_fusion.2
  34.9 0.1 pad_maximum_fusion.2
  34.9 1.3 %collective-permute-start.6 = (bf16[1,6,2048]{2,1,0:T(8,128)(2,1)S(1)}, bf16[1,6,2048]{2,1,0:T(8,128)(2,1)S(1)}, u32[]{:S(2)}, u32[]{:S(2)}) collective-permute-start(bf16[1,6,2048]{2,1,0:T(8,128)(2,1)S(1)} %get-tuple-element.37), channel_id=1, source_target_pairs={{32,0},{64,32},{96,64},{128,96},{160,128},{192,160},{224,192},{256... | collective-permute-start | bytes 73736 | tf_op jit(solution)/shard_map/ppermute | solution.py:49
  36.2 4.0 %collective-permute-start.5 = (bf16[1,6,2048]{2,1,0:T(8,128)(2,1)S(1)}, bf16[1,6,2048]{2,1,0:T(8,128)(2,1)S(1)}, u32[]{:S(2)}, u32[]{:S(2)}) collective-permute-start(bf16[1,6,2048]{2,1,0:T(8,128)(2,1)S(1)} %get-tuple-element.36), channel_id=1, source_target_pairs={{0,32},{32,64},{64,96},{96,128},{128,160},{160,192},{192,224},{224... | collective-permute-start | bytes 73736 | tf_op jit(solution)/shard_map/ppermute | solution.py:49
  40.2 0.0 collective-permute-done.6
  40.2 1.0 %collective-permute-done.5 = bf16[1,6,2048]{2,1,0:T(8,128)(2,1)S(1)} collective-permute-done((bf16[1,6,2048]{2,1,0:T(8,128)(2,1)S(1)}, bf16[1,6,2048]{2,1,0:T(8,128)(2,1)S(1)}, u32[]{:S(2)}, u32[]{:S(2)}) %collective-permute-start.5) | collective-permute-done | bytes 24608 | tf_op jit(solution)/shard_map/ppermute | solution.py:49
  41.2 0.5 fusion.1
  41.7 11.0 %all-to-all-done = f16[8,2,128,128]{3,2,1,0:T(8,128)(2,1)S(1)} async-done(((f16[8,2,128,128]{3,2,1,0:T(8,128)(2,1)}), f16[8,2,128,128]{3,2,1,0:T(8,128)(2,1)S(1)}, u32[]{:S(2)}, u32[]{:S(2)}) %all-to-all-start) | async-done | bytes 524320 | tf_op jit(solution)/shard_map/all_to_all | solution.py:370
  52.7 0.1 convert_reduce_fusion
  52.8 0.0 copy-done.1
  52.8 0.1 multiply_convert_fusion
  52.9 1.9 %collective-permute-start.1 = (f16[2,128,128]{2,1,0:T(8,128)(2,1)S(1)}, f16[2,128,128]{2,1,0:T(8,128)(2,1)S(1)}, u32[]{:S(2)}, u32[]{:S(2)}) collective-permute-start(f16[2,128,128]{2,1,0:T(8,128)(2,1)S(1)} %multiply_convert_fusion), channel_id=1, source_target_pairs={{0,16},{16,0},{1,17},{17,1},{2,18},{18,2},{3,19},{19,3},{4,20},{20... | collective-permute-start | bytes 196616 | tf_op jit(solution)/shard_map/ppermute | solution.py:346
  54.8 0.5 fusion.9
  55.3 9.1 %collective-permute-done.1 = f16[2,128,128]{2,1,0:T(8,128)(2,1)S(1)} collective-permute-done((f16[2,128,128]{2,1,0:T(8,128)(2,1)S(1)}, f16[2,128,128]{2,1,0:T(8,128)(2,1)S(1)}, u32[]{:S(2)}, u32[]{:S(2)}) %collective-permute-start.1) | collective-permute-done | bytes 65568 | tf_op jit(solution)/shard_map/ppermute | solution.py:346
  64.3 0.1 fusion.12
  64.4 0.9 broadcast_in_dim.35
  65.3 3.5 %all-to-all-start.1 = ((bf16[8,2,128,128]{3,2,1,0:T(8,128)(2,1)}), bf16[8,2,128,128]{3,2,1,0:T(8,128)(2,1)S(1)}, u32[]{:S(2)}, u32[]{:S(2)}) async-start(bf16[8,2,128,128]{3,2,1,0:T(8,128)(2,1)} %broadcast_in_dim.35), calls=%async_computation.1 | async-start | bytes 1048576 | tf_op jit(solution)/shard_map/all_to_all | solution.py:379
  68.8 0.3 fusion.10
  69.1 0.8 fusion.8.base
  69.9 1.2 %own_view.1 = f32[1,8,2048]{2,1,0:T(8,128)} custom-call(s32[3]{0:T(128)S(1)} %pad_add_fusion.place, f32[2,128,128]{2,1,0:T(8,128)S(1)} %get-tuple-element.33.both), custom_call_target="tpu_custom_call" | custom-call | bytes 131072 | tf_op jit(solution)/shard_map/own_view/pallas_call | solution.py:334
  71.1 13.5 %all-to-all-done.1.views = bf16[8,2,128,128]{3,2,1,0:T(8,128)(2,1)S(1)} async-done(((bf16[8,2,128,128]{3,2,1,0:T(8,128)(2,1)}), bf16[8,2,128,128]{3,2,1,0:T(8,128)(2,1)S(1)}, u32[]{:S(2)}, u32[]{:S(2)}) %all-to-all-start.1) | async-done | bytes 524320 | tf_op jit(solution)/shard_map/all_to_all | solution.py:379
  84.6 4.5 %collective-permute-start.7 = (bf16[8,2,128,128]{3,2,1,0:T(8,128)(2,1)S(1)}, bf16[8,2,128,128]{3,2,1,0:T(8,128)(2,1)S(1)}, u32[]{:S(2)}, u32[]{:S(2)}) collective-permute-start(bf16[8,2,128,128]{3,2,1,0:T(8,128)(2,1)S(1)} %all-to-all-done.1.views), channel_id=1, source_target_pairs={{0,1},{1,0},{2,3},{3,2},{4,5},{5,4},{6,7},{7,6},{8,9},{9,8},{10,11... | collective-permute-start | bytes 1572872 | tf_op jit(solution)/shard_map/ppermute | solution.py:346
  89.1 4.4 %load_spread.1 = (f32[4,128,128]{2,1,0:T(8,128)S(1)}, bf16[32,4,2,128,128]{4,3,2,1,0:T(8,128)(2,1)S(1)}) custom-call(s32[3]{0:T(128)S(1)} %pad_add_fusion.place, s32[32,128]{1,0:T(8,128)S(4)} %get-tuple-element.17.offsets, s32[32,128]{1,0:T(8,128)S(4)} %get-tuple-element.18.counts, bf16[8,2,128,128]{3,2,1,0:T(8,128)(2,1)S(1)} %all-to-all-done.1.views, ...), custom_call_target="tpu_custom_call" | custom-call | flops 536870912 | bytes 4194304 | tf_op jit(solution)/shard_map/load_spread/pallas_call | solution.py:292
  93.5 0.0 collective-permute-done.7.views
  93.5 2.8 %spread.1 = f32[8,4,2048]{2,1,0:T(4,128)} custom-call(s32[3]{0:T(128)S(1)} %pad_add_fusion.place, s32[32,128]{1,0:T(8,128)S(4)} %get-tuple-element.17.offsets, s32[32,128]{1,0:T(8,128)S(4)} %get-tuple-element.18.counts, bf16[8,2,128,128]{3,2,1,0:T(8,128)(2,1)S(1)} %collective-permute-done.7.views, bf16[32,4,2,128,128]{4,3,2,1,0:T(8,128)(2,1)S(1)} %get-tuple-element.26.tiles, ...), custom_call_target="tpu_custom_call" | custom-call | flops 536870912 | bytes 4194304 | tf_op jit(solution)/shard_map/spread/pallas_call | solution.py:312
  (1 shorter events, 0.0 us)
Async XLA Ops:
  0.6 17.2 %copy-start = (bf16[8,4,2048]{2,1,0:T(4,128)(2,1)S(1)}, bf16[8,4,2048]{2,1,0:T(4,128)(2,1)}, u32[]{:S(2)}) copy-start(bf16[8,4,2048]{2,1,0:T(4,128)(2,1)} %volume_hbm.1) | copy-start | bytes 393220
  5.3 47.5 %copy-start.1 = (f32[1,8,2048]{2,1,0:T(8,128)S(1)}, f32[1,8,2048]{2,1,0:T(8,128)}, u32[]{:S(2)}) copy-start(f32[1,8,2048]{2,1,0:T(8,128)} %param.6) | copy-start | bytes 196612
  5.3 19.7 %collective-permute-start = (f32[8,2,128,128]{3,2,1,0:T(8,128)S(1)}, f32[8,2,128,128]{3,2,1,0:T(8,128)S(1)}, u32[]{:S(2)}, u32[]{:S(2)}) collective-permute-start(f32[8,2,128,128]{3,2,1,0:T(8,128)S(1)} %get-tuple-element.21), channel_id=1, source_target_pairs={{0,1},{1,0},{2,3},{3,2},{4,5},{5,4},{6,7},{7,6},{8,9},{9,8},{10,11... | collective-permute-start | bytes 3145736 | tf_op jit(solution)/shard_map/ppermute | solution.py:346
  18.0 16.6 %collective-permute-start.2 = (bf16[8,1,2048]{2,1,0:T(2,128)(2,1)S(1)}, bf16[8,1,2048]{2,1,0:T(2,128)(2,1)S(1)}, u32[]{:S(2)}, u32[]{:S(2)}) collective-permute-start(bf16[8,1,2048]{2,1,0:T(2,128)(2,1)S(1)} %get-tuple-element.39), channel_id=1, source_target_pairs={{15,16},{16,15},{47,48},{48,47},{79,80},{80,79},{111,112},{112,111... | collective-permute-start | bytes 98312 | tf_op jit(solution)/shard_map/ppermute | solution.py:40
  18.7 16.0 %collective-permute-start.3 = (bf16[8,1,2048]{2,1,0:T(2,128)(2,1)S(1)}, bf16[8,1,2048]{2,1,0:T(2,128)(2,1)S(1)}, u32[]{:S(2)}, u32[]{:S(2)}) collective-permute-start(bf16[8,1,2048]{2,1,0:T(2,128)(2,1)S(1)} %get-tuple-element.38), channel_id=1, source_target_pairs={{0,1},{1,2},{2,3},{3,4},{4,5},{5,6},{6,7},{7,8},{8,9},{9,10},{10,1... | collective-permute-start | bytes 98312 | tf_op jit(solution)/shard_map/ppermute | solution.py:39
  20.6 14.1 %collective-permute-start.4 = (bf16[8,1,2048]{2,1,0:T(2,128)(2,1)S(1)}, bf16[8,1,2048]{2,1,0:T(2,128)(2,1)S(1)}, u32[]{:S(2)}, u32[]{:S(2)}) collective-permute-start(bf16[8,1,2048]{2,1,0:T(2,128)(2,1)S(1)} %get-tuple-element.40), channel_id=1, source_target_pairs={{1,0},{2,1},{3,2},{4,3},{5,4},{6,5},{7,6},{8,7},{9,8},{10,9},{11,1... | collective-permute-start | bytes 98312 | tf_op jit(solution)/shard_map/ppermute | solution.py:39
  25.9 26.8 %all-to-all-start = ((f16[8,2,128,128]{3,2,1,0:T(8,128)(2,1)}), f16[8,2,128,128]{3,2,1,0:T(8,128)(2,1)S(1)}, u32[]{:S(2)}, u32[]{:S(2)}) async-start(f16[8,2,128,128]{3,2,1,0:T(8,128)(2,1)} %add_convert_fusion), calls=%async_computation | async-start | bytes 1048576 | tf_op jit(solution)/shard_map/all_to_all | solution.py:370
  34.9 5.3 %collective-permute-start.6 = (bf16[1,6,2048]{2,1,0:T(8,128)(2,1)S(1)}, bf16[1,6,2048]{2,1,0:T(8,128)(2,1)S(1)}, u32[]{:S(2)}, u32[]{:S(2)}) collective-permute-start(bf16[1,6,2048]{2,1,0:T(8,128)(2,1)S(1)} %get-tuple-element.37), channel_id=1, source_target_pairs={{32,0},{64,32},{96,64},{128,96},{160,128},{192,160},{224,192},{256... | collective-permute-start | bytes 73736 | tf_op jit(solution)/shard_map/ppermute | solution.py:49
  36.2 5.0 %collective-permute-start.5 = (bf16[1,6,2048]{2,1,0:T(8,128)(2,1)S(1)}, bf16[1,6,2048]{2,1,0:T(8,128)(2,1)S(1)}, u32[]{:S(2)}, u32[]{:S(2)}) collective-permute-start(bf16[1,6,2048]{2,1,0:T(8,128)(2,1)S(1)} %get-tuple-element.36), channel_id=1, source_target_pairs={{0,32},{32,64},{64,96},{96,128},{128,160},{160,192},{192,224},{224... | collective-permute-start | bytes 73736 | tf_op jit(solution)/shard_map/ppermute | solution.py:49
  52.9 11.5 %collective-permute-start.1 = (f16[2,128,128]{2,1,0:T(8,128)(2,1)S(1)}, f16[2,128,128]{2,1,0:T(8,128)(2,1)S(1)}, u32[]{:S(2)}, u32[]{:S(2)}) collective-permute-start(f16[2,128,128]{2,1,0:T(8,128)(2,1)S(1)} %multiply_convert_fusion), channel_id=1, source_target_pairs={{0,16},{16,0},{1,17},{17,1},{2,18},{18,2},{3,19},{19,3},{4,20},{20... | collective-permute-start | bytes 196616 | tf_op jit(solution)/shard_map/ppermute | solution.py:346
  65.3 19.2 %all-to-all-start.1 = ((bf16[8,2,128,128]{3,2,1,0:T(8,128)(2,1)}), bf16[8,2,128,128]{3,2,1,0:T(8,128)(2,1)S(1)}, u32[]{:S(2)}, u32[]{:S(2)}) async-start(bf16[8,2,128,128]{3,2,1,0:T(8,128)(2,1)} %broadcast_in_dim.35), calls=%async_computation.1 | async-start | bytes 1048576 | tf_op jit(solution)/shard_map/all_to_all | solution.py:379
  84.6 9.0 %collective-permute-start.7 = (bf16[8,2,128,128]{3,2,1,0:T(8,128)(2,1)S(1)}, bf16[8,2,128,128]{3,2,1,0:T(8,128)(2,1)S(1)}, u32[]{:S(2)}, u32[]{:S(2)}) collective-permute-start(bf16[8,2,128,128]{3,2,1,0:T(8,128)(2,1)S(1)} %all-to-all-done.1.views), channel_id=1, source_target_pairs={{0,1},{1,0},{2,3},{3,2},{4,5},{5,4},{6,7},{7,6},{8,9},{9,8},{10,11... | collective-permute-start | bytes 1572872 | tf_op jit(solution)/shard_map/ppermute | solution.py:346

commit v4 on v3

--- a/solution.py
+++ b/solution.py
@@ -47,20 +47,6 @@
     up, down = shifts_of(lax.axis_size(SLAB))
     last, first = edges(shard, 0)
     return jnp.concatenate([lax.ppermute(last, SLAB, up), shard, lax.ppermute(first, SLAB, down)], axis=0)
-
-
-def divergence(field):
-    base = field[:-1, :-1, :-1]
-    step_z = field[1:, :-1, :-1] - base
-    step_y = field[:-1, 1:, :-1] - base
-    step_x = field[:-1, :-1, 1:] - base
-    scale = jnp.sqrt(step_z * step_z + step_y * step_y + step_x * step_x + smooth_floor)
-    flow_z = step_z / scale
-    flow_y = step_y / scale
-    flow_x = step_x / scale
-    result = flow_z[1:, 1:, 1:] - flow_z[:-1, 1:, 1:]
-    result = result + flow_y[1:, 1:, 1:] - flow_y[1:, :-1, 1:]
-    return result + flow_x[1:, 1:, 1:] - flow_x[1:, 1:, :-1]
 
 
 PAD = 4
@@ -206,11 +192,40 @@
     fill_zeros(windows, blocks, views.shape[2])
 
 
-def load_spread_kernel(place, offsets, counts, views, tiles_hbm, out, tiles, windows, sems):
+def next_x(block):
+    width = block.shape[1]
+    lane = lax.broadcasted_iota(jnp.int32, block.shape, 1)
+    return jnp.where(lane == width - 1, 0.0, pltpu.roll(block, width - 1, 1))
+
+
+def smooth(field, row):
+    wide = lambda i, j: field[i, j].astype(jnp.float32)
+
+    def flow(i, j):
+        base = wide(i, j)
+        steps = (wide(i + 1, j) - base, wide(i, j + 1) - base, next_x(base) - base)
+        inverse = lax.rsqrt(sum(step * step for step in steps) + smooth_floor)
+        return [step * inverse for step in steps]
+
+    here = wide(1, row + 1)
+    flow_z, flow_y, flow_x = flow(1, row + 1)
+    lane = lax.broadcasted_iota(jnp.int32, here.shape, 1)
+    edge = here * lax.rsqrt(here * here + smooth_floor)
+    before_x = jnp.where(lane == 0, edge, pltpu.roll(flow_x, 1, 1))
+    div = flow_z - flow(0, row + 1)[0] + flow_y - flow(1, row)[1] + flow_x - before_x
+    return here + step_size * smooth_weight * div
+
+
+def load_spread_kernel(place, offsets, counts, views, field, tiles_hbm, out, tiles, base, windows, sems):
     copies = tile_copies(tiles_hbm, tiles, sems, place[0])
     for copy in copies[: ZHI * YS]:
         copy.start()
     fill_views(windows, views)
+    depth, lanes = field.shape[2], base.shape[2]
+    for r in range(base.shape[0]):
+        line = smooth(field, r)
+        for t in range(line.shape[1] // lanes):
+            base[r, t * depth : (t + 1) * depth, :] = line[:, t * lanes : (t + 1) * lanes]
     for first in range(0, ZHI * YS, GROUP):
         wait_group(copies, first)
         spread_group(first, place[0], place[1], offsets, counts, windows, tiles, None, out)
@@ -226,8 +241,8 @@
     lanes = total.shape[2]
     for r in range(rows):
         for t in range(width // lanes):
-            here = slice(t * lanes, (t + 1) * lanes)
-            out[:, r, here] = base[:, r, here] - step_size * total[r, t * depth : (t + 1) * depth, :]
+            some = slice(t * depth, (t + 1) * depth)
+            out[:, r, t * lanes : (t + 1) * lanes] = base[r, some, :] - step_size * total[r, some, :]
 
 
 ANY = pl.BlockSpec(memory_space=pl.ANY)
@@ -287,15 +302,17 @@
     )(place, offsets, counts, windows, tiles)
 
 
-def load_spread(place, offsets, counts, views, tiles):
+def load_spread(place, offsets, counts, views, field, tiles):
     count, lanes = views.shape[2:]
+    lines = (tiles.shape[1], count, lanes)
     return pl.pallas_call(
         load_spread_kernel,
-        in_specs=[SMEM, SMEM, SMEM, VMEM, ANY],
-        out_specs=[VMEM, VMEM],
+        in_specs=[SMEM, SMEM, SMEM, VMEM, VMEM, ANY],
+        out_specs=[VMEM, VMEM, VMEM],
         out_shape=[
-            pltpu.VMEM((tiles.shape[1], count, lanes), jnp.float32),
+            pltpu.VMEM(lines, jnp.float32),
             pltpu.VMEM(tiles.shape, tiles.dtype),
+            pltpu.VMEM(lines, jnp.float32),
         ],
         scratch_shapes=[
             pltpu.VMEM((window_rows(ZHI * YS, count), lanes), jnp.bfloat16),
@@ -304,16 +321,16 @@
         compiler_params=params(),
         cost_estimate=cost(tiles, 2),
         name="load_spread",
-    )(place, offsets, counts, views, in_hbm(tiles))
-
-
-def spread(place, offsets, counts, views, tiles, begin, base):
+    )(place, offsets, counts, views, field, in_hbm(tiles))
+
+
+def spread(place, offsets, counts, views, tiles, begin, base, shape):
     count, lanes = views.shape[2:]
     return pl.pallas_call(
         spread_kernel,
         in_specs=[SMEM, SMEM, SMEM] + [VMEM] * 4,
         out_specs=VMEM,
-        out_shape=jax.ShapeDtypeStruct(base.shape, base.dtype),
+        out_shape=jax.ShapeDtypeStruct(shape, base.dtype),
         scratch_shapes=[
             pltpu.VMEM(begin.shape, begin.dtype),
             pltpu.VMEM((window_rows(ZHI * YS, count), lanes), jnp.bfloat16),
@@ -367,7 +384,10 @@
     arrived = swap(away, "core")
     kept = project(place, offsets, counts, windows, tiles, away, PAIR_SCALE)
     pair = (kept + arrived).astype(f16)
+    pair, late_volume = lax.optimization_barrier((pair, volume))
     parts = lax.all_to_all(pair, "y", 0, 0, tiled=True)
+    with_rows = with_row_neighbours(late_volume, ends_plane, begins_plane)
+    parts, with_rows = lax.optimization_barrier((parts, with_rows))
     plane = jnp.sum(parts.astype(f32), axis=0) * (1 / PAIR_SCALE)
     seen = measured.reshape(depth, tile_count, tile).transpose(1, 0, 2).reshape(count, tile)
     plane = plane - jnp.where(is_mine, seen[None], 0.0)
@@ -375,14 +395,14 @@
     both = plane + far.astype(f32) * (1 / PLANE_SCALE)
     residual = own_view(place, both, measured)
     copies = jnp.broadcast_to(both.astype(bf16)[None], (YS,) + both.shape)
-    with_rows = with_row_neighbours(volume, ends_plane, begins_plane)
     views = lax.all_to_all(copies, "y", 0, 0, tiled=True)
-    field = jnp.pad(with_slab_neighbours(with_rows).astype(f32), ((0, 0), (0, 0), (1, 1)))
-    base = volume.astype(f32) + step_size * smooth_weight * divergence(field)
-    views, base, residual = lax.optimization_barrier((views, base, residual))
+    beside = with_slab_neighbours(with_rows)
+    field = jnp.stack([lax.slice_in_dim(beside, i, i + depth, axis=0) for i in range(3)])
+    field = field.transpose(0, 2, 1, 3)
+    views, residual, field = lax.optimization_barrier((views, residual, field))
     views_other = swap(views, "core")
-    gradient, tiles = load_spread(place, offsets, counts, views, ray_tiles)
-    updated = spread(place, offsets, counts, views_other, tiles, gradient, base)
+    gradient, tiles, base = load_spread(place, offsets, counts, views, field, ray_tiles)
+    updated = spread(place, offsets, counts, views_other, tiles, gradient, base, volume.shape)
     return (updated, residual)
 
 

time: 96.9 us -> 86.7 us (0.89)
  waiting for transfers between devices: 34.6 us -> 24.1 us
  starting transfers between devices: 41.5 us -> 43.6 us
  other arithmetic: 3.62 us -> 1.59 us
    all_to_all x1, waiting for transfers between devices: 13.5 us -> 6.21 us  [per_device(): views = lax.all_to_all(copies, 'y', 0, 0, tiled=True)]
    all_to_all x1, waiting for transfers between devices: 11 us -> 3.78 us  [per_device(): parts = lax.all_to_all(pair, 'y', 0, 0, tiled=True)]
    ppermute x3, starting transfers between devices: 19 us -> 25.9 us  [swap(): return lax.ppermute(array, axis, [(0, 1), (1, 0)])]
    ppermute x3, waiting for transfers between devices: 9.08 us -> 2.74 us  [swap(): return lax.ppermute(array, axis, [(0, 1), (1, 0)])]
    all_to_all x1, starting transfers between devices: 8.75 us -> 3.49 us  [per_device(): parts = lax.all_to_all(pair, 'y', 0, 0, tiled=True)]
    ppermute x1, waiting for transfers between devices: 0.01 us -> 4.1 us  [with_row_neighbours(): lax.ppermute(last, ANGLE, up)]
    ppermute x1, waiting for transfers between devices: 0.01 us -> 3.82 us  [with_slab_neighbours(): lax.ppermute(first, SLAB, down)]
    ppermute x1, waiting for transfers between devices: 0.01 us -> 3.48 us  [with_row_neighbours(): lax.ppermute(first, ANGLE, down)]
  transfers between devices with their start and end apart: 10 -> 10, of which waited for: 4 -> 7; matrix products, arithmetic and copies ran while one was open for 3% -> 1% of each run, Pallas kernels for 8% -> 9%
where the time goes in v4:
time: 86.7 us; the launch traced here: 86.2 us
  starting transfers between devices  43.6 us (50%)
  waiting for transfers between devices  24.1 us (28%)
  Pallas kernels  14.9 us (17%)
  other arithmetic  1.59 us (2%)
  local copies, waits for them, and re-layouts  1.07 us (1%)
    ppermute x3, starting transfers between devices, swap(): return lax.ppermute(array, axis, [(0, 1), (1, 0)])  25.9 us
    all_to_all x1, waiting for transfers between devices, per_device(): views = lax.all_to_all(copies, 'y', 0, 0, tiled=True)  6.21 us
    pallas_call x1, Pallas kernels, load_spread(): pl.pallas_call(load_spread_kernel, in_specs=[SMEM, SMEM, SMEM, VMEM, VMEM...  4.61 us
    pallas_call x1, Pallas kernels, load_project(): pl.pallas_call(partial(load_project_kernel, scale=scale), in_specs=[SMEM,...  4.5 us
    ppermute x1, waiting for transfers between devices, with_row_neighbours(): lax.ppermute(last, ANGLE, up)  4.1 us
    ppermute x1, waiting for transfers between devices, with_slab_neighbours(): lax.ppermute(first, SLAB, down)  3.82 us
    ppermute x1, starting transfers between devices, with_row_neighbours(): lax.ppermute(last, ANGLE, up)  3.79 us
    all_to_all x1, waiting for transfers between devices, per_device(): parts = lax.all_to_all(pair, 'y', 0, 0, tiled=True)  3.78 us
  transfers between devices with their start and end apart: 10, of which 7 were waited for; matrix products, arithmetic and copies ran while one was open for 1% of the time, Pallas kernels for 9%

profile of v4, /device:TPU:1, one launch (start us, length us, event | category | flops | bytes accessed | tf_op | source)
XLA Modules:
  0.0 86.2 jit_solution(17255387342150225258)
XLA Ops:
  0.7 0.1 pad_add_fusion.place
  0.7 4.5 %load_project.1 = (f32[8,2,128,128]{3,2,1,0:T(8,128)S(1)}, bf16[32,4,2,128,128]{4,3,2,1,0:T(8,128)(2,1)S(1)}, bf16[1664,128]{1,0:T(8,128)(2,1)S(1)}, s32[32,128]{1,0:T(8,128)S(4)}, s32[32,128]{1,0:T(8,128)S(4)}) custom-call(s32[3]{0:T(128)S(1)} %pad_add_fusion.place, s32[32,128]{1,0:T(8,128)} %offsets_hbm.1, s32[32,128]{1,0:T(8,128)} %counts_hbm.1, ...), custom_call_target="tpu_custom_call" | custom-call | flops 536870912 | bytes 4194304 | tf_op jit(solution)/shard_map/load_project/pallas_call | solution.py:271
  5.3 0.0 copy-start
  5.3 0.0 copy-start.1
  5.3 12.6 %collective-permute-start = (f32[8,2,128,128]{3,2,1,0:T(8,128)S(1)}, f32[8,2,128,128]{3,2,1,0:T(8,128)S(1)}, u32[]{:S(2)}, u32[]{:S(2)}) collective-permute-start(f32[8,2,128,128]{3,2,1,0:T(8,128)S(1)} %get-tuple-element.26), channel_id=1, source_target_pairs={{0,1},{1,0},{2,3},{3,2},{4,5},{5,4},{6,7},{7,6},{8,9},{9,8},{10,11... | collective-permute-start | bytes 3145736 | tf_op jit(solution)/shard_map/ppermute | solution.py:363
  17.8 1.9 %project.1 = f32[8,2,128,128]{3,2,1,0:T(8,128)S(1)} custom-call(s32[3]{0:T(128)S(1)} %pad_add_fusion.place, s32[32,128]{1,0:T(8,128)S(4)} %get-tuple-element.22.offsets, s32[32,128]{1,0:T(8,128)S(4)} %get-tuple-element.23.counts, bf16[1664,128]{1,0:T(8,128)(2,1)S(1)} %get-tuple-element.24.windows, bf16[32,4,2,128,128]{4,3,2,1,0:T(8,128)(2,1)S(1)} %get-tuple-element.25.tiles), custom_call_target="tpu_custom_call" | custom-call | flops 536870912 | bytes 4194304 | tf_op jit(solution)/shard_map/project/pallas_call | solution.py:294
  19.8 0.4 collective-permute-done
  20.1 0.9 %add_convert_fusion = f16[8,2,128,128]{3,2,1,0:T(8,128)(2,1)} fusion(f32[8,2,128,128]{3,2,1,0:T(8,128)S(1)} %project.1, f32[8,2,128,128]{3,2,1,0:T(8,128)S(1)} %collective-permute-done), kind=kLoop, calls=%fused_computation.1 | loop fusion | flops 524288 | bytes 2621440 | tf_op jit(solution)/shard_map/convert_element_type | solution.py:386
  21.1 3.5 %all-to-all-start = ((f16[8,2,128,128]{3,2,1,0:T(8,128)(2,1)}), f16[8,2,128,128]{3,2,1,0:T(8,128)(2,1)S(1)}, u32[]{:S(2)}, u32[]{:S(2)}) async-start(f16[8,2,128,128]{3,2,1,0:T(8,128)(2,1)} %add_convert_fusion), calls=%async_computation | async-start | bytes 1048576 | tf_op jit(solution)/shard_map/all_to_all | solution.py:388
  24.6 0.0 copy-done
  24.6 0.1 copy.7
  24.7 3.8 %collective-permute-start.2 = (bf16[8,1,2048]{2,0,1:T(8,128)(2,1)S(1)}, bf16[8,1,2048]{2,0,1:T(8,128)(2,1)S(1)}, u32[]{:S(2)}, u32[]{:S(2)}) collective-permute-start(bf16[8,1,2048]{2,0,1:T(8,128)(2,1)S(1)} %get-tuple-element.46), channel_id=1, source_target_pairs={{0,1},{1,2},{2,3},{3,4},{4,5},{5,6},{6,7},{7,8},{8,9},{9,10},{10,1... | collective-permute-start | bytes 98312 | tf_op jit(solution)/shard_map/ppermute | solution.py:39
  28.5 0.7 collective-permute-start.1
  29.1 1.9 %collective-permute-start.3 = (bf16[8,1,2048]{2,0,1:T(8,128)(2,1)S(1)}, bf16[8,1,2048]{2,0,1:T(8,128)(2,1)S(1)}, u32[]{:S(2)}, u32[]{:S(2)}) collective-permute-start(bf16[8,1,2048]{2,0,1:T(8,128)(2,1)S(1)} %get-tuple-element.48), channel_id=1, source_target_pairs={{1,0},{2,1},{3,2},{4,3},{5,4},{6,5},{7,6},{8,7},{9,8},{10,9},{11,1... | collective-permute-start | bytes 98312 | tf_op jit(solution)/shard_map/ppermute | solution.py:39
  31.1 4.1 %collective-permute-done.2 = bf16[8,1,2048]{2,0,1:T(8,128)(2,1)S(1)} collective-permute-done((bf16[8,1,2048]{2,0,1:T(8,128)(2,1)S(1)}, bf16[8,1,2048]{2,0,1:T(8,128)(2,1)S(1)}, u32[]{:S(2)}, u32[]{:S(2)}) %collective-permute-start.2) | collective-permute-done | bytes 32800 | tf_op jit(solution)/shard_map/ppermute | solution.py:39
  35.2 0.0 collective-permute-done.1
  35.2 3.5 %collective-permute-done.3 = bf16[8,1,2048]{2,0,1:T(8,128)(2,1)S(1)} collective-permute-done((bf16[8,1,2048]{2,0,1:T(8,128)(2,1)S(1)}, bf16[8,1,2048]{2,0,1:T(8,128)(2,1)S(1)}, u32[]{:S(2)}, u32[]{:S(2)}) %collective-permute-start.3) | collective-permute-done | bytes 32800 | tf_op jit(solution)/shard_map/ppermute | solution.py:39
  38.7 3.8 %all-to-all-done = f16[8,2,128,128]{3,2,1,0:T(8,128)(2,1)S(1)} async-done(((f16[8,2,128,128]{3,2,1,0:T(8,128)(2,1)}), f16[8,2,128,128]{3,2,1,0:T(8,128)(2,1)S(1)}, u32[]{:S(2)}, u32[]{:S(2)}) %all-to-all-start) | async-done | bytes 524320 | tf_op jit(solution)/shard_map/all_to_all | solution.py:388
  42.5 0.1 convert_reduce_fusion
  42.6 0.0 copy-done.1
  42.6 0.1 multiply_convert_fusion
  42.7 9.0 %collective-permute-start.4 = (f16[2,128,128]{2,1,0:T(8,128)(2,1)S(1)}, f16[2,128,128]{2,1,0:T(8,128)(2,1)S(1)}, u32[]{:S(2)}, u32[]{:S(2)}) collective-permute-start(f16[2,128,128]{2,1,0:T(8,128)(2,1)S(1)} %multiply_convert_fusion), channel_id=1, source_target_pairs={{0,16},{16,0},{1,17},{17,1},{2,18},{18,2},{3,19},{19,3},{4,20},{20... | collective-permute-start | bytes 196616 | tf_op jit(solution)/shard_map/ppermute | solution.py:363
  51.7 2.4 %collective-permute-done.4 = f16[2,128,128]{2,1,0:T(8,128)(2,1)S(1)} collective-permute-done((f16[2,128,128]{2,1,0:T(8,128)(2,1)S(1)}, f16[2,128,128]{2,1,0:T(8,128)(2,1)S(1)}, u32[]{:S(2)}, u32[]{:S(2)}) %collective-permute-start.4) | collective-permute-done | bytes 65568 | tf_op jit(solution)/shard_map/ppermute | solution.py:363
  54.1 0.1 fusion.2
  54.2 0.9 %broadcast_in_dim.35 = bf16[8,2,128,128]{3,2,1,0:T(8,128)(2,1)} broadcast(bf16[2,128,128]{2,1,0:T(8,128)(2,1)S(1)} %get-tuple-element.40), dimensions={1,2,3} | broadcast | bytes 589824 | tf_op jit(solution)/shard_map/broadcast_in_dim | solution.py:397
  55.1 3.5 %all-to-all-start.1 = ((bf16[8,2,128,128]{3,2,1,0:T(8,128)(2,1)}), bf16[8,2,128,128]{3,2,1,0:T(8,128)(2,1)S(1)}, u32[]{:S(2)}, u32[]{:S(2)}) async-start(bf16[8,2,128,128]{3,2,1,0:T(8,128)(2,1)} %broadcast_in_dim.35), calls=%async_computation.1 | async-start | bytes 1048576 | tf_op jit(solution)/shard_map/all_to_all | solution.py:398
  58.6 0.1 fusion.3
  58.7 3.1 %collective-permute-start.5 = (bf16[1,6,2048]{2,0,1:T(2,128)(2,1)S(1)}, bf16[1,6,2048]{2,0,1:T(2,128)(2,1)S(1)}, u32[]{:S(2)}, u32[]{:S(2)}) collective-permute-start(bf16[1,6,2048]{2,0,1:T(2,128)(2,1)S(1)} %get-tuple-element.44), channel_id=1, source_target_pairs={{0,32},{32,64},{64,96},{96,128},{128,160},{160,192},{192,224},{224... | collective-permute-start | bytes 73736 | tf_op jit(solution)/shard_map/ppermute | solution.py:49
  61.8 1.3 %collective-permute-start.6 = (bf16[1,6,2048]{2,0,1:T(2,128)(2,1)S(1)}, bf16[1,6,2048]{2,0,1:T(2,128)(2,1)S(1)}, u32[]{:S(2)}, u32[]{:S(2)}) collective-permute-start(bf16[1,6,2048]{2,0,1:T(2,128)(2,1)S(1)} %get-tuple-element.45), channel_id=1, source_target_pairs={{32,0},{64,32},{96,64},{128,96},{160,128},{192,160},{224,192},{256... | collective-permute-start | bytes 73736 | tf_op jit(solution)/shard_map/ppermute | solution.py:49
  63.1 0.0 collective-permute-done.5
  63.1 3.8 %collective-permute-done.6 = bf16[1,6,2048]{2,0,1:T(2,128)(2,1)S(1)} collective-permute-done((bf16[1,6,2048]{2,0,1:T(2,128)(2,1)S(1)}, bf16[1,6,2048]{2,0,1:T(2,128)(2,1)S(1)}, u32[]{:S(2)}, u32[]{:S(2)}) %collective-permute-start.6) | collective-permute-done | bytes 24608 | tf_op jit(solution)/shard_map/ppermute | solution.py:49
  66.9 0.2 fusion.1
  67.1 0.1 maximum_bitcast_fusion.field
  67.2 1.2 %own_view.1 = f32[1,8,2048]{2,1,0:T(8,128)} custom-call(s32[3]{0:T(128)S(1)} %pad_add_fusion.place, f32[2,128,128]{2,1,0:T(8,128)S(1)} %get-tuple-element.41.both), custom_call_target="tpu_custom_call" | custom-call | bytes 131072 | tf_op jit(solution)/shard_map/own_view/pallas_call | solution.py:351
  68.3 6.2 %all-to-all-done.1.views = bf16[8,2,128,128]{3,2,1,0:T(8,128)(2,1)S(1)} async-done(((bf16[8,2,128,128]{3,2,1,0:T(8,128)(2,1)}), bf16[8,2,128,128]{3,2,1,0:T(8,128)(2,1)S(1)}, u32[]{:S(2)}, u32[]{:S(2)}) %all-to-all-start.1) | async-done | bytes 524320 | tf_op jit(solution)/shard_map/all_to_all | solution.py:398
  74.5 4.3 %collective-permute-start.7 = (bf16[8,2,128,128]{3,2,1,0:T(8,128)(2,1)S(1)}, bf16[8,2,128,128]{3,2,1,0:T(8,128)(2,1)S(1)}, u32[]{:S(2)}, u32[]{:S(2)}) collective-permute-start(bf16[8,2,128,128]{3,2,1,0:T(8,128)(2,1)S(1)} %all-to-all-done.1.views), channel_id=1, source_target_pairs={{0,1},{1,0},{2,3},{3,2},{4,5},{5,4},{6,7},{7,6},{8,9},{9,8},{10,11... | collective-permute-start | bytes 1572872 | tf_op jit(solution)/shard_map/ppermute | solution.py:363
  78.9 4.6 %load_spread.1 = (f32[4,128,128]{2,1,0:T(8,128)S(1)}, bf16[32,4,2,128,128]{4,3,2,1,0:T(8,128)(2,1)S(1)}, f32[4,128,128]{2,1,0:T(8,128)S(1)}) custom-call(s32[3]{0:T(128)S(1)} %pad_add_fusion.place, s32[32,128]{1,0:T(8,128)S(4)} %get-tuple-element.22.offsets, s32[32,128]{1,0:T(8,128)S(4)} %get-tuple-element.23.counts, ...), custom_call_target="tpu_custom_call" | custom-call | flops 536870912 | bytes 4194304 | tf_op jit(solution)/shard_map/load_spread/pallas_call | solution.py:308
  83.5 0.0 collective-permute-done.7.views
  83.5 2.8 %spread.1 = f32[8,4,2048]{2,1,0:T(4,128)} custom-call(s32[3]{0:T(128)S(1)} %pad_add_fusion.place, s32[32,128]{1,0:T(8,128)S(4)} %get-tuple-element.22.offsets, s32[32,128]{1,0:T(8,128)S(4)} %get-tuple-element.23.counts, bf16[8,2,128,128]{3,2,1,0:T(8,128)(2,1)S(1)} %collective-permute-done.7.views, bf16[32,4,2,128,128]{4,3,2,1,0:T(8,128)(2,1)S(1)} %get-tuple-element.36.tiles, ...), custom_call_target="tpu_custom_call" | custom-call | flops 536870912 | bytes 4194304 | tf_op jit(solution)/shard_map/spread/pallas_call | solution.py:329
  (4 shorter events, 0.1 us)
Async XLA Ops:
  5.3 19.3 %copy-start = (bf16[8,4,2048]{2,1,0:T(4,128)(2,1)S(1)}, bf16[8,4,2048]{2,1,0:T(4,128)(2,1)}, u32[]{:S(2)}) copy-start(bf16[8,4,2048]{2,1,0:T(4,128)(2,1)} %volume_hbm.1) | copy-start | bytes 393220
  5.3 37.3 %copy-start.1 = (f32[1,8,2048]{2,1,0:T(8,128)S(1)}, f32[1,8,2048]{2,1,0:T(8,128)}, u32[]{:S(2)}) copy-start(f32[1,8,2048]{2,1,0:T(8,128)} %param.6) | copy-start | bytes 196612
  5.3 14.8 %collective-permute-start = (f32[8,2,128,128]{3,2,1,0:T(8,128)S(1)}, f32[8,2,128,128]{3,2,1,0:T(8,128)S(1)}, u32[]{:S(2)}, u32[]{:S(2)}) collective-permute-start(f32[8,2,128,128]{3,2,1,0:T(8,128)S(1)} %get-tuple-element.26), channel_id=1, source_target_pairs={{0,1},{1,0},{2,3},{3,2},{4,5},{5,4},{6,7},{7,6},{8,9},{9,8},{10,11... | collective-permute-start | bytes 3145736 | tf_op jit(solution)/shard_map/ppermute | solution.py:363
  21.1 21.4 %all-to-all-start = ((f16[8,2,128,128]{3,2,1,0:T(8,128)(2,1)}), f16[8,2,128,128]{3,2,1,0:T(8,128)(2,1)S(1)}, u32[]{:S(2)}, u32[]{:S(2)}) async-start(f16[8,2,128,128]{3,2,1,0:T(8,128)(2,1)} %add_convert_fusion), calls=%async_computation | async-start | bytes 1048576 | tf_op jit(solution)/shard_map/all_to_all | solution.py:388
  24.7 10.5 %collective-permute-start.2 = (bf16[8,1,2048]{2,0,1:T(8,128)(2,1)S(1)}, bf16[8,1,2048]{2,0,1:T(8,128)(2,1)S(1)}, u32[]{:S(2)}, u32[]{:S(2)}) collective-permute-start(bf16[8,1,2048]{2,0,1:T(8,128)(2,1)S(1)} %get-tuple-element.46), channel_id=1, source_target_pairs={{0,1},{1,2},{2,3},{3,4},{4,5},{5,6},{6,7},{7,8},{8,9},{9,10},{10,1... | collective-permute-start | bytes 98312 | tf_op jit(solution)/shard_map/ppermute | solution.py:39
  28.5 6.7 %collective-permute-start.1 = (bf16[8,1,2048]{2,0,1:T(8,128)(2,1)S(1)}, bf16[8,1,2048]{2,0,1:T(8,128)(2,1)S(1)}, u32[]{:S(2)}, u32[]{:S(2)}) collective-permute-start(bf16[8,1,2048]{2,0,1:T(8,128)(2,1)S(1)} %get-tuple-element.47), channel_id=1, source_target_pairs={{15,16},{16,15},{47,48},{48,47},{79,80},{80,79},{111,112},{112,111... | collective-permute-start | bytes 98312 | tf_op jit(solution)/shard_map/ppermute | solution.py:40
  29.1 9.5 %collective-permute-start.3 = (bf16[8,1,2048]{2,0,1:T(8,128)(2,1)S(1)}, bf16[8,1,2048]{2,0,1:T(8,128)(2,1)S(1)}, u32[]{:S(2)}, u32[]{:S(2)}) collective-permute-start(bf16[8,1,2048]{2,0,1:T(8,128)(2,1)S(1)} %get-tuple-element.48), channel_id=1, source_target_pairs={{1,0},{2,1},{3,2},{4,3},{5,4},{6,5},{7,6},{8,7},{9,8},{10,9},{11,1... | collective-permute-start | bytes 98312 | tf_op jit(solution)/shard_map/ppermute | solution.py:39
  42.7 11.4 %collective-permute-start.4 = (f16[2,128,128]{2,1,0:T(8,128)(2,1)S(1)}, f16[2,128,128]{2,1,0:T(8,128)(2,1)S(1)}, u32[]{:S(2)}, u32[]{:S(2)}) collective-permute-start(f16[2,128,128]{2,1,0:T(8,128)(2,1)S(1)} %multiply_convert_fusion), channel_id=1, source_target_pairs={{0,16},{16,0},{1,17},{17,1},{2,18},{18,2},{3,19},{19,3},{4,20},{20... | collective-permute-start | bytes 196616 | tf_op jit(solution)/shard_map/ppermute | solution.py:363
  55.1 19.5 %all-to-all-start.1 = ((bf16[8,2,128,128]{3,2,1,0:T(8,128)(2,1)}), bf16[8,2,128,128]{3,2,1,0:T(8,128)(2,1)S(1)}, u32[]{:S(2)}, u32[]{:S(2)}) async-start(bf16[8,2,128,128]{3,2,1,0:T(8,128)(2,1)} %broadcast_in_dim.35), calls=%async_computation.1 | async-start | bytes 1048576 | tf_op jit(solution)/shard_map/all_to_all | solution.py:398
  58.7 4.4 %collective-permute-start.5 = (bf16[1,6,2048]{2,0,1:T(2,128)(2,1)S(1)}, bf16[1,6,2048]{2,0,1:T(2,128)(2,1)S(1)}, u32[]{:S(2)}, u32[]{:S(2)}) collective-permute-start(bf16[1,6,2048]{2,0,1:T(2,128)(2,1)S(1)} %get-tuple-element.44), channel_id=1, source_target_pairs={{0,32},{32,64},{64,96},{96,128},{128,160},{160,192},{192,224},{224... | collective-permute-start | bytes 73736 | tf_op jit(solution)/shard_map/ppermute | solution.py:49
  61.8 5.1 %collective-permute-start.6 = (bf16[1,6,2048]{2,0,1:T(2,128)(2,1)S(1)}, bf16[1,6,2048]{2,0,1:T(2,128)(2,1)S(1)}, u32[]{:S(2)}, u32[]{:S(2)}) collective-permute-start(bf16[1,6,2048]{2,0,1:T(2,128)(2,1)S(1)} %get-tuple-element.45), channel_id=1, source_target_pairs={{32,0},{64,32},{96,64},{128,96},{160,128},{192,160},{224,192},{256... | collective-permute-start | bytes 73736 | tf_op jit(solution)/shard_map/ppermute | solution.py:49
  74.5 8.9 %collective-permute-start.7 = (bf16[8,2,128,128]{3,2,1,0:T(8,128)(2,1)S(1)}, bf16[8,2,128,128]{3,2,1,0:T(8,128)(2,1)S(1)}, u32[]{:S(2)}, u32[]{:S(2)}) collective-permute-start(bf16[8,2,128,128]{3,2,1,0:T(8,128)(2,1)S(1)} %all-to-all-done.1.views), channel_id=1, source_target_pairs={{0,1},{1,0},{2,3},{3,2},{4,5},{5,4},{6,7},{7,6},{8,9},{9,8},{10,11... | collective-permute-start | bytes 1572872 | tf_op jit(solution)/shard_map/ppermute | solution.py:363

commit v5 on v4

--- a/solution.py
+++ b/solution.py
@@ -51,6 +51,8 @@
 
 PAD = 4
 GROUP = 4
+BLOCKS = ZHI * YS
+EARLY = 12
 
 
 def copy_rows(count):
@@ -145,9 +147,15 @@
 
 
 def tile_copies(tiles_hbm, tiles, sems, first_core):
-    blocks = ZHI * YS
-    order = [angle_of(j, first_core) for j in range(blocks)] + [angle_of(j, 1 - first_core) for j in range(blocks)]
+    order = [angle_of(j, first_core) for j in range(BLOCKS)] + [angle_of(j, 1 - first_core) for j in range(BLOCKS)]
     return [pltpu.make_async_copy(tiles_hbm.at[a], tiles.at[a], sems.at[i]) for i, a in enumerate(order)]
+
+
+def block_copies(tiles_hbm, tiles, sems, core, blocks, place=0):
+    return [
+        pltpu.make_async_copy(tiles_hbm.at[angle_of(j, core)], tiles.at[place + i], sems.at[place + i])
+        for i, j in enumerate(blocks)
+    ]
 
 
 def wait_group(copies, first):
@@ -160,7 +168,7 @@
 
 
 def spread_group(first, core, first_row, offsets, counts, windows, tiles, begin, out):
-    blocks, rows = ZHI * YS, tiles.shape[1]
+    blocks, rows = BLOCKS, tiles.shape[1]
     count = out.shape[1]
     for r in range(rows):
         row = first_row + r
@@ -170,7 +178,7 @@
             starts = band_windows(offsets[angle, row], counts[angle, row], -1, j, blocks, count)
             for k, start in enumerate(starts):
                 lhs.append(windows[pl.ds(start, count), :])
-                rhs.append(tiles[angle, r, k])
+                rhs.append(tiles[j - first, r, k])
         part = lax.dot_general(
             jnp.concatenate(lhs, 1),
             jnp.concatenate(rhs, 1),
@@ -216,27 +224,27 @@
     return here + step_size * smooth_weight * div
 
 
-def load_spread_kernel(place, offsets, counts, views, field, tiles_hbm, out, tiles, base, windows, sems):
-    copies = tile_copies(tiles_hbm, tiles, sems, place[0])
-    for copy in copies[: ZHI * YS]:
+def load_spread_kernel(place, offsets, counts, views, early, tiles_hbm, out, later, windows, tiles, sems, later_sems):
+    now = block_copies(tiles_hbm, tiles, sems, place[0], range(EARLY, BLOCKS))
+    then = block_copies(tiles_hbm, later, later_sems, 1 - place[0], range(BLOCKS))
+    for copy in now + then:
         copy.start()
     fill_views(windows, views)
-    depth, lanes = field.shape[2], base.shape[2]
-    for r in range(base.shape[0]):
-        line = smooth(field, r)
-        for t in range(line.shape[1] // lanes):
-            base[r, t * depth : (t + 1) * depth, :] = line[:, t * lanes : (t + 1) * lanes]
-    for first in range(0, ZHI * YS, GROUP):
-        wait_group(copies, first)
-        spread_group(first, place[0], place[1], offsets, counts, windows, tiles, None, out)
-    for copy in copies[ZHI * YS :]:
+    for first in range(0, BLOCKS, GROUP):
+        if first == EARLY:
+            for copy in now:
+                copy.wait()
+        group = early.at[pl.ds(first, GROUP)] if first < EARLY else tiles.at[pl.ds(first - EARLY, GROUP)]
+        spread_group(first, place[0], place[1], offsets, counts, windows, group, None, out)
+    for copy in then:
         copy.wait()
 
 
 def spread_kernel(place, offsets, counts, views, tiles, begin, base, out, total, windows):
     fill_views(windows, views)
-    for first in range(0, ZHI * YS, GROUP):
-        spread_group(first, 1 - place[0], place[1], offsets, counts, windows, tiles, begin, total)
+    for first in range(0, BLOCKS, GROUP):
+        group = tiles.at[pl.ds(first, GROUP)]
+        spread_group(first, 1 - place[0], place[1], offsets, counts, windows, group, begin, total)
     depth, rows, width = out.shape
     lanes = total.shape[2]
     for r in range(rows):
@@ -302,26 +310,27 @@
     )(place, offsets, counts, windows, tiles)
 
 
-def load_spread(place, offsets, counts, views, field, tiles):
+def load_spread(place, offsets, counts, views, early, tiles):
     count, lanes = views.shape[2:]
     lines = (tiles.shape[1], count, lanes)
     return pl.pallas_call(
         load_spread_kernel,
         in_specs=[SMEM, SMEM, SMEM, VMEM, VMEM, ANY],
-        out_specs=[VMEM, VMEM, VMEM],
+        out_specs=[VMEM, VMEM],
         out_shape=[
             pltpu.VMEM(lines, jnp.float32),
-            pltpu.VMEM(tiles.shape, tiles.dtype),
-            pltpu.VMEM(lines, jnp.float32),
+            pltpu.VMEM((BLOCKS,) + tiles.shape[1:], tiles.dtype),
         ],
         scratch_shapes=[
             pltpu.VMEM((window_rows(ZHI * YS, count), lanes), jnp.bfloat16),
-            pltpu.SemaphoreType.DMA((tiles.shape[0],)),
+            pltpu.VMEM((BLOCKS - EARLY,) + tiles.shape[1:], tiles.dtype),
+            pltpu.SemaphoreType.DMA((BLOCKS - EARLY,)),
+            pltpu.SemaphoreType.DMA((BLOCKS,)),
         ],
         compiler_params=params(),
         cost_estimate=cost(tiles, 2),
         name="load_spread",
-    )(place, offsets, counts, views, field, in_hbm(tiles))
+    )(place, offsets, counts, views, early, in_hbm(tiles))
 
 
 def spread(place, offsets, counts, views, tiles, begin, base, shape):
@@ -341,22 +350,36 @@
     )(place, offsets, counts, views, tiles, begin, base)
 
 
-def own_view_kernel(place, both, out):
+def close_window_kernel(place, both, field, tiles_hbm, out, early, base, sems):
+    copies = block_copies(tiles_hbm, early, sems, place[0], range(EARLY))
+    for copy in copies:
+        copy.start()
     depth, lanes = out.shape[1], both.shape[2]
     for t in range(out.shape[2] // lanes):
         out[0, :, t * lanes : (t + 1) * lanes] = both[place[2], t * depth : (t + 1) * depth, :]
-
-
-def own_view(place, both, like):
+    for r in range(base.shape[0]):
+        line = smooth(field, r)
+        for t in range(line.shape[1] // lanes):
+            base[r, t * depth : (t + 1) * depth, :] = line[:, t * lanes : (t + 1) * lanes]
+    for copy in copies:
+        copy.wait()
+
+
+def close_window(place, both, field, tiles, like):
     return pl.pallas_call(
-        own_view_kernel,
-        in_specs=[SMEM, VMEM],
-        out_specs=VMEM,
-        out_shape=jax.ShapeDtypeStruct(like.shape, like.dtype),
+        close_window_kernel,
+        in_specs=[SMEM, VMEM, VMEM, ANY],
+        out_specs=[VMEM, VMEM, VMEM],
+        out_shape=[
+            jax.ShapeDtypeStruct(like.shape, like.dtype),
+            pltpu.VMEM((EARLY,) + tiles.shape[1:], tiles.dtype),
+            pltpu.VMEM((tiles.shape[1],) + both.shape[1:], both.dtype),
+        ],
+        scratch_shapes=[pltpu.SemaphoreType.DMA((EARLY,))],
         compiler_params=params(),
         cost_estimate=pl.CostEstimate(flops=0, bytes_accessed=8 * like.size, transcendentals=0),
-        name="own_view",
-    )(place, both)
+        name="close_window",
+    )(place, both, field, in_hbm(tiles))
 
 
 def swap(array, axis):
@@ -393,15 +416,15 @@
     plane = plane - jnp.where(is_mine, seen[None], 0.0)
     far = swap((plane * PLANE_SCALE).astype(f16), "zhi")
     both = plane + far.astype(f32) * (1 / PLANE_SCALE)
-    residual = own_view(place, both, measured)
     copies = jnp.broadcast_to(both.astype(bf16)[None], (YS,) + both.shape)
     views = lax.all_to_all(copies, "y", 0, 0, tiled=True)
     beside = with_slab_neighbours(with_rows)
     field = jnp.stack([lax.slice_in_dim(beside, i, i + depth, axis=0) for i in range(3)])
     field = field.transpose(0, 2, 1, 3)
-    views, residual, field = lax.optimization_barrier((views, residual, field))
+    residual, early, base = close_window(place, both, field, ray_tiles, measured)
+    views, residual, early, base = lax.optimization_barrier((views, residual, early, base))
     views_other = swap(views, "core")
-    gradient, tiles, base = load_spread(place, offsets, counts, views, field, ray_tiles)
+    gradient, tiles = load_spread(place, offsets, counts, views, early, ray_tiles)
     updated = spread(place, offsets, counts, views_other, tiles, gradient, base, volume.shape)
     return (updated, residual)
 

time: 86.7 us -> 87.9 us (1.014)
  Pallas kernels: 14.9 us -> 17.4 us
  waiting for transfers between devices: 24.1 us -> 22.7 us
    pallas_call x1, Pallas kernels: 1.18 us -> 3.25 us  [close_window(): pl.pallas_call(close_window_kernel, in_specs=[SMEM, VMEM, VMEM, ANY], out...]
    all_to_all x1, waiting for transfers between devices: 6.21 us -> 4.63 us  [per_device(): views = lax.all_to_all(copies, 'y', 0, 0, tiled=True)]
  transfers between devices with their start and end apart: 10 -> 10, of which waited for: 7 -> 7; matrix products, arithmetic and copies ran while one was open for 1% -> 1% of each run, Pallas kernels for 9% -> 12%
where the time goes in v5:
time: 87.9 us; the launch traced here: 87.4 us
  starting transfers between devices  43.8 us (50%)
  waiting for transfers between devices  22.7 us (26%)
  Pallas kernels  17.4 us (20%)
  other arithmetic  1.58 us (2%)
  local copies, waits for them, and re-layouts  1.06 us (1%)
    ppermute x3, starting transfers between devices, swap(): return lax.ppermute(array, axis, [(0, 1), (1, 0)])  25.9 us
    pallas_call x1, Pallas kernels, load_spread(): pl.pallas_call(load_spread_kernel, in_specs=[SMEM, SMEM, SMEM, VMEM, VMEM...  5.03 us
    all_to_all x1, waiting for transfers between devices, per_device(): views = lax.all_to_all(copies, 'y', 0, 0, tiled=True)  4.63 us
    pallas_call x1, Pallas kernels, load_project(): pl.pallas_call(partial(load_project_kernel, scale=scale), in_specs=[SMEM,...  4.5 us
    all_to_all x1, starting transfers between devices, per_device(): views = lax.all_to_all(copies, 'y', 0, 0, tiled=True)  4.15 us
    ppermute x1, waiting for transfers between devices, with_row_neighbours(): lax.ppermute(last, ANGLE, up)  4.1 us
    ppermute x1, waiting for transfers between devices, with_slab_neighbours(): lax.ppermute(first, SLAB, down)  3.92 us
    ppermute x1, starting transfers between devices, with_row_neighbours(): lax.ppermute(last, ANGLE, up)  3.79 us
  transfers between devices with their start and end apart: 10, of which 7 were waited for; matrix products, arithmetic and copies ran while one was open for 1% of the time, Pallas kernels for 12%

profile of v5, /device:TPU:1, one launch (start us, length us, event | category | flops | bytes accessed | tf_op | source)
XLA Modules:
  0.0 87.4 jit_solution(14207017563147155838)
XLA Ops:
  0.7 0.1 pad_add_fusion.place
  0.7 4.5 %load_project.1 = (f32[8,2,128,128]{3,2,1,0:T(8,128)S(1)}, bf16[32,4,2,128,128]{4,3,2,1,0:T(8,128)(2,1)S(1)}, bf16[1664,128]{1,0:T(8,128)(2,1)S(1)}, s32[32,128]{1,0:T(8,128)S(4)}, s32[32,128]{1,0:T(8,128)S(4)}) custom-call(s32[3]{0:T(128)S(1)} %pad_add_fusion.place, s32[32,128]{1,0:T(8,128)} %offsets_hbm.1, s32[32,128]{1,0:T(8,128)} %counts_hbm.1, ...), custom_call_target="tpu_custom_call" | custom-call | flops 536870912 | bytes 4194304 | tf_op jit(solution)/shard_map/load_project/pallas_call | solution.py:279
  5.3 0.0 copy-start
  5.3 0.0 copy-start.1
  5.3 12.6 %collective-permute-start = (f32[8,2,128,128]{3,2,1,0:T(8,128)S(1)}, f32[8,2,128,128]{3,2,1,0:T(8,128)S(1)}, u32[]{:S(2)}, u32[]{:S(2)}) collective-permute-start(f32[8,2,128,128]{3,2,1,0:T(8,128)S(1)} %get-tuple-element.29), channel_id=1, source_target_pairs={{0,1},{1,0},{2,3},{3,2},{4,5},{5,4},{6,7},{7,6},{8,9},{9,8},{10,11... | collective-permute-start | bytes 3145736 | tf_op jit(solution)/shard_map/ppermute | solution.py:386
  17.8 1.9 %project.1 = f32[8,2,128,128]{3,2,1,0:T(8,128)S(1)} custom-call(s32[3]{0:T(128)S(1)} %pad_add_fusion.place, s32[32,128]{1,0:T(8,128)S(4)} %get-tuple-element.25.offsets, s32[32,128]{1,0:T(8,128)S(4)} %get-tuple-element.26.counts, bf16[1664,128]{1,0:T(8,128)(2,1)S(1)} %get-tuple-element.27.windows, bf16[32,4,2,128,128]{4,3,2,1,0:T(8,128)(2,1)S(1)} %get-tuple-element.28.tiles), custom_call_target="tpu_custom_call" | custom-call | flops 536870912 | bytes 4194304 | tf_op jit(solution)/shard_map/project/pallas_call | solution.py:302
  19.8 0.3 collective-permute-done
  20.1 0.9 %add_convert_fusion = f16[8,2,128,128]{3,2,1,0:T(8,128)(2,1)} fusion(f32[8,2,128,128]{3,2,1,0:T(8,128)S(1)} %project.1, f32[8,2,128,128]{3,2,1,0:T(8,128)S(1)} %collective-permute-done), kind=kLoop, calls=%fused_computation.1 | loop fusion | flops 524288 | bytes 2621440 | tf_op jit(solution)/shard_map/convert_element_type | solution.py:409
  21.0 3.5 %all-to-all-start = ((f16[8,2,128,128]{3,2,1,0:T(8,128)(2,1)}), f16[8,2,128,128]{3,2,1,0:T(8,128)(2,1)S(1)}, u32[]{:S(2)}, u32[]{:S(2)}) async-start(f16[8,2,128,128]{3,2,1,0:T(8,128)(2,1)} %add_convert_fusion), calls=%async_computation | async-start | bytes 1048576 | tf_op jit(solution)/shard_map/all_to_all | solution.py:411
  24.5 0.0 copy-done
  24.6 0.1 copy.7
  24.7 3.8 %collective-permute-start.2 = (bf16[8,1,2048]{2,0,1:T(8,128)(2,1)S(1)}, bf16[8,1,2048]{2,0,1:T(8,128)(2,1)S(1)}, u32[]{:S(2)}, u32[]{:S(2)}) collective-permute-start(bf16[8,1,2048]{2,0,1:T(8,128)(2,1)S(1)} %get-tuple-element.52), channel_id=1, source_target_pairs={{0,1},{1,2},{2,3},{3,4},{4,5},{5,6},{6,7},{7,8},{8,9},{9,10},{10,1... | collective-permute-start | bytes 98312 | tf_op jit(solution)/shard_map/ppermute | solution.py:39
  28.5 0.7 collective-permute-start.1
  29.1 1.9 %collective-permute-start.3 = (bf16[8,1,2048]{2,0,1:T(8,128)(2,1)S(1)}, bf16[8,1,2048]{2,0,1:T(8,128)(2,1)S(1)}, u32[]{:S(2)}, u32[]{:S(2)}) collective-permute-start(bf16[8,1,2048]{2,0,1:T(8,128)(2,1)S(1)} %get-tuple-element.54), channel_id=1, source_target_pairs={{1,0},{2,1},{3,2},{4,3},{5,4},{6,5},{7,6},{8,7},{9,8},{10,9},{11,1... | collective-permute-start | bytes 98312 | tf_op jit(solution)/shard_map/ppermute | solution.py:39
  31.1 4.1 %collective-permute-done.2 = bf16[8,1,2048]{2,0,1:T(8,128)(2,1)S(1)} collective-permute-done((bf16[8,1,2048]{2,0,1:T(8,128)(2,1)S(1)}, bf16[8,1,2048]{2,0,1:T(8,128)(2,1)S(1)}, u32[]{:S(2)}, u32[]{:S(2)}) %collective-permute-start.2) | collective-permute-done | bytes 32800 | tf_op jit(solution)/shard_map/ppermute | solution.py:39
  35.2 0.0 collective-permute-done.1
  35.2 3.5 %collective-permute-done.3 = bf16[8,1,2048]{2,0,1:T(8,128)(2,1)S(1)} collective-permute-done((bf16[8,1,2048]{2,0,1:T(8,128)(2,1)S(1)}, bf16[8,1,2048]{2,0,1:T(8,128)(2,1)S(1)}, u32[]{:S(2)}, u32[]{:S(2)}) %collective-permute-start.3) | collective-permute-done | bytes 32800 | tf_op jit(solution)/shard_map/ppermute | solution.py:39
  38.7 3.8 %all-to-all-done = f16[8,2,128,128]{3,2,1,0:T(8,128)(2,1)S(1)} async-done(((f16[8,2,128,128]{3,2,1,0:T(8,128)(2,1)}), f16[8,2,128,128]{3,2,1,0:T(8,128)(2,1)S(1)}, u32[]{:S(2)}, u32[]{:S(2)}) %all-to-all-start) | async-done | bytes 524320 | tf_op jit(solution)/shard_map/all_to_all | solution.py:411
  42.5 0.1 convert_reduce_fusion
  42.5 0.0 copy-done.1
  42.6 0.1 multiply_convert_fusion
  42.7 9.0 %collective-permute-start.4 = (f16[2,128,128]{2,1,0:T(8,128)(2,1)S(1)}, f16[2,128,128]{2,1,0:T(8,128)(2,1)S(1)}, u32[]{:S(2)}, u32[]{:S(2)}) collective-permute-start(f16[2,128,128]{2,1,0:T(8,128)(2,1)S(1)} %multiply_convert_fusion), channel_id=1, source_target_pairs={{0,16},{16,0},{1,17},{17,1},{2,18},{18,2},{3,19},{19,3},{4,20},{20... | collective-permute-start | bytes 196616 | tf_op jit(solution)/shard_map/ppermute | solution.py:386
  51.7 2.4 %collective-permute-done.4 = f16[2,128,128]{2,1,0:T(8,128)(2,1)S(1)} collective-permute-done((f16[2,128,128]{2,1,0:T(8,128)(2,1)S(1)}, f16[2,128,128]{2,1,0:T(8,128)(2,1)S(1)}, u32[]{:S(2)}, u32[]{:S(2)}) %collective-permute-start.4) | collective-permute-done | bytes 65568 | tf_op jit(solution)/shard_map/ppermute | solution.py:386
  54.1 0.1 fusion.2
  54.2 0.9 %broadcast_in_dim.35 = bf16[8,2,128,128]{3,2,1,0:T(8,128)(2,1)} broadcast(bf16[2,128,128]{2,1,0:T(8,128)(2,1)S(1)} %get-tuple-element.46), dimensions={1,2,3} | broadcast | bytes 589824 | tf_op jit(solution)/shard_map/broadcast_in_dim | solution.py:419
  55.1 4.2 %all-to-all-start.1 = ((bf16[8,2,128,128]{3,2,1,0:T(8,128)(2,1)}), bf16[8,2,128,128]{3,2,1,0:T(8,128)(2,1)}, u32[]{:S(2)}, u32[]{:S(2)}) async-start(bf16[8,2,128,128]{3,2,1,0:T(8,128)(2,1)} %broadcast_in_dim.35), calls=%async_computation.1 | async-start | bytes 1048576 | tf_op jit(solution)/shard_map/all_to_all | solution.py:420
  59.2 0.1 fusion.3
  59.3 2.6 %collective-permute-start.5 = (bf16[1,6,2048]{2,0,1:T(2,128)(2,1)S(1)}, bf16[1,6,2048]{2,0,1:T(2,128)(2,1)S(1)}, u32[]{:S(2)}, u32[]{:S(2)}) collective-permute-start(bf16[1,6,2048]{2,0,1:T(2,128)(2,1)S(1)} %get-tuple-element.50), channel_id=1, source_target_pairs={{0,32},{32,64},{64,96},{96,128},{128,160},{160,192},{192,224},{224... | collective-permute-start | bytes 73736 | tf_op jit(solution)/shard_map/ppermute | solution.py:49
  61.9 1.3 %collective-permute-start.6 = (bf16[1,6,2048]{2,0,1:T(2,128)(2,1)S(1)}, bf16[1,6,2048]{2,0,1:T(2,128)(2,1)S(1)}, u32[]{:S(2)}, u32[]{:S(2)}) collective-permute-start(bf16[1,6,2048]{2,0,1:T(2,128)(2,1)S(1)} %get-tuple-element.51), channel_id=1, source_target_pairs={{32,0},{64,32},{96,64},{128,96},{160,128},{192,160},{224,192},{256... | collective-permute-start | bytes 73736 | tf_op jit(solution)/shard_map/ppermute | solution.py:49
  63.2 0.0 collective-permute-done.5
  63.2 3.9 %collective-permute-done.6 = bf16[1,6,2048]{2,0,1:T(2,128)(2,1)S(1)} collective-permute-done((bf16[1,6,2048]{2,0,1:T(2,128)(2,1)S(1)}, bf16[1,6,2048]{2,0,1:T(2,128)(2,1)S(1)}, u32[]{:S(2)}, u32[]{:S(2)}) %collective-permute-start.6) | collective-permute-done | bytes 24608 | tf_op jit(solution)/shard_map/ppermute | solution.py:49
  67.1 0.2 fusion.1
  67.3 0.1 maximum_bitcast_fusion.field
  67.4 3.2 %close_window.1 = (f32[1,8,2048]{2,1,0:T(8,128)}, bf16[12,4,2,128,128]{4,3,2,1,0:T(8,128)(2,1)S(1)}, f32[4,128,128]{2,1,0:T(8,128)S(1)}) custom-call(s32[3]{0:T(128)S(1)} %pad_add_fusion.place, f32[2,128,128]{2,1,0:T(8,128)S(1)} %get-tuple-element.47.both, bf16[3,6,8,2048]{3,2,1,0:T(8,128)(2,1)S(1)} %maximum_bitcast_fusion.field, ...), custom_call_target="tpu_custom_call" | custom-call | bytes 131072 | tf_op jit(solution)/shard_map/close_window/pallas_call | solution.py:369
  70.6 4.6 %all-to-all-done.1.views = bf16[8,2,128,128]{3,2,1,0:T(8,128)(2,1)} async-done(((bf16[8,2,128,128]{3,2,1,0:T(8,128)(2,1)}), bf16[8,2,128,128]{3,2,1,0:T(8,128)(2,1)}, u32[]{:S(2)}, u32[]{:S(2)}) %all-to-all-start.1) | async-done | bytes 524320 | tf_op jit(solution)/shard_map/all_to_all | solution.py:420
  75.3 4.3 %collective-permute-start.7 = (bf16[8,2,128,128]{3,2,1,0:T(8,128)(2,1)}, bf16[8,2,128,128]{3,2,1,0:T(8,128)(2,1)S(1)}, u32[]{:S(2)}, u32[]{:S(2)}) collective-permute-start(bf16[8,2,128,128]{3,2,1,0:T(8,128)(2,1)} %all-to-all-done.1.views), channel_id=1, source_target_pairs={{0,1},{1,0},{2,3},{3,2},{4,5},{5,4},{6,7},{7,6},{8,9},{9,8},{10,11... | collective-permute-start | bytes 1572872 | tf_op jit(solution)/shard_map/ppermute | solution.py:386
  79.6 5.0 %load_spread.1 = (f32[4,128,128]{2,1,0:T(8,128)S(1)}, bf16[16,4,2,128,128]{4,3,2,1,0:T(8,128)(2,1)S(1)}) custom-call(s32[3]{0:T(128)S(1)} %pad_add_fusion.place, s32[32,128]{1,0:T(8,128)S(4)} %get-tuple-element.25.offsets, s32[32,128]{1,0:T(8,128)S(4)} %get-tuple-element.26.counts, bf16[8,2,128,128]{3,2,1,0:T(8,128)(2,1)} %all-to-all-done.1.views, ...), custom_call_target="tpu_custom_call" | custom-call | flops 536870912 | bytes 4194304 | tf_op jit(solution)/shard_map/load_spread/pallas_call | solution.py:316
  84.6 0.0 collective-permute-done.7.views
  84.6 2.7 %spread.1 = f32[8,4,2048]{2,1,0:T(4,128)} custom-call(s32[3]{0:T(128)S(1)} %pad_add_fusion.place, s32[32,128]{1,0:T(8,128)S(4)} %get-tuple-element.25.offsets, s32[32,128]{1,0:T(8,128)S(4)} %get-tuple-element.26.counts, bf16[8,2,128,128]{3,2,1,0:T(8,128)(2,1)S(1)} %collective-permute-done.7.views, bf16[16,4,2,128,128]{4,3,2,1,0:T(8,128)(2,1)S(1)} %get-tuple-element.42.tiles, ...), custom_call_target="tpu_custom_call" | custom-call | flops 268435456 | bytes 2097152 | tf_op jit(solution)/shard_map/spread/pallas_call | solution.py:338
  (4 shorter events, 0.1 us)
Async XLA Ops:
  5.3 19.3 %copy-start = (bf16[8,4,2048]{2,1,0:T(4,128)(2,1)S(1)}, bf16[8,4,2048]{2,1,0:T(4,128)(2,1)}, u32[]{:S(2)}) copy-start(bf16[8,4,2048]{2,1,0:T(4,128)(2,1)} %volume_hbm.1) | copy-start | bytes 393220
  5.3 37.3 %copy-start.1 = (f32[1,8,2048]{2,1,0:T(8,128)S(1)}, f32[1,8,2048]{2,1,0:T(8,128)}, u32[]{:S(2)}) copy-start(f32[1,8,2048]{2,1,0:T(8,128)} %param.6) | copy-start | bytes 196612
  5.3 14.8 %collective-permute-start = (f32[8,2,128,128]{3,2,1,0:T(8,128)S(1)}, f32[8,2,128,128]{3,2,1,0:T(8,128)S(1)}, u32[]{:S(2)}, u32[]{:S(2)}) collective-permute-start(f32[8,2,128,128]{3,2,1,0:T(8,128)S(1)} %get-tuple-element.29), channel_id=1, source_target_pairs={{0,1},{1,0},{2,3},{3,2},{4,5},{5,4},{6,7},{7,6},{8,9},{9,8},{10,11... | collective-permute-start | bytes 3145736 | tf_op jit(solution)/shard_map/ppermute | solution.py:386
  21.0 21.4 %all-to-all-start = ((f16[8,2,128,128]{3,2,1,0:T(8,128)(2,1)}), f16[8,2,128,128]{3,2,1,0:T(8,128)(2,1)S(1)}, u32[]{:S(2)}, u32[]{:S(2)}) async-start(f16[8,2,128,128]{3,2,1,0:T(8,128)(2,1)} %add_convert_fusion), calls=%async_computation | async-start | bytes 1048576 | tf_op jit(solution)/shard_map/all_to_all | solution.py:411
  24.7 10.5 %collective-permute-start.2 = (bf16[8,1,2048]{2,0,1:T(8,128)(2,1)S(1)}, bf16[8,1,2048]{2,0,1:T(8,128)(2,1)S(1)}, u32[]{:S(2)}, u32[]{:S(2)}) collective-permute-start(bf16[8,1,2048]{2,0,1:T(8,128)(2,1)S(1)} %get-tuple-element.52), channel_id=1, source_target_pairs={{0,1},{1,2},{2,3},{3,4},{4,5},{5,6},{6,7},{7,8},{8,9},{9,10},{10,1... | collective-permute-start | bytes 98312 | tf_op jit(solution)/shard_map/ppermute | solution.py:39
  28.5 6.7 %collective-permute-start.1 = (bf16[8,1,2048]{2,0,1:T(8,128)(2,1)S(1)}, bf16[8,1,2048]{2,0,1:T(8,128)(2,1)S(1)}, u32[]{:S(2)}, u32[]{:S(2)}) collective-permute-start(bf16[8,1,2048]{2,0,1:T(8,128)(2,1)S(1)} %get-tuple-element.53), channel_id=1, source_target_pairs={{15,16},{16,15},{47,48},{48,47},{79,80},{80,79},{111,112},{112,111... | collective-permute-start | bytes 98312 | tf_op jit(solution)/shard_map/ppermute | solution.py:40
  29.1 9.5 %collective-permute-start.3 = (bf16[8,1,2048]{2,0,1:T(8,128)(2,1)S(1)}, bf16[8,1,2048]{2,0,1:T(8,128)(2,1)S(1)}, u32[]{:S(2)}, u32[]{:S(2)}) collective-permute-start(bf16[8,1,2048]{2,0,1:T(8,128)(2,1)S(1)} %get-tuple-element.54), channel_id=1, source_target_pairs={{1,0},{2,1},{3,2},{4,3},{5,4},{6,5},{7,6},{8,7},{9,8},{10,9},{11,1... | collective-permute-start | bytes 98312 | tf_op jit(solution)/shard_map/ppermute | solution.py:39
  42.7 11.4 %collective-permute-start.4 = (f16[2,128,128]{2,1,0:T(8,128)(2,1)S(1)}, f16[2,128,128]{2,1,0:T(8,128)(2,1)S(1)}, u32[]{:S(2)}, u32[]{:S(2)}) collective-permute-start(f16[2,128,128]{2,1,0:T(8,128)(2,1)S(1)} %multiply_convert_fusion), channel_id=1, source_target_pairs={{0,16},{16,0},{1,17},{17,1},{2,18},{18,2},{3,19},{19,3},{4,20},{20... | collective-permute-start | bytes 196616 | tf_op jit(solution)/shard_map/ppermute | solution.py:386
  55.1 20.2 %all-to-all-start.1 = ((bf16[8,2,128,128]{3,2,1,0:T(8,128)(2,1)}), bf16[8,2,128,128]{3,2,1,0:T(8,128)(2,1)}, u32[]{:S(2)}, u32[]{:S(2)}) async-start(bf16[8,2,128,128]{3,2,1,0:T(8,128)(2,1)} %broadcast_in_dim.35), calls=%async_computation.1 | async-start | bytes 1048576 | tf_op jit(solution)/shard_map/all_to_all | solution.py:420
  59.3 3.9 %collective-permute-start.5 = (bf16[1,6,2048]{2,0,1:T(2,128)(2,1)S(1)}, bf16[1,6,2048]{2,0,1:T(2,128)(2,1)S(1)}, u32[]{:S(2)}, u32[]{:S(2)}) collective-permute-start(bf16[1,6,2048]{2,0,1:T(2,128)(2,1)S(1)} %get-tuple-element.50), channel_id=1, source_target_pairs={{0,32},{32,64},{64,96},{96,128},{128,160},{160,192},{192,224},{224... | collective-permute-start | bytes 73736 | tf_op jit(solution)/shard_map/ppermute | solution.py:49
  61.9 5.2 %collective-permute-start.6 = (bf16[1,6,2048]{2,0,1:T(2,128)(2,1)S(1)}, bf16[1,6,2048]{2,0,1:T(2,128)(2,1)S(1)}, u32[]{:S(2)}, u32[]{:S(2)}) collective-permute-start(bf16[1,6,2048]{2,0,1:T(2,128)(2,1)S(1)} %get-tuple-element.51), channel_id=1, source_target_pairs={{32,0},{64,32},{96,64},{128,96},{160,128},{192,160},{224,192},{256... | collective-permute-start | bytes 73736 | tf_op jit(solution)/shard_map/ppermute | solution.py:49
  75.3 9.3 %collective-permute-start.7 = (bf16[8,2,128,128]{3,2,1,0:T(8,128)(2,1)}, bf16[8,2,128,128]{3,2,1,0:T(8,128)(2,1)S(1)}, u32[]{:S(2)}, u32[]{:S(2)}) collective-permute-start(bf16[8,2,128,128]{3,2,1,0:T(8,128)(2,1)} %all-to-all-done.1.views), channel_id=1, source_target_pairs={{0,1},{1,0},{2,3},{3,2},{4,5},{5,4},{6,7},{7,6},{8,9},{9,8},{10,11... | collective-permute-start | bytes 1572872 | tf_op jit(solution)/shard_map/ppermute | solution.py:386

commit v6 on v4

--- a/solution.py
+++ b/solution.py
@@ -51,6 +51,7 @@
 
 PAD = 4
 GROUP = 4
+BLOCKS = ZHI * YS
 
 
 def copy_rows(count):
@@ -93,7 +94,7 @@
 
 
 def project_one(j, core, first_row, offsets, counts, windows, tiles, out, scale):
-    rows = tiles.shape[1]
+    rows = tiles.shape[2]
     count, lanes = out.shape[2:]
     angle = angle_of(j, core)
     pieces = []
@@ -101,26 +102,27 @@
         row = first_row + r
         for start in band_windows(offsets[angle, row], counts[angle, row], 1, r, rows, count):
             pieces.append(windows[pl.ds(start, count), :])
-    weights = tiles[angle].reshape(len(pieces) * lanes, lanes)
+    weights = tiles[j % ZHI, j // ZHI].reshape(len(pieces) * lanes, lanes)
     view = jnp.dot(jnp.concatenate(pieces, 1), weights, preferred_element_type=jnp.float32)
     out[j // ZHI, j % ZHI] = view * scale
 
 
 def load_project_kernel(
-    place, offsets_hbm, counts_hbm, volume_hbm, tiles_hbm, out, tiles, windows, offsets, counts, volume, tile_sems, sems,
+    place, offsets_hbm, counts_hbm, volume_hbm, tiles_hbm, out, later, windows, offsets, counts, volume, tiles, sems, more_sems,
     *, scale
 ):
     core, first_row = place[0], place[1]
-    blocks, rows = ZHI * YS, tiles.shape[1]
+    rows = tiles.shape[2]
     count, lanes = out.shape[2:]
     small = [
-        pltpu.make_async_copy(source, target, sems.at[i])
+        pltpu.make_async_copy(source, target, more_sems.at[i])
         for i, (source, target) in enumerate(
             ((volume_hbm, volume), (offsets_hbm, offsets), (counts_hbm, counts))
         )
     ]
-    copies = tile_copies(tiles_hbm, tiles, tile_sems, 1 - core)
-    for copy in small + copies[:blocks]:
+    now = group_copies(tiles_hbm, tiles, sems, 1 - core)
+    then = tile_copy(tiles_hbm, later, more_sems.at[len(small)], core, 0, BLOCKS)
+    for copy in small + now:
         copy.start()
     small[0].wait()
     for r in range(rows):
@@ -131,12 +133,13 @@
     fill_zeros(windows, rows, count)
     small[1].wait()
     small[2].wait()
-    for first in range(0, blocks, GROUP):
-        wait_group(copies, first)
+    for i, first in enumerate(range(0, BLOCKS, GROUP)):
+        now[i].wait()
+        if i == 0:
+            then.start()
         for j in range(first, first + GROUP):
             project_one(j, 1 - core, first_row, offsets, counts, windows, tiles, out, scale)
-    for copy in copies[blocks:]:
-        copy.wait()
+    then.wait()
 
 
 def project_kernel(place, offsets, counts, windows, tiles, out, *, scale):
@@ -144,23 +147,25 @@
         project_one(j, place[0], place[1], offsets, counts, windows, tiles, out, scale)
 
 
-def tile_copies(tiles_hbm, tiles, sems, first_core):
-    blocks = ZHI * YS
-    order = [angle_of(j, first_core) for j in range(blocks)] + [angle_of(j, 1 - first_core) for j in range(blocks)]
-    return [pltpu.make_async_copy(tiles_hbm.at[a], tiles.at[a], sems.at[i]) for i, a in enumerate(order)]
-
-
-def wait_group(copies, first):
-    blocks = ZHI * YS
-    for copy in copies[first : first + GROUP]:
-        copy.wait()
-    if first == 0:
-        for copy in copies[blocks:]:
-            copy.start()
+def tile_copy(tiles_hbm, tiles, sem, core, first, end):
+    by_core = tiles_hbm.reshape((ZHI, YS, CORES) + tuple(tiles_hbm.shape[1:]))
+    ys = pl.ds(first // ZHI, (end - first) // ZHI)
+    return pltpu.make_async_copy(by_core.at[:, ys, core], tiles.at[:, ys], sem)
+
+
+def group_copies(tiles_hbm, tiles, sems, core):
+    return [
+        tile_copy(tiles_hbm, tiles, sems.at[i], core, first, first + GROUP)
+        for i, first in enumerate(range(0, BLOCKS, GROUP))
+    ]
+
+
+def tiles_of(tiles):
+    return (ZHI, YS) + tuple(tiles.shape[1:])
 
 
 def spread_group(first, core, first_row, offsets, counts, windows, tiles, begin, out):
-    blocks, rows = ZHI * YS, tiles.shape[1]
+    blocks, rows = BLOCKS, tiles.shape[2]
     count = out.shape[1]
     for r in range(rows):
         row = first_row + r
@@ -170,7 +175,7 @@
             starts = band_windows(offsets[angle, row], counts[angle, row], -1, j, blocks, count)
             for k, start in enumerate(starts):
                 lhs.append(windows[pl.ds(start, count), :])
-                rhs.append(tiles[angle, r, k])
+                rhs.append(tiles[j % ZHI, j // ZHI, r, k])
         part = lax.dot_general(
             jnp.concatenate(lhs, 1),
             jnp.concatenate(rhs, 1),
@@ -216,9 +221,10 @@
     return here + step_size * smooth_weight * div
 
 
-def load_spread_kernel(place, offsets, counts, views, field, tiles_hbm, out, tiles, base, windows, sems):
-    copies = tile_copies(tiles_hbm, tiles, sems, place[0])
-    for copy in copies[: ZHI * YS]:
+def load_spread_kernel(place, offsets, counts, views, field, tiles_hbm, out, later, base, windows, tiles, sems, later_sem):
+    now = group_copies(tiles_hbm, tiles, sems, place[0])
+    then = tile_copy(tiles_hbm, later, later_sem, 1 - place[0], 0, BLOCKS)
+    for copy in now:
         copy.start()
     fill_views(windows, views)
     depth, lanes = field.shape[2], base.shape[2]
@@ -226,11 +232,12 @@
         line = smooth(field, r)
         for t in range(line.shape[1] // lanes):
             base[r, t * depth : (t + 1) * depth, :] = line[:, t * lanes : (t + 1) * lanes]
-    for first in range(0, ZHI * YS, GROUP):
-        wait_group(copies, first)
+    for i, first in enumerate(range(0, BLOCKS, GROUP)):
+        now[i].wait()
+        if i == 0:
+            then.start()
         spread_group(first, place[0], place[1], offsets, counts, windows, tiles, None, out)
-    for copy in copies[ZHI * YS :]:
-        copy.wait()
+    then.wait()
 
 
 def spread_kernel(place, offsets, counts, views, tiles, begin, base, out, total, windows):
@@ -274,15 +281,16 @@
         out_specs=[VMEM, VMEM, VMEM, SMEM, SMEM],
         out_shape=[
             pltpu.VMEM((YS, ZHI, count, lanes), jnp.float32),
-            pltpu.VMEM(tiles.shape, tiles.dtype),
+            pltpu.VMEM(tiles_of(tiles), tiles.dtype),
             pltpu.VMEM((window_rows(rows, count), lanes), volume.dtype),
             pltpu.SMEM(offsets.shape, offsets.dtype),
             pltpu.SMEM(counts.shape, counts.dtype),
         ],
         scratch_shapes=[
             pltpu.VMEM(volume.shape, volume.dtype),
-            pltpu.SemaphoreType.DMA((tiles.shape[0],)),
-            pltpu.SemaphoreType.DMA((3,)),
+            pltpu.VMEM(tiles_of(tiles), tiles.dtype),
+            pltpu.SemaphoreType.DMA((BLOCKS // GROUP,)),
+            pltpu.SemaphoreType.DMA((4,)),
         ],
         compiler_params=params(),
         cost_estimate=cost(tiles, 2),
@@ -311,12 +319,14 @@
         out_specs=[VMEM, VMEM, VMEM],
         out_shape=[
             pltpu.VMEM(lines, jnp.float32),
-            pltpu.VMEM(tiles.shape, tiles.dtype),
+            pltpu.VMEM(tiles_of(tiles), tiles.dtype),
             pltpu.VMEM(lines, jnp.float32),
         ],
         scratch_shapes=[
             pltpu.VMEM((window_rows(ZHI * YS, count), lanes), jnp.bfloat16),
-            pltpu.SemaphoreType.DMA((tiles.shape[0],)),
+            pltpu.VMEM(tiles_of(tiles), tiles.dtype),
+            pltpu.SemaphoreType.DMA((BLOCKS // GROUP,)),
+            pltpu.SemaphoreType.DMA,
         ],
         compiler_params=params(),
         cost_estimate=cost(tiles, 2),

time: 86.7 us -> 86.5 us (level)
  no operation moved by 1% of the time
where the time goes in v6:
time: 86.5 us; the launch traced here: 86 us
  starting transfers between devices  43.5 us (50%)
  waiting for transfers between devices  24.1 us (28%)
  Pallas kernels  14.8 us (17%)
  other arithmetic  1.59 us (2%)
  local copies, waits for them, and re-layouts  1.07 us (1%)
    ppermute x3, starting transfers between devices, swap(): return lax.ppermute(array, axis, [(0, 1), (1, 0)])  25.8 us
    all_to_all x1, waiting for transfers between devices, per_device(): views = lax.all_to_all(copies, 'y', 0, 0, tiled=True)  6.21 us
    pallas_call x1, Pallas kernels, load_project(): pl.pallas_call(partial(load_project_kernel, scale=scale), in_specs=[SMEM,...  4.59 us
    pallas_call x1, Pallas kernels, load_spread(): pl.pallas_call(load_spread_kernel, in_specs=[SMEM, SMEM, SMEM, VMEM, VMEM...  4.43 us
    ppermute x1, waiting for transfers between devices, with_row_neighbours(): lax.ppermute(last, ANGLE, up)  4.1 us
    ppermute x1, waiting for transfers between devices, with_slab_neighbours(): lax.ppermute(first, SLAB, down)  3.82 us
    ppermute x1, starting transfers between devices, with_row_neighbours(): lax.ppermute(last, ANGLE, up)  3.79 us
    all_to_all x1, waiting for transfers between devices, per_device(): parts = lax.all_to_all(pair, 'y', 0, 0, tiled=True)  3.78 us
  transfers between devices with their start and end apart: 10, of which 7 were waited for; matrix products, arithmetic and copies ran while one was open for 1% of the time, Pallas kernels for 9%

profile of v6, /device:TPU:1, one launch (start us, length us, event | category | flops | bytes accessed | tf_op | source)
XLA Modules:
  0.0 86.0 jit_solution(15790729142948541838)
XLA Ops:
  0.7 0.1 pad_add_fusion.place
  0.7 4.6 %load_project.1 = (f32[8,2,128,128]{3,2,1,0:T(8,128)S(1)}, bf16[2,8,4,2,128,128]{5,4,3,2,1,0:T(8,128)(2,1)S(1)}, bf16[1664,128]{1,0:T(8,128)(2,1)S(1)}, s32[32,128]{1,0:T(8,128)S(4)}, s32[32,128]{1,0:T(8,128)S(4)}) custom-call(s32[3]{0:T(128)S(1)} %pad_add_fusion.place, s32[32,128]{1,0:T(8,128)} %offsets_hbm.1, s32[32,128]{1,0:T(8,128)} %counts_hbm.1, ...), custom_call_target="tpu_custom_call" | custom-call | flops 536870912 | bytes 4194304 | tf_op jit(solution)/shard_map/load_project/pallas_call | solution.py:278
  5.3 12.4 %collective-permute-start = (f32[8,2,128,128]{3,2,1,0:T(8,128)S(1)}, f32[8,2,128,128]{3,2,1,0:T(8,128)S(1)}, u32[]{:S(2)}, u32[]{:S(2)}) collective-permute-start(f32[8,2,128,128]{3,2,1,0:T(8,128)S(1)} %get-tuple-element.26), channel_id=1, source_target_pairs={{0,1},{1,0},{2,3},{3,2},{4,5},{5,4},{6,7},{7,6},{8,9},{9,8},{10,11... | collective-permute-start | bytes 3145736 | tf_op jit(solution)/shard_map/ppermute | solution.py:373
  17.8 0.0 copy-start
  17.8 0.0 copy-start.1
  17.8 1.9 %project.1 = f32[8,2,128,128]{3,2,1,0:T(8,128)S(1)} custom-call(s32[3]{0:T(128)S(1)} %pad_add_fusion.place, s32[32,128]{1,0:T(8,128)S(4)} %get-tuple-element.22.offsets, s32[32,128]{1,0:T(8,128)S(4)} %get-tuple-element.23.counts, bf16[1664,128]{1,0:T(8,128)(2,1)S(1)} %get-tuple-element.24.windows, bf16[2,8,4,2,128,128]{5,4,3,2,1,0:T(8,128)(2,1)S(1)} %get-tuple-element.25.tiles), custom_call_target="tpu_custom_call" | custom-call | flops 268435456 | bytes 2097152 | tf_op jit(solution)/shard_map/project/pallas_call | solution.py:302
  19.7 0.3 collective-permute-done
  20.0 0.9 %add_convert_fusion = f16[8,2,128,128]{3,2,1,0:T(8,128)(2,1)} fusion(f32[8,2,128,128]{3,2,1,0:T(8,128)S(1)} %project.1, f32[8,2,128,128]{3,2,1,0:T(8,128)S(1)} %collective-permute-done), kind=kLoop, calls=%fused_computation.1 | loop fusion | flops 524288 | bytes 2621440 | tf_op jit(solution)/shard_map/convert_element_type | solution.py:396
  21.0 3.5 %all-to-all-start = ((f16[8,2,128,128]{3,2,1,0:T(8,128)(2,1)}), f16[8,2,128,128]{3,2,1,0:T(8,128)(2,1)S(1)}, u32[]{:S(2)}, u32[]{:S(2)}) async-start(f16[8,2,128,128]{3,2,1,0:T(8,128)(2,1)} %add_convert_fusion), calls=%async_computation | async-start | bytes 1048576 | tf_op jit(solution)/shard_map/all_to_all | solution.py:398
  24.5 0.0 copy-done
  24.5 0.1 copy.7
  24.6 3.8 %collective-permute-start.2 = (bf16[8,1,2048]{2,0,1:T(8,128)(2,1)S(1)}, bf16[8,1,2048]{2,0,1:T(8,128)(2,1)S(1)}, u32[]{:S(2)}, u32[]{:S(2)}) collective-permute-start(bf16[8,1,2048]{2,0,1:T(8,128)(2,1)S(1)} %get-tuple-element.46), channel_id=1, source_target_pairs={{0,1},{1,2},{2,3},{3,4},{4,5},{5,6},{6,7},{7,8},{8,9},{9,10},{10,1... | collective-permute-start | bytes 98312 | tf_op jit(solution)/shard_map/ppermute | solution.py:39
  28.4 0.7 collective-permute-start.1
  29.1 1.9 %collective-permute-start.3 = (bf16[8,1,2048]{2,0,1:T(8,128)(2,1)S(1)}, bf16[8,1,2048]{2,0,1:T(8,128)(2,1)S(1)}, u32[]{:S(2)}, u32[]{:S(2)}) collective-permute-start(bf16[8,1,2048]{2,0,1:T(8,128)(2,1)S(1)} %get-tuple-element.48), channel_id=1, source_target_pairs={{1,0},{2,1},{3,2},{4,3},{5,4},{6,5},{7,6},{8,7},{9,8},{10,9},{11,1... | collective-permute-start | bytes 98312 | tf_op jit(solution)/shard_map/ppermute | solution.py:39
  31.0 4.1 %collective-permute-done.2 = bf16[8,1,2048]{2,0,1:T(8,128)(2,1)S(1)} collective-permute-done((bf16[8,1,2048]{2,0,1:T(8,128)(2,1)S(1)}, bf16[8,1,2048]{2,0,1:T(8,128)(2,1)S(1)}, u32[]{:S(2)}, u32[]{:S(2)}) %collective-permute-start.2) | collective-permute-done | bytes 32800 | tf_op jit(solution)/shard_map/ppermute | solution.py:39
  35.1 0.0 collective-permute-done.1
  35.1 3.5 %collective-permute-done.3 = bf16[8,1,2048]{2,0,1:T(8,128)(2,1)S(1)} collective-permute-done((bf16[8,1,2048]{2,0,1:T(8,128)(2,1)S(1)}, bf16[8,1,2048]{2,0,1:T(8,128)(2,1)S(1)}, u32[]{:S(2)}, u32[]{:S(2)}) %collective-permute-start.3) | collective-permute-done | bytes 32800 | tf_op jit(solution)/shard_map/ppermute | solution.py:39
  38.6 3.8 %all-to-all-done = f16[8,2,128,128]{3,2,1,0:T(8,128)(2,1)S(1)} async-done(((f16[8,2,128,128]{3,2,1,0:T(8,128)(2,1)}), f16[8,2,128,128]{3,2,1,0:T(8,128)(2,1)S(1)}, u32[]{:S(2)}, u32[]{:S(2)}) %all-to-all-start) | async-done | bytes 524320 | tf_op jit(solution)/shard_map/all_to_all | solution.py:398
  42.4 0.1 convert_reduce_fusion
  42.5 0.0 copy-done.1
  42.5 0.1 multiply_convert_fusion
  42.6 9.0 %collective-permute-start.4 = (f16[2,128,128]{2,1,0:T(8,128)(2,1)S(1)}, f16[2,128,128]{2,1,0:T(8,128)(2,1)S(1)}, u32[]{:S(2)}, u32[]{:S(2)}) collective-permute-start(f16[2,128,128]{2,1,0:T(8,128)(2,1)S(1)} %multiply_convert_fusion), channel_id=1, source_target_pairs={{0,16},{16,0},{1,17},{17,1},{2,18},{18,2},{3,19},{19,3},{4,20},{20... | collective-permute-start | bytes 196616 | tf_op jit(solution)/shard_map/ppermute | solution.py:373
  51.6 2.4 %collective-permute-done.4 = f16[2,128,128]{2,1,0:T(8,128)(2,1)S(1)} collective-permute-done((f16[2,128,128]{2,1,0:T(8,128)(2,1)S(1)}, f16[2,128,128]{2,1,0:T(8,128)(2,1)S(1)}, u32[]{:S(2)}, u32[]{:S(2)}) %collective-permute-start.4) | collective-permute-done | bytes 65568 | tf_op jit(solution)/shard_map/ppermute | solution.py:373
  54.0 0.1 fusion.2
  54.1 0.9 %broadcast_in_dim.35 = bf16[8,2,128,128]{3,2,1,0:T(8,128)(2,1)} broadcast(bf16[2,128,128]{2,1,0:T(8,128)(2,1)S(1)} %get-tuple-element.40), dimensions={1,2,3} | broadcast | bytes 589824 | tf_op jit(solution)/shard_map/broadcast_in_dim | solution.py:407
  55.0 3.5 %all-to-all-start.1 = ((bf16[8,2,128,128]{3,2,1,0:T(8,128)(2,1)}), bf16[8,2,128,128]{3,2,1,0:T(8,128)(2,1)S(1)}, u32[]{:S(2)}, u32[]{:S(2)}) async-start(bf16[8,2,128,128]{3,2,1,0:T(8,128)(2,1)} %broadcast_in_dim.35), calls=%async_computation.1 | async-start | bytes 1048576 | tf_op jit(solution)/shard_map/all_to_all | solution.py:408
  58.5 0.1 fusion.3
  58.6 3.1 %collective-permute-start.5 = (bf16[1,6,2048]{2,0,1:T(2,128)(2,1)S(1)}, bf16[1,6,2048]{2,0,1:T(2,128)(2,1)S(1)}, u32[]{:S(2)}, u32[]{:S(2)}) collective-permute-start(bf16[1,6,2048]{2,0,1:T(2,128)(2,1)S(1)} %get-tuple-element.44), channel_id=1, source_target_pairs={{0,32},{32,64},{64,96},{96,128},{128,160},{160,192},{192,224},{224... | collective-permute-start | bytes 73736 | tf_op jit(solution)/shard_map/ppermute | solution.py:49
  61.7 1.3 %collective-permute-start.6 = (bf16[1,6,2048]{2,0,1:T(2,128)(2,1)S(1)}, bf16[1,6,2048]{2,0,1:T(2,128)(2,1)S(1)}, u32[]{:S(2)}, u32[]{:S(2)}) collective-permute-start(bf16[1,6,2048]{2,0,1:T(2,128)(2,1)S(1)} %get-tuple-element.45), channel_id=1, source_target_pairs={{32,0},{64,32},{96,64},{128,96},{160,128},{192,160},{224,192},{256... | collective-permute-start | bytes 73736 | tf_op jit(solution)/shard_map/ppermute | solution.py:49
  63.0 0.0 collective-permute-done.5
  63.0 3.8 %collective-permute-done.6 = bf16[1,6,2048]{2,0,1:T(2,128)(2,1)S(1)} collective-permute-done((bf16[1,6,2048]{2,0,1:T(2,128)(2,1)S(1)}, bf16[1,6,2048]{2,0,1:T(2,128)(2,1)S(1)}, u32[]{:S(2)}, u32[]{:S(2)}) %collective-permute-start.6) | collective-permute-done | bytes 24608 | tf_op jit(solution)/shard_map/ppermute | solution.py:49
  66.8 0.2 fusion.1
  67.0 0.1 maximum_bitcast_fusion.field
  67.1 1.2 %own_view.1 = f32[1,8,2048]{2,1,0:T(8,128)} custom-call(s32[3]{0:T(128)S(1)} %pad_add_fusion.place, f32[2,128,128]{2,1,0:T(8,128)S(1)} %get-tuple-element.41.both), custom_call_target="tpu_custom_call" | custom-call | bytes 131072 | tf_op jit(solution)/shard_map/own_view/pallas_call | solution.py:361
  68.3 6.2 %all-to-all-done.1.views = bf16[8,2,128,128]{3,2,1,0:T(8,128)(2,1)S(1)} async-done(((bf16[8,2,128,128]{3,2,1,0:T(8,128)(2,1)}), bf16[8,2,128,128]{3,2,1,0:T(8,128)(2,1)S(1)}, u32[]{:S(2)}, u32[]{:S(2)}) %all-to-all-start.1) | async-done | bytes 524320 | tf_op jit(solution)/shard_map/all_to_all | solution.py:408
  74.5 4.3 %collective-permute-start.7 = (bf16[8,2,128,128]{3,2,1,0:T(8,128)(2,1)S(1)}, bf16[8,2,128,128]{3,2,1,0:T(8,128)(2,1)S(1)}, u32[]{:S(2)}, u32[]{:S(2)}) collective-permute-start(bf16[8,2,128,128]{3,2,1,0:T(8,128)(2,1)S(1)} %all-to-all-done.1.views), channel_id=1, source_target_pairs={{0,1},{1,0},{2,3},{3,2},{4,5},{5,4},{6,7},{7,6},{8,9},{9,8},{10,11... | collective-permute-start | bytes 1572872 | tf_op jit(solution)/shard_map/ppermute | solution.py:373
  78.8 4.4 %load_spread.1 = (f32[4,128,128]{2,1,0:T(8,128)S(1)}, bf16[2,8,4,2,128,128]{5,4,3,2,1,0:T(8,128)(2,1)S(1)}, f32[4,128,128]{2,1,0:T(8,128)S(1)}) custom-call(s32[3]{0:T(128)S(1)} %pad_add_fusion.place, s32[32,128]{1,0:T(8,128)S(4)} %get-tuple-element.22.offsets, s32[32,128]{1,0:T(8,128)S(4)} %get-tuple-element.23.counts, ...), custom_call_target="tpu_custom_call" | custom-call | flops 536870912 | bytes 4194304 | tf_op jit(solution)/shard_map/load_spread/pallas_call | solution.py:316
  83.2 0.0 collective-permute-done.7.views
  83.2 2.7 %spread.1 = f32[8,4,2048]{2,1,0:T(4,128)} custom-call(s32[3]{0:T(128)S(1)} %pad_add_fusion.place, s32[32,128]{1,0:T(8,128)S(4)} %get-tuple-element.22.offsets, s32[32,128]{1,0:T(8,128)S(4)} %get-tuple-element.23.counts, bf16[8,2,128,128]{3,2,1,0:T(8,128)(2,1)S(1)} %collective-permute-done.7.views, ...), custom_call_target="tpu_custom_call" | custom-call | flops 268435456 | bytes 2097152 | tf_op jit(solution)/shard_map/spread/pallas_call | solution.py:339
  (4 shorter events, 0.1 us)
Async XLA Ops:
  5.3 14.7 %collective-permute-start = (f32[8,2,128,128]{3,2,1,0:T(8,128)S(1)}, f32[8,2,128,128]{3,2,1,0:T(8,128)S(1)}, u32[]{:S(2)}, u32[]{:S(2)}) collective-permute-start(f32[8,2,128,128]{3,2,1,0:T(8,128)S(1)} %get-tuple-element.26), channel_id=1, source_target_pairs={{0,1},{1,0},{2,3},{3,2},{4,5},{5,4},{6,7},{7,6},{8,9},{9,8},{10,11... | collective-permute-start | bytes 3145736 | tf_op jit(solution)/shard_map/ppermute | solution.py:373
  17.8 6.7 %copy-start = (bf16[8,4,2048]{2,1,0:T(4,128)(2,1)S(1)}, bf16[8,4,2048]{2,1,0:T(4,128)(2,1)}, u32[]{:S(2)}) copy-start(bf16[8,4,2048]{2,1,0:T(4,128)(2,1)} %volume_hbm.1) | copy-start | bytes 393220
  17.8 24.7 %copy-start.1 = (f32[1,8,2048]{2,1,0:T(8,128)S(1)}, f32[1,8,2048]{2,1,0:T(8,128)}, u32[]{:S(2)}) copy-start(f32[1,8,2048]{2,1,0:T(8,128)} %param.6) | copy-start | bytes 196612
  21.0 21.4 %all-to-all-start = ((f16[8,2,128,128]{3,2,1,0:T(8,128)(2,1)}), f16[8,2,128,128]{3,2,1,0:T(8,128)(2,1)S(1)}, u32[]{:S(2)}, u32[]{:S(2)}) async-start(f16[8,2,128,128]{3,2,1,0:T(8,128)(2,1)} %add_convert_fusion), calls=%async_computation | async-start | bytes 1048576 | tf_op jit(solution)/shard_map/all_to_all | solution.py:398
  24.6 10.5 %collective-permute-start.2 = (bf16[8,1,2048]{2,0,1:T(8,128)(2,1)S(1)}, bf16[8,1,2048]{2,0,1:T(8,128)(2,1)S(1)}, u32[]{:S(2)}, u32[]{:S(2)}) collective-permute-start(bf16[8,1,2048]{2,0,1:T(8,128)(2,1)S(1)} %get-tuple-element.46), channel_id=1, source_target_pairs={{0,1},{1,2},{2,3},{3,4},{4,5},{5,6},{6,7},{7,8},{8,9},{9,10},{10,1... | collective-permute-start | bytes 98312 | tf_op jit(solution)/shard_map/ppermute | solution.py:39
  28.4 6.7 %collective-permute-start.1 = (bf16[8,1,2048]{2,0,1:T(8,128)(2,1)S(1)}, bf16[8,1,2048]{2,0,1:T(8,128)(2,1)S(1)}, u32[]{:S(2)}, u32[]{:S(2)}) collective-permute-start(bf16[8,1,2048]{2,0,1:T(8,128)(2,1)S(1)} %get-tuple-element.47), channel_id=1, source_target_pairs={{15,16},{16,15},{47,48},{48,47},{79,80},{80,79},{111,112},{112,111... | collective-permute-start | bytes 98312 | tf_op jit(solution)/shard_map/ppermute | solution.py:40
  29.1 9.5 %collective-permute-start.3 = (bf16[8,1,2048]{2,0,1:T(8,128)(2,1)S(1)}, bf16[8,1,2048]{2,0,1:T(8,128)(2,1)S(1)}, u32[]{:S(2)}, u32[]{:S(2)}) collective-permute-start(bf16[8,1,2048]{2,0,1:T(8,128)(2,1)S(1)} %get-tuple-element.48), channel_id=1, source_target_pairs={{1,0},{2,1},{3,2},{4,3},{5,4},{6,5},{7,6},{8,7},{9,8},{10,9},{11,1... | collective-permute-start | bytes 98312 | tf_op jit(solution)/shard_map/ppermute | solution.py:39
  42.6 11.4 %collective-permute-start.4 = (f16[2,128,128]{2,1,0:T(8,128)(2,1)S(1)}, f16[2,128,128]{2,1,0:T(8,128)(2,1)S(1)}, u32[]{:S(2)}, u32[]{:S(2)}) collective-permute-start(f16[2,128,128]{2,1,0:T(8,128)(2,1)S(1)} %multiply_convert_fusion), channel_id=1, source_target_pairs={{0,16},{16,0},{1,17},{17,1},{2,18},{18,2},{3,19},{19,3},{4,20},{20... | collective-permute-start | bytes 196616 | tf_op jit(solution)/shard_map/ppermute | solution.py:373
  55.0 19.5 %all-to-all-start.1 = ((bf16[8,2,128,128]{3,2,1,0:T(8,128)(2,1)}), bf16[8,2,128,128]{3,2,1,0:T(8,128)(2,1)S(1)}, u32[]{:S(2)}, u32[]{:S(2)}) async-start(bf16[8,2,128,128]{3,2,1,0:T(8,128)(2,1)} %broadcast_in_dim.35), calls=%async_computation.1 | async-start | bytes 1048576 | tf_op jit(solution)/shard_map/all_to_all | solution.py:408
  58.6 4.4 %collective-permute-start.5 = (bf16[1,6,2048]{2,0,1:T(2,128)(2,1)S(1)}, bf16[1,6,2048]{2,0,1:T(2,128)(2,1)S(1)}, u32[]{:S(2)}, u32[]{:S(2)}) collective-permute-start(bf16[1,6,2048]{2,0,1:T(2,128)(2,1)S(1)} %get-tuple-element.44), channel_id=1, source_target_pairs={{0,32},{32,64},{64,96},{96,128},{128,160},{160,192},{192,224},{224... | collective-permute-start | bytes 73736 | tf_op jit(solution)/shard_map/ppermute | solution.py:49
  61.7 5.1 %collective-permute-start.6 = (bf16[1,6,2048]{2,0,1:T(2,128)(2,1)S(1)}, bf16[1,6,2048]{2,0,1:T(2,128)(2,1)S(1)}, u32[]{:S(2)}, u32[]{:S(2)}) collective-permute-start(bf16[1,6,2048]{2,0,1:T(2,128)(2,1)S(1)} %get-tuple-element.45), channel_id=1, source_target_pairs={{32,0},{64,32},{96,64},{128,96},{160,128},{192,160},{224,192},{256... | collective-permute-start | bytes 73736 | tf_op jit(solution)/shard_map/ppermute | solution.py:49
  74.5 8.8 %collective-permute-start.7 = (bf16[8,2,128,128]{3,2,1,0:T(8,128)(2,1)S(1)}, bf16[8,2,128,128]{3,2,1,0:T(8,128)(2,1)S(1)}, u32[]{:S(2)}, u32[]{:S(2)}) collective-permute-start(bf16[8,2,128,128]{3,2,1,0:T(8,128)(2,1)S(1)} %all-to-all-done.1.views), channel_id=1, source_target_pairs={{0,1},{1,0},{2,3},{3,2},{4,5},{5,4},{6,7},{7,6},{8,9},{9,8},{10,11... | collective-permute-start | bytes 1572872 | tf_op jit(solution)/shard_map/ppermute | solution.py:373

commit v7 on v6

--- a/solution.py
+++ b/solution.py
@@ -1,5 +1,3 @@
-from functools import partial
-
 import jax
 import jax.numpy as jnp
 from jax import lax
@@ -16,10 +14,6 @@
 ZHI, YS, CORES = 2, 8, 2
 SLAB = ("zlo", "x")
 ANGLE = ("zhi", "y", "core")
-
-PAIR_SCALE = 2.0**6
-PLANE_SCALE = 2.0**3
-
 
 def shifts_of(size, gap=None):
     up = [(i, i + 1) for i in range(size - 1) if i != gap]
@@ -93,7 +87,7 @@
     return ((j % ZHI) * YS + j // ZHI) * CORES + core
 
 
-def project_one(j, core, first_row, offsets, counts, windows, tiles, out, scale):
+def project_one(j, core, first_row, offsets, counts, windows, tiles, out):
     rows = tiles.shape[2]
     count, lanes = out.shape[2:]
     angle = angle_of(j, core)
@@ -104,12 +98,11 @@
             pieces.append(windows[pl.ds(start, count), :])
     weights = tiles[j % ZHI, j // ZHI].reshape(len(pieces) * lanes, lanes)
     view = jnp.dot(jnp.concatenate(pieces, 1), weights, preferred_element_type=jnp.float32)
-    out[j // ZHI, j % ZHI] = view * scale
+    out[j // ZHI, j % ZHI] = view
 
 
 def load_project_kernel(
-    place, offsets_hbm, counts_hbm, volume_hbm, tiles_hbm, out, later, windows, offsets, counts, volume, tiles, sems, more_sems,
-    *, scale
+    place, offsets_hbm, counts_hbm, volume_hbm, tiles_hbm, out, later, windows, offsets, counts, volume, tiles, sems, more_sems
 ):
     core, first_row = place[0], place[1]
     rows = tiles.shape[2]
@@ -138,13 +131,13 @@
         if i == 0:
             then.start()
         for j in range(first, first + GROUP):
-            project_one(j, 1 - core, first_row, offsets, counts, windows, tiles, out, scale)
+            project_one(j, 1 - core, first_row, offsets, counts, windows, tiles, out)
     then.wait()
 
 
-def project_kernel(place, offsets, counts, windows, tiles, out, *, scale):
+def project_kernel(place, offsets, counts, windows, tiles, out):
     for j in range(ZHI * YS):
-        project_one(j, place[0], place[1], offsets, counts, windows, tiles, out, scale)
+        project_one(j, place[0], place[1], offsets, counts, windows, tiles, out)
 
 
 def tile_copy(tiles_hbm, tiles, sem, core, first, end):
@@ -271,12 +264,12 @@
     return pltpu.with_memory_space_constraint(array, pltpu.HBM)
 
 
-def load_project(place, offsets, counts, volume, tiles, scale):
+def load_project(place, offsets, counts, volume, tiles):
     depth, rows, width = volume.shape
     lanes = tiles.shape[-1]
     count = depth * width // lanes
     return pl.pallas_call(
-        partial(load_project_kernel, scale=scale),
+        load_project_kernel,
         in_specs=[SMEM, ANY, ANY, ANY, ANY],
         out_specs=[VMEM, VMEM, VMEM, SMEM, SMEM],
         out_shape=[
@@ -298,9 +291,9 @@
     )(place, in_hbm(offsets), in_hbm(counts), in_hbm(volume), in_hbm(tiles))
 
 
-def project(place, offsets, counts, windows, tiles, like, scale):
+def project(place, offsets, counts, windows, tiles, like):
     return pl.pallas_call(
-        partial(project_kernel, scale=scale),
+        project_kernel,
         in_specs=[SMEM, SMEM, SMEM, VMEM, VMEM],
         out_specs=VMEM,
         out_shape=pltpu.VMEM(like.shape, jnp.float32),
@@ -374,7 +367,7 @@
 
 
 def per_device(volume, measured, ray_tiles, tile_offsets, band_counts):
-    f32, f16, bf16 = jnp.float32, jnp.float16, jnp.bfloat16
+    f32, bf16 = jnp.float32, jnp.bfloat16
     depth, row_count, width = volume.shape
     tile = ray_tiles.shape[3]
     tile_count = width // tile
@@ -389,20 +382,20 @@
     )
 
     away, tiles, windows, offsets, counts = load_project(
-        place, tile_offsets, band_counts, volume, ray_tiles, PAIR_SCALE
+        place, tile_offsets, band_counts, volume, ray_tiles
     )
     arrived = swap(away, "core")
-    kept = project(place, offsets, counts, windows, tiles, away, PAIR_SCALE)
-    pair = (kept + arrived).astype(f16)
+    kept = project(place, offsets, counts, windows, tiles, away)
+    pair = kept + arrived
     pair, late_volume = lax.optimization_barrier((pair, volume))
     parts = lax.all_to_all(pair, "y", 0, 0, tiled=True)
     with_rows = with_row_neighbours(late_volume, ends_plane, begins_plane)
     parts, with_rows = lax.optimization_barrier((parts, with_rows))
-    plane = jnp.sum(parts.astype(f32), axis=0) * (1 / PAIR_SCALE)
+    plane = jnp.sum(parts, axis=0)
     seen = measured.reshape(depth, tile_count, tile).transpose(1, 0, 2).reshape(count, tile)
     plane = plane - jnp.where(is_mine, seen[None], 0.0)
-    far = swap((plane * PLANE_SCALE).astype(f16), "zhi")
-    both = plane + far.astype(f32) * (1 / PLANE_SCALE)
+    far = swap(plane, "zhi")
+    both = plane + far
     residual = own_view(place, both, measured)
     copies = jnp.broadcast_to(both.astype(bf16)[None], (YS,) + both.shape)
     views = lax.all_to_all(copies, "y", 0, 0, tiled=True)

time: 86.5 us -> 103 us (1.19)
  the two profiles are of different devices: /device:TPU:1 before, /device:TPU:71 now
where the time goes in v7:
time: 103 us; the launch traced here: 102 us
  starting transfers between devices  42.2 us (41%)
  waiting for transfers between devices  41.7 us (40%)
  Pallas kernels  14.8 us (14%)
  other arithmetic  1.71 us (2%)
  local copies, waits for them, and re-layouts  1.07 us (1%)
    ppermute x3, starting transfers between devices, swap(): return lax.ppermute(array, axis, [(0, 1), (1, 0)])  19.8 us
    ppermute x1, waiting for transfers between devices, with_row_neighbours(): lax.ppermute(last, ANGLE, up)  13.4 us
    ppermute x3, waiting for transfers between devices, swap(): return lax.ppermute(array, axis, [(0, 1), (1, 0)])  9.29 us
    all_to_all x1, starting transfers between devices, per_device(): parts = lax.all_to_all(pair, 'y', 0, 0, tiled=True)  6.82 us
    all_to_all x1, waiting for transfers between devices, per_device(): views = lax.all_to_all(copies, 'y', 0, 0, tiled=True)  6.29 us
    ppermute x1, waiting for transfers between devices, with_row_neighbours(): lax.ppermute(first, ANGLE, down)  5.59 us
    pallas_call x1, Pallas kernels, load_project(): pl.pallas_call(load_project_kernel, in_specs=[SMEM, ANY, ANY, ANY, ANY],...  4.59 us
    pallas_call x1, Pallas kernels, load_spread(): pl.pallas_call(load_spread_kernel, in_specs=[SMEM, SMEM, SMEM, VMEM, VMEM...  4.43 us
  transfers between devices with their start and end apart: 10, of which 7 were waited for; matrix products, arithmetic and copies ran while one was open for 0% of the time, Pallas kernels for 7%

profile of v7, /device:TPU:71, one launch (start us, length us, event | category | flops | bytes accessed | tf_op | source)
XLA Modules:
  0.0 102.4 jit_solution(1542383607995893098)
XLA Ops:
  0.7 0.1 pad_add_fusion.place
  0.7 4.6 %load_project.1 = (f32[8,2,128,128]{3,2,1,0:T(8,128)S(1)}, bf16[2,8,4,2,128,128]{5,4,3,2,1,0:T(8,128)(2,1)S(1)}, bf16[1664,128]{1,0:T(8,128)(2,1)S(1)}, s32[32,128]{1,0:T(8,128)S(4)}, s32[32,128]{1,0:T(8,128)S(4)}) custom-call(s32[3]{0:T(128)S(1)} %pad_add_fusion.place, s32[32,128]{1,0:T(8,128)} %offsets_hbm.1, s32[32,128]{1,0:T(8,128)} %counts_hbm.1, ...), custom_call_target="tpu_custom_call" | custom-call | flops 536870912 | bytes 4194304 | tf_op jit(solution)/shard_map/load_project/pallas_call | solution.py:271
  5.3 2.6 %collective-permute-start = (f32[8,2,128,128]{3,2,1,0:T(8,128)S(1)}, f32[8,2,128,128]{3,2,1,0:T(8,128)S(1)}, u32[]{:S(2)}, u32[]{:S(2)}) collective-permute-start(f32[8,2,128,128]{3,2,1,0:T(8,128)S(1)} %get-tuple-element.26), channel_id=1, source_target_pairs={{0,1},{1,0},{2,3},{3,2},{4,5},{5,4},{6,7},{7,6},{8,9},{9,8},{10,11... | collective-permute-start | bytes 3145736 | tf_op jit(solution)/shard_map/ppermute | solution.py:366
  7.9 0.0 copy-start
  7.9 1.9 %project.1 = f32[8,2,128,128]{3,2,1,0:T(8,128)S(1)} custom-call(s32[3]{0:T(128)S(1)} %pad_add_fusion.place, s32[32,128]{1,0:T(8,128)S(4)} %get-tuple-element.22.offsets, s32[32,128]{1,0:T(8,128)S(4)} %get-tuple-element.23.counts, bf16[1664,128]{1,0:T(8,128)(2,1)S(1)} %get-tuple-element.24.windows, bf16[2,8,4,2,128,128]{5,4,3,2,1,0:T(8,128)(2,1)S(1)} %get-tuple-element.25.tiles), custom_call_target="tpu_custom_call" | custom-call | flops 268435456 | bytes 2097152 | tf_op jit(solution)/shard_map/project/pallas_call | solution.py:295
  9.8 0.0 copy-start.1
  9.8 0.4 collective-permute-done
  10.2 1.1 %add.14 = f32[8,2,128,128]{3,2,1,0:T(8,128)} add(f32[8,2,128,128]{3,2,1,0:T(8,128)S(1)} %project.1, f32[8,2,128,128]{3,2,1,0:T(8,128)S(1)} %collective-permute-done) | non-fusion elementwise | flops 262144 | bytes 3145728 | tf_op jit(solution)/shard_map/add | solution.py:389
  11.3 6.8 %all-to-all-start = ((f32[8,2,128,128]{3,2,1,0:T(8,128)}), f32[8,2,128,128]{3,2,1,0:T(8,128)S(1)}, u32[]{:S(2)}, u32[]{:S(2)}) async-start(f32[8,2,128,128]{3,2,1,0:T(8,128)} %add.14), calls=%async_computation | async-start | bytes 2097152 | tf_op jit(solution)/shard_map/all_to_all | solution.py:391
  18.1 0.0 copy-done
  18.1 0.1 copy.7
  18.2 4.2 %collective-permute-start.2 = (bf16[8,1,2048]{2,0,1:T(8,128)(2,1)S(1)}, bf16[8,1,2048]{2,0,1:T(8,128)(2,1)S(1)}, u32[]{:S(2)}, u32[]{:S(2)}) collective-permute-start(bf16[8,1,2048]{2,0,1:T(8,128)(2,1)S(1)} %get-tuple-element.46), channel_id=1, source_target_pairs={{0,1},{1,2},{2,3},{3,4},{4,5},{5,6},{6,7},{7,8},{8,9},{9,10},{10,1... | collective-permute-start | bytes 98312 | tf_op jit(solution)/shard_map/ppermute | solution.py:33
  22.4 0.7 collective-permute-start.1
  23.1 1.9 %collective-permute-start.3 = (bf16[8,1,2048]{2,0,1:T(8,128)(2,1)S(1)}, bf16[8,1,2048]{2,0,1:T(8,128)(2,1)S(1)}, u32[]{:S(2)}, u32[]{:S(2)}) collective-permute-start(bf16[8,1,2048]{2,0,1:T(8,128)(2,1)S(1)} %get-tuple-element.48), channel_id=1, source_target_pairs={{1,0},{2,1},{3,2},{4,3},{5,4},{6,5},{7,6},{8,7},{9,8},{10,9},{11,1... | collective-permute-start | bytes 98312 | tf_op jit(solution)/shard_map/ppermute | solution.py:33
  25.0 13.4 %collective-permute-done.2 = bf16[8,1,2048]{2,0,1:T(8,128)(2,1)S(1)} collective-permute-done((bf16[8,1,2048]{2,0,1:T(8,128)(2,1)S(1)}, bf16[8,1,2048]{2,0,1:T(8,128)(2,1)S(1)}, u32[]{:S(2)}, u32[]{:S(2)}) %collective-permute-start.2) | collective-permute-done | bytes 32800 | tf_op jit(solution)/shard_map/ppermute | solution.py:33
  38.5 0.0 collective-permute-done.1
  38.5 5.6 %collective-permute-done.3 = bf16[8,1,2048]{2,0,1:T(8,128)(2,1)S(1)} collective-permute-done((bf16[8,1,2048]{2,0,1:T(8,128)(2,1)S(1)}, bf16[8,1,2048]{2,0,1:T(8,128)(2,1)S(1)}, u32[]{:S(2)}, u32[]{:S(2)}) %collective-permute-start.3) | collective-permute-done | bytes 32800 | tf_op jit(solution)/shard_map/ppermute | solution.py:33
  44.1 3.3 %all-to-all-done = f32[8,2,128,128]{3,2,1,0:T(8,128)S(1)} async-done(((f32[8,2,128,128]{3,2,1,0:T(8,128)}), f32[8,2,128,128]{3,2,1,0:T(8,128)S(1)}, u32[]{:S(2)}, u32[]{:S(2)}) %all-to-all-start) | async-done | bytes 1048608 | tf_op jit(solution)/shard_map/all_to_all | solution.py:391
  47.4 0.1 reduce_sum.9
  47.4 0.0 copy-done.1
  47.4 0.1 select_subtract_fusion
  47.5 14.0 %collective-permute-start.4 = (f32[2,128,128]{2,1,0:T(8,128)S(1)}, f32[2,128,128]{2,1,0:T(8,128)S(1)}, u32[]{:S(2)}, u32[]{:S(2)}) collective-permute-start(f32[2,128,128]{2,1,0:T(8,128)S(1)} %select_subtract_fusion), channel_id=1, source_target_pairs={{0,16},{16,0},{1,17},{17,1},{2,18},{18,2},{3,19},{19,3},{4,20},{20... | collective-permute-start | bytes 393224 | tf_op jit(solution)/shard_map/ppermute | solution.py:366
  61.5 8.9 %collective-permute-done.4 = f32[2,128,128]{2,1,0:T(8,128)S(1)} collective-permute-done((f32[2,128,128]{2,1,0:T(8,128)S(1)}, f32[2,128,128]{2,1,0:T(8,128)S(1)}, u32[]{:S(2)}, u32[]{:S(2)}) %collective-permute-start.4) | collective-permute-done | bytes 131104 | tf_op jit(solution)/shard_map/ppermute | solution.py:366
  70.4 0.1 fusion.2
  70.5 0.9 broadcast_in_dim.35
  71.4 3.5 %all-to-all-start.1 = ((bf16[8,2,128,128]{3,2,1,0:T(8,128)(2,1)}), bf16[8,2,128,128]{3,2,1,0:T(8,128)(2,1)S(1)}, u32[]{:S(2)}, u32[]{:S(2)}) async-start(bf16[8,2,128,128]{3,2,1,0:T(8,128)(2,1)} %broadcast_in_dim.35), calls=%async_computation.1 | async-start | bytes 1048576 | tf_op jit(solution)/shard_map/all_to_all | solution.py:401
  74.9 0.1 fusion.3
  75.0 1.9 %collective-permute-start.5 = (bf16[1,6,2048]{2,0,1:T(2,128)(2,1)S(1)}, bf16[1,6,2048]{2,0,1:T(2,128)(2,1)S(1)}, u32[]{:S(2)}, u32[]{:S(2)}) collective-permute-start(bf16[1,6,2048]{2,0,1:T(2,128)(2,1)S(1)} %get-tuple-element.44), channel_id=1, source_target_pairs={{0,32},{32,64},{64,96},{96,128},{128,160},{160,192},{192,224},{224... | collective-permute-start | bytes 73736 | tf_op jit(solution)/shard_map/ppermute | solution.py:43
  76.9 3.4 %collective-permute-start.6 = (bf16[1,6,2048]{2,0,1:T(2,128)(2,1)S(1)}, bf16[1,6,2048]{2,0,1:T(2,128)(2,1)S(1)}, u32[]{:S(2)}, u32[]{:S(2)}) collective-permute-start(bf16[1,6,2048]{2,0,1:T(2,128)(2,1)S(1)} %get-tuple-element.45), channel_id=1, source_target_pairs={{32,0},{64,32},{96,64},{128,96},{160,128},{192,160},{224,192},{256... | collective-permute-start | bytes 73736 | tf_op jit(solution)/shard_map/ppermute | solution.py:43
  80.3 0.0 collective-permute-done.5
  80.3 3.9 %collective-permute-done.6 = bf16[1,6,2048]{2,0,1:T(2,128)(2,1)S(1)} collective-permute-done((bf16[1,6,2048]{2,0,1:T(2,128)(2,1)S(1)}, bf16[1,6,2048]{2,0,1:T(2,128)(2,1)S(1)}, u32[]{:S(2)}, u32[]{:S(2)}) %collective-permute-start.6) | collective-permute-done | bytes 24608 | tf_op jit(solution)/shard_map/ppermute | solution.py:43
  84.2 0.2 fusion.1
  84.3 0.1 maximum_bitcast_fusion.field
  84.4 1.2 %own_view.1 = f32[1,8,2048]{2,1,0:T(8,128)} custom-call(s32[3]{0:T(128)S(1)} %pad_add_fusion.place, f32[2,128,128]{2,1,0:T(8,128)S(1)} %get-tuple-element.41.both), custom_call_target="tpu_custom_call" | custom-call | bytes 131072 | tf_op jit(solution)/shard_map/own_view/pallas_call | solution.py:354
  85.6 6.3 %all-to-all-done.1.views = bf16[8,2,128,128]{3,2,1,0:T(8,128)(2,1)S(1)} async-done(((bf16[8,2,128,128]{3,2,1,0:T(8,128)(2,1)}), bf16[8,2,128,128]{3,2,1,0:T(8,128)(2,1)S(1)}, u32[]{:S(2)}, u32[]{:S(2)}) %all-to-all-start.1) | async-done | bytes 524320 | tf_op jit(solution)/shard_map/all_to_all | solution.py:401
  91.9 3.3 %collective-permute-start.7 = (bf16[8,2,128,128]{3,2,1,0:T(8,128)(2,1)S(1)}, bf16[8,2,128,128]{3,2,1,0:T(8,128)(2,1)S(1)}, u32[]{:S(2)}, u32[]{:S(2)}) collective-permute-start(bf16[8,2,128,128]{3,2,1,0:T(8,128)(2,1)S(1)} %all-to-all-done.1.views), channel_id=1, source_target_pairs={{0,1},{1,0},{2,3},{3,2},{4,5},{5,4},{6,7},{7,6},{8,9},{9,8},{10,11... | collective-permute-start | bytes 1572872 | tf_op jit(solution)/shard_map/ppermute | solution.py:366
  95.2 4.4 %load_spread.1 = (f32[4,128,128]{2,1,0:T(8,128)S(1)}, bf16[2,8,4,2,128,128]{5,4,3,2,1,0:T(8,128)(2,1)S(1)}, f32[4,128,128]{2,1,0:T(8,128)S(1)}) custom-call(s32[3]{0:T(128)S(1)} %pad_add_fusion.place, s32[32,128]{1,0:T(8,128)S(4)} %get-tuple-element.22.offsets, s32[32,128]{1,0:T(8,128)S(4)} %get-tuple-element.23.counts, ...), custom_call_target="tpu_custom_call" | custom-call | flops 536870912 | bytes 4194304 | tf_op jit(solution)/shard_map/load_spread/pallas_call | solution.py:309
  99.6 0.0 collective-permute-done.7.views
  99.6 2.7 %spread.1 = f32[8,4,2048]{2,1,0:T(4,128)} custom-call(s32[3]{0:T(128)S(1)} %pad_add_fusion.place, s32[32,128]{1,0:T(8,128)S(4)} %get-tuple-element.22.offsets, s32[32,128]{1,0:T(8,128)S(4)} %get-tuple-element.23.counts, bf16[8,2,128,128]{3,2,1,0:T(8,128)(2,1)S(1)} %collective-permute-done.7.views, ...), custom_call_target="tpu_custom_call" | custom-call | flops 268435456 | bytes 2097152 | tf_op jit(solution)/shard_map/spread/pallas_call | solution.py:332
  (4 shorter events, 0.1 us)
Async XLA Ops:
  5.3 4.9 %collective-permute-start = (f32[8,2,128,128]{3,2,1,0:T(8,128)S(1)}, f32[8,2,128,128]{3,2,1,0:T(8,128)S(1)}, u32[]{:S(2)}, u32[]{:S(2)}) collective-permute-start(f32[8,2,128,128]{3,2,1,0:T(8,128)S(1)} %get-tuple-element.26), channel_id=1, source_target_pairs={{0,1},{1,0},{2,3},{3,2},{4,5},{5,4},{6,7},{7,6},{8,9},{9,8},{10,11... | collective-permute-start | bytes 3145736 | tf_op jit(solution)/shard_map/ppermute | solution.py:366
  7.9 10.2 %copy-start = (bf16[8,4,2048]{2,1,0:T(4,128)(2,1)S(1)}, bf16[8,4,2048]{2,1,0:T(4,128)(2,1)}, u32[]{:S(2)}) copy-start(bf16[8,4,2048]{2,1,0:T(4,128)(2,1)} %volume_hbm.1) | copy-start | bytes 393220
  9.8 37.6 %copy-start.1 = (f32[1,8,2048]{2,1,0:T(8,128)S(1)}, f32[1,8,2048]{2,1,0:T(8,128)}, u32[]{:S(2)}) copy-start(f32[1,8,2048]{2,1,0:T(8,128)} %param.6) | copy-start | bytes 196612
  11.3 36.1 %all-to-all-start = ((f32[8,2,128,128]{3,2,1,0:T(8,128)}), f32[8,2,128,128]{3,2,1,0:T(8,128)S(1)}, u32[]{:S(2)}, u32[]{:S(2)}) async-start(f32[8,2,128,128]{3,2,1,0:T(8,128)} %add.14), calls=%async_computation | async-start | bytes 2097152 | tf_op jit(solution)/shard_map/all_to_all | solution.py:391
  18.2 20.2 %collective-permute-start.2 = (bf16[8,1,2048]{2,0,1:T(8,128)(2,1)S(1)}, bf16[8,1,2048]{2,0,1:T(8,128)(2,1)S(1)}, u32[]{:S(2)}, u32[]{:S(2)}) collective-permute-start(bf16[8,1,2048]{2,0,1:T(8,128)(2,1)S(1)} %get-tuple-element.46), channel_id=1, source_target_pairs={{0,1},{1,2},{2,3},{3,4},{4,5},{5,6},{6,7},{7,8},{8,9},{9,10},{10,1... | collective-permute-start | bytes 98312 | tf_op jit(solution)/shard_map/ppermute | solution.py:33
  22.4 16.0 %collective-permute-start.1 = (bf16[8,1,2048]{2,0,1:T(8,128)(2,1)S(1)}, bf16[8,1,2048]{2,0,1:T(8,128)(2,1)S(1)}, u32[]{:S(2)}, u32[]{:S(2)}) collective-permute-start(bf16[8,1,2048]{2,0,1:T(8,128)(2,1)S(1)} %get-tuple-element.47), channel_id=1, source_target_pairs={{15,16},{16,15},{47,48},{48,47},{79,80},{80,79},{111,112},{112,111... | collective-permute-start | bytes 98312 | tf_op jit(solution)/shard_map/ppermute | solution.py:34
  23.1 20.9 %collective-permute-start.3 = (bf16[8,1,2048]{2,0,1:T(8,128)(2,1)S(1)}, bf16[8,1,2048]{2,0,1:T(8,128)(2,1)S(1)}, u32[]{:S(2)}, u32[]{:S(2)}) collective-permute-start(bf16[8,1,2048]{2,0,1:T(8,128)(2,1)S(1)} %get-tuple-element.48), channel_id=1, source_target_pairs={{1,0},{2,1},{3,2},{4,3},{5,4},{6,5},{7,6},{8,7},{9,8},{10,9},{11,1... | collective-permute-start | bytes 98312 | tf_op jit(solution)/shard_map/ppermute | solution.py:33
  47.5 22.9 %collective-permute-start.4 = (f32[2,128,128]{2,1,0:T(8,128)S(1)}, f32[2,128,128]{2,1,0:T(8,128)S(1)}, u32[]{:S(2)}, u32[]{:S(2)}) collective-permute-start(f32[2,128,128]{2,1,0:T(8,128)S(1)} %select_subtract_fusion), channel_id=1, source_target_pairs={{0,16},{16,0},{1,17},{17,1},{2,18},{18,2},{3,19},{19,3},{4,20},{20... | collective-permute-start | bytes 393224 | tf_op jit(solution)/shard_map/ppermute | solution.py:366
  71.4 20.5 %all-to-all-start.1 = ((bf16[8,2,128,128]{3,2,1,0:T(8,128)(2,1)}), bf16[8,2,128,128]{3,2,1,0:T(8,128)(2,1)S(1)}, u32[]{:S(2)}, u32[]{:S(2)}) async-start(bf16[8,2,128,128]{3,2,1,0:T(8,128)(2,1)} %broadcast_in_dim.35), calls=%async_computation.1 | async-start | bytes 1048576 | tf_op jit(solution)/shard_map/all_to_all | solution.py:401
  75.0 5.3 %collective-permute-start.5 = (bf16[1,6,2048]{2,0,1:T(2,128)(2,1)S(1)}, bf16[1,6,2048]{2,0,1:T(2,128)(2,1)S(1)}, u32[]{:S(2)}, u32[]{:S(2)}) collective-permute-start(bf16[1,6,2048]{2,0,1:T(2,128)(2,1)S(1)} %get-tuple-element.44), channel_id=1, source_target_pairs={{0,32},{32,64},{64,96},{96,128},{128,160},{160,192},{192,224},{224... | collective-permute-start | bytes 73736 | tf_op jit(solution)/shard_map/ppermute | solution.py:43
  76.9 7.2 %collective-permute-start.6 = (bf16[1,6,2048]{2,0,1:T(2,128)(2,1)S(1)}, bf16[1,6,2048]{2,0,1:T(2,128)(2,1)S(1)}, u32[]{:S(2)}, u32[]{:S(2)}) collective-permute-start(bf16[1,6,2048]{2,0,1:T(2,128)(2,1)S(1)} %get-tuple-element.45), channel_id=1, source_target_pairs={{32,0},{64,32},{96,64},{128,96},{160,128},{192,160},{224,192},{256... | collective-permute-start | bytes 73736 | tf_op jit(solution)/shard_map/ppermute | solution.py:43
  91.9 7.7 %collective-permute-start.7 = (bf16[8,2,128,128]{3,2,1,0:T(8,128)(2,1)S(1)}, bf16[8,2,128,128]{3,2,1,0:T(8,128)(2,1)S(1)}, u32[]{:S(2)}, u32[]{:S(2)}) collective-permute-start(bf16[8,2,128,128]{3,2,1,0:T(8,128)(2,1)S(1)} %all-to-all-done.1.views), channel_id=1, source_target_pairs={{0,1},{1,0},{2,3},{3,2},{4,5},{5,4},{6,7},{7,6},{8,9},{9,8},{10,11... | collective-permute-start | bytes 1572872 | tf_op jit(solution)/shard_map/ppermute | solution.py:366

commit v8 on v7

--- a/solution.py
+++ b/solution.py
@@ -29,12 +29,12 @@
     size = lax.axis_size(ANGLE)
     gap = size // ZHI - 1
     up, down = shifts_of(size, gap)
-    last, first = edges(shard, 1)
+    last, first = (edge[:, 0] for edge in edges(shard, 1))
     before, after = lax.ppermute(last, ANGLE, up), lax.ppermute(first, ANGLE, down)
     across = lax.ppermute(jnp.where(ends_plane, last, first), ANGLE, [(gap, gap + 1), (gap + 1, gap)])
     before = jnp.where(begins_plane, across, before)
     after = jnp.where(ends_plane, across, after)
-    return jnp.concatenate([before, shard, after], axis=1)
+    return jnp.concatenate([before[:, None], shard, after[:, None]], axis=1)
 
 
 def with_slab_neighbours(shard):

time: 103 us -> 103 us (level)
  no operation moved by 1% of the time
where the time goes in v8:
time: 103 us; the launch traced here: 102 us
  starting transfers between devices  42.2 us (41%)
  waiting for transfers between devices  41.7 us (40%)
  Pallas kernels  14.8 us (14%)
  other arithmetic  1.71 us (2%)
  local copies, waits for them, and re-layouts  1.08 us (1%)
    ppermute x3, starting transfers between devices, swap(): return lax.ppermute(array, axis, [(0, 1), (1, 0)])  19.8 us
    ppermute x1, waiting for transfers between devices, with_row_neighbours(): lax.ppermute(last, ANGLE, up)  13.4 us
    ppermute x3, waiting for transfers between devices, swap(): return lax.ppermute(array, axis, [(0, 1), (1, 0)])  9.28 us
    all_to_all x1, starting transfers between devices, per_device(): parts = lax.all_to_all(pair, 'y', 0, 0, tiled=True)  6.82 us
    all_to_all x1, waiting for transfers between devices, per_device(): views = lax.all_to_all(copies, 'y', 0, 0, tiled=True)  6.3 us
    ppermute x1, waiting for transfers between devices, with_row_neighbours(): lax.ppermute(first, ANGLE, down)  5.41 us
    pallas_call x1, Pallas kernels, load_project(): pl.pallas_call(load_project_kernel, in_specs=[SMEM, ANY, ANY, ANY, ANY],...  4.59 us
    pallas_call x1, Pallas kernels, load_spread(): pl.pallas_call(load_spread_kernel, in_specs=[SMEM, SMEM, SMEM, VMEM, VMEM...  4.43 us
  transfers between devices with their start and end apart: 10, of which 7 were waited for; matrix products, arithmetic and copies ran while one was open for 0% of the time, Pallas kernels for 7%

profile of v8, /device:TPU:71, one launch (start us, length us, event | category | flops | bytes accessed | tf_op | source)
XLA Modules:
  0.0 102.4 jit_solution(4297193382029135914)
XLA Ops:
  0.7 0.1 pad_add_fusion.place
  0.7 4.6 %load_project.1 = (f32[8,2,128,128]{3,2,1,0:T(8,128)S(1)}, bf16[2,8,4,2,128,128]{5,4,3,2,1,0:T(8,128)(2,1)S(1)}, bf16[1664,128]{1,0:T(8,128)(2,1)S(1)}, s32[32,128]{1,0:T(8,128)S(4)}, s32[32,128]{1,0:T(8,128)S(4)}) custom-call(s32[3]{0:T(128)S(1)} %pad_add_fusion.place, s32[32,128]{1,0:T(8,128)} %offsets_hbm.1, s32[32,128]{1,0:T(8,128)} %counts_hbm.1, ...), custom_call_target="tpu_custom_call" | custom-call | flops 536870912 | bytes 4194304 | tf_op jit(solution)/shard_map/load_project/pallas_call | solution.py:271
  5.3 2.6 %collective-permute-start = (f32[8,2,128,128]{3,2,1,0:T(8,128)S(1)}, f32[8,2,128,128]{3,2,1,0:T(8,128)S(1)}, u32[]{:S(2)}, u32[]{:S(2)}) collective-permute-start(f32[8,2,128,128]{3,2,1,0:T(8,128)S(1)} %get-tuple-element.26), channel_id=1, source_target_pairs={{0,1},{1,0},{2,3},{3,2},{4,5},{5,4},{6,7},{7,6},{8,9},{9,8},{10,11... | collective-permute-start | bytes 3145736 | tf_op jit(solution)/shard_map/ppermute | solution.py:366
  7.9 0.0 copy-start
  7.9 1.9 %project.1 = f32[8,2,128,128]{3,2,1,0:T(8,128)S(1)} custom-call(s32[3]{0:T(128)S(1)} %pad_add_fusion.place, s32[32,128]{1,0:T(8,128)S(4)} %get-tuple-element.22.offsets, s32[32,128]{1,0:T(8,128)S(4)} %get-tuple-element.23.counts, bf16[1664,128]{1,0:T(8,128)(2,1)S(1)} %get-tuple-element.24.windows, bf16[2,8,4,2,128,128]{5,4,3,2,1,0:T(8,128)(2,1)S(1)} %get-tuple-element.25.tiles), custom_call_target="tpu_custom_call" | custom-call | flops 268435456 | bytes 2097152 | tf_op jit(solution)/shard_map/project/pallas_call | solution.py:295
  9.8 0.0 copy-start.1
  9.8 0.4 collective-permute-done
  10.2 1.1 %add.14 = f32[8,2,128,128]{3,2,1,0:T(8,128)} add(f32[8,2,128,128]{3,2,1,0:T(8,128)S(1)} %project.1, f32[8,2,128,128]{3,2,1,0:T(8,128)S(1)} %collective-permute-done) | non-fusion elementwise | flops 262144 | bytes 3145728 | tf_op jit(solution)/shard_map/add | solution.py:389
  11.3 6.8 %all-to-all-start = ((f32[8,2,128,128]{3,2,1,0:T(8,128)}), f32[8,2,128,128]{3,2,1,0:T(8,128)S(1)}, u32[]{:S(2)}, u32[]{:S(2)}) async-start(f32[8,2,128,128]{3,2,1,0:T(8,128)} %add.14), calls=%async_computation | async-start | bytes 2097152 | tf_op jit(solution)/shard_map/all_to_all | solution.py:391
  18.1 0.0 copy-done
  18.1 0.1 copy.7
  18.2 0.7 collective-permute-start.1
  18.9 4.2 %collective-permute-start.2 = (bf16[8,2048]{1,0:T(8,128)(2,1)S(1)}, bf16[8,2048]{1,0:T(8,128)(2,1)S(1)}, u32[]{:S(2)}, u32[]{:S(2)}) collective-permute-start(bf16[8,2048]{1,0:T(8,128)(2,1)S(1)} %get-tuple-element.46), channel_id=1, source_target_pairs={{0,1},{1,2},{2,3},{3,4},{4,5},{5,6},{6,7},{7,8},{8,9},{9,10},{10,1... | collective-permute-start | bytes 98312 | tf_op jit(solution)/shard_map/ppermute | solution.py:33
  23.1 1.9 %collective-permute-start.3 = (bf16[8,2048]{1,0:T(8,128)(2,1)S(1)}, bf16[8,2048]{1,0:T(8,128)(2,1)S(1)}, u32[]{:S(2)}, u32[]{:S(2)}) collective-permute-start(bf16[8,2048]{1,0:T(8,128)(2,1)S(1)} %get-tuple-element.47), channel_id=1, source_target_pairs={{1,0},{2,1},{3,2},{4,3},{5,4},{6,5},{7,6},{8,7},{9,8},{10,9},{11,1... | collective-permute-start | bytes 98312 | tf_op jit(solution)/shard_map/ppermute | solution.py:33
  25.0 0.0 collective-permute-done.1
  25.0 13.4 %collective-permute-done.2 = bf16[8,2048]{1,0:T(8,128)(2,1)S(1)} collective-permute-done((bf16[8,2048]{1,0:T(8,128)(2,1)S(1)}, bf16[8,2048]{1,0:T(8,128)(2,1)S(1)}, u32[]{:S(2)}, u32[]{:S(2)}) %collective-permute-start.2) | collective-permute-done | bytes 32800 | tf_op jit(solution)/shard_map/ppermute | solution.py:33
  38.4 5.4 %collective-permute-done.3 = bf16[8,2048]{1,0:T(8,128)(2,1)S(1)} collective-permute-done((bf16[8,2048]{1,0:T(8,128)(2,1)S(1)}, bf16[8,2048]{1,0:T(8,128)(2,1)S(1)}, u32[]{:S(2)}, u32[]{:S(2)}) %collective-permute-start.3) | collective-permute-done | bytes 32800 | tf_op jit(solution)/shard_map/ppermute | solution.py:33
  43.9 3.5 %all-to-all-done = f32[8,2,128,128]{3,2,1,0:T(8,128)S(1)} async-done(((f32[8,2,128,128]{3,2,1,0:T(8,128)}), f32[8,2,128,128]{3,2,1,0:T(8,128)S(1)}, u32[]{:S(2)}, u32[]{:S(2)}) %all-to-all-start) | async-done | bytes 1048608 | tf_op jit(solution)/shard_map/all_to_all | solution.py:391
  47.4 0.1 reduce_sum.9
  47.4 0.0 copy-done.1
  47.4 0.1 select_subtract_fusion
  47.5 14.0 %collective-permute-start.4 = (f32[2,128,128]{2,1,0:T(8,128)S(1)}, f32[2,128,128]{2,1,0:T(8,128)S(1)}, u32[]{:S(2)}, u32[]{:S(2)}) collective-permute-start(f32[2,128,128]{2,1,0:T(8,128)S(1)} %select_subtract_fusion), channel_id=1, source_target_pairs={{0,16},{16,0},{1,17},{17,1},{2,18},{18,2},{3,19},{19,3},{4,20},{20... | collective-permute-start | bytes 393224 | tf_op jit(solution)/shard_map/ppermute | solution.py:366
  61.5 8.9 %collective-permute-done.4 = f32[2,128,128]{2,1,0:T(8,128)S(1)} collective-permute-done((f32[2,128,128]{2,1,0:T(8,128)S(1)}, f32[2,128,128]{2,1,0:T(8,128)S(1)}, u32[]{:S(2)}, u32[]{:S(2)}) %collective-permute-start.4) | collective-permute-done | bytes 131104 | tf_op jit(solution)/shard_map/ppermute | solution.py:366
  70.4 0.1 fusion.2
  70.5 0.9 broadcast_in_dim.43
  71.4 3.5 %all-to-all-start.1 = ((bf16[8,2,128,128]{3,2,1,0:T(8,128)(2,1)}), bf16[8,2,128,128]{3,2,1,0:T(8,128)(2,1)S(1)}, u32[]{:S(2)}, u32[]{:S(2)}) async-start(bf16[8,2,128,128]{3,2,1,0:T(8,128)(2,1)} %broadcast_in_dim.43), calls=%async_computation.1 | async-start | bytes 1048576 | tf_op jit(solution)/shard_map/all_to_all | solution.py:401
  74.9 0.1 fusion.3
  75.0 1.9 %collective-permute-start.5 = (bf16[1,6,2048]{2,0,1:T(2,128)(2,1)S(1)}, bf16[1,6,2048]{2,0,1:T(2,128)(2,1)S(1)}, u32[]{:S(2)}, u32[]{:S(2)}) collective-permute-start(bf16[1,6,2048]{2,0,1:T(2,128)(2,1)S(1)} %get-tuple-element.44), channel_id=1, source_target_pairs={{0,32},{32,64},{64,96},{96,128},{128,160},{160,192},{192,224},{224... | collective-permute-start | bytes 73736 | tf_op jit(solution)/shard_map/ppermute | solution.py:43
  76.9 3.4 %collective-permute-start.6 = (bf16[1,6,2048]{2,0,1:T(2,128)(2,1)S(1)}, bf16[1,6,2048]{2,0,1:T(2,128)(2,1)S(1)}, u32[]{:S(2)}, u32[]{:S(2)}) collective-permute-start(bf16[1,6,2048]{2,0,1:T(2,128)(2,1)S(1)} %get-tuple-element.45), channel_id=1, source_target_pairs={{32,0},{64,32},{96,64},{128,96},{160,128},{192,160},{224,192},{256... | collective-permute-start | bytes 73736 | tf_op jit(solution)/shard_map/ppermute | solution.py:43
  80.3 0.0 collective-permute-done.5
  80.3 3.9 %collective-permute-done.6 = bf16[1,6,2048]{2,0,1:T(2,128)(2,1)S(1)} collective-permute-done((bf16[1,6,2048]{2,0,1:T(2,128)(2,1)S(1)}, bf16[1,6,2048]{2,0,1:T(2,128)(2,1)S(1)}, u32[]{:S(2)}, u32[]{:S(2)}) %collective-permute-start.6) | collective-permute-done | bytes 24608 | tf_op jit(solution)/shard_map/ppermute | solution.py:43
  84.2 0.2 fusion.1
  84.3 0.1 maximum_bitcast_fusion.field
  84.4 1.2 %own_view.1 = f32[1,8,2048]{2,1,0:T(8,128)} custom-call(s32[3]{0:T(128)S(1)} %pad_add_fusion.place, f32[2,128,128]{2,1,0:T(8,128)S(1)} %get-tuple-element.41.both), custom_call_target="tpu_custom_call" | custom-call | bytes 131072 | tf_op jit(solution)/shard_map/own_view/pallas_call | solution.py:354
  85.6 6.3 %all-to-all-done.1.views = bf16[8,2,128,128]{3,2,1,0:T(8,128)(2,1)S(1)} async-done(((bf16[8,2,128,128]{3,2,1,0:T(8,128)(2,1)}), bf16[8,2,128,128]{3,2,1,0:T(8,128)(2,1)S(1)}, u32[]{:S(2)}, u32[]{:S(2)}) %all-to-all-start.1) | async-done | bytes 524320 | tf_op jit(solution)/shard_map/all_to_all | solution.py:401
  91.9 3.3 %collective-permute-start.7 = (bf16[8,2,128,128]{3,2,1,0:T(8,128)(2,1)S(1)}, bf16[8,2,128,128]{3,2,1,0:T(8,128)(2,1)S(1)}, u32[]{:S(2)}, u32[]{:S(2)}) collective-permute-start(bf16[8,2,128,128]{3,2,1,0:T(8,128)(2,1)S(1)} %all-to-all-done.1.views), channel_id=1, source_target_pairs={{0,1},{1,0},{2,3},{3,2},{4,5},{5,4},{6,7},{7,6},{8,9},{9,8},{10,11... | collective-permute-start | bytes 1572872 | tf_op jit(solution)/shard_map/ppermute | solution.py:366
  95.2 4.4 %load_spread.1 = (f32[4,128,128]{2,1,0:T(8,128)S(1)}, bf16[2,8,4,2,128,128]{5,4,3,2,1,0:T(8,128)(2,1)S(1)}, f32[4,128,128]{2,1,0:T(8,128)S(1)}) custom-call(s32[3]{0:T(128)S(1)} %pad_add_fusion.place, s32[32,128]{1,0:T(8,128)S(4)} %get-tuple-element.22.offsets, s32[32,128]{1,0:T(8,128)S(4)} %get-tuple-element.23.counts, ...), custom_call_target="tpu_custom_call" | custom-call | flops 536870912 | bytes 4194304 | tf_op jit(solution)/shard_map/load_spread/pallas_call | solution.py:309
  99.6 0.0 collective-permute-done.7.views
  99.6 2.7 %spread.1 = f32[8,4,2048]{2,1,0:T(4,128)} custom-call(s32[3]{0:T(128)S(1)} %pad_add_fusion.place, s32[32,128]{1,0:T(8,128)S(4)} %get-tuple-element.22.offsets, s32[32,128]{1,0:T(8,128)S(4)} %get-tuple-element.23.counts, bf16[8,2,128,128]{3,2,1,0:T(8,128)(2,1)S(1)} %collective-permute-done.7.views, ...), custom_call_target="tpu_custom_call" | custom-call | flops 268435456 | bytes 2097152 | tf_op jit(solution)/shard_map/spread/pallas_call | solution.py:332
  (5 shorter events, 0.1 us)
Async XLA Ops:
  5.3 4.9 %collective-permute-start = (f32[8,2,128,128]{3,2,1,0:T(8,128)S(1)}, f32[8,2,128,128]{3,2,1,0:T(8,128)S(1)}, u32[]{:S(2)}, u32[]{:S(2)}) collective-permute-start(f32[8,2,128,128]{3,2,1,0:T(8,128)S(1)} %get-tuple-element.26), channel_id=1, source_target_pairs={{0,1},{1,0},{2,3},{3,2},{4,5},{5,4},{6,7},{7,6},{8,9},{9,8},{10,11... | collective-permute-start | bytes 3145736 | tf_op jit(solution)/shard_map/ppermute | solution.py:366
  7.9 10.2 %copy-start = (bf16[8,4,2048]{2,1,0:T(4,128)(2,1)S(1)}, bf16[8,4,2048]{2,1,0:T(4,128)(2,1)}, u32[]{:S(2)}) copy-start(bf16[8,4,2048]{2,1,0:T(4,128)(2,1)} %volume_hbm.1) | copy-start | bytes 393220
  9.8 37.6 %copy-start.1 = (f32[1,8,2048]{2,1,0:T(8,128)S(1)}, f32[1,8,2048]{2,1,0:T(8,128)}, u32[]{:S(2)}) copy-start(f32[1,8,2048]{2,1,0:T(8,128)} %param.6) | copy-start | bytes 196612
  11.3 36.1 %all-to-all-start = ((f32[8,2,128,128]{3,2,1,0:T(8,128)}), f32[8,2,128,128]{3,2,1,0:T(8,128)S(1)}, u32[]{:S(2)}, u32[]{:S(2)}) async-start(f32[8,2,128,128]{3,2,1,0:T(8,128)} %add.14), calls=%async_computation | async-start | bytes 2097152 | tf_op jit(solution)/shard_map/all_to_all | solution.py:391
  18.2 6.8 %collective-permute-start.1 = (bf16[8,2048]{1,0:T(8,128)(2,1)S(1)}, bf16[8,2048]{1,0:T(8,128)(2,1)S(1)}, u32[]{:S(2)}, u32[]{:S(2)}) collective-permute-start(bf16[8,2048]{1,0:T(8,128)(2,1)S(1)} %broadcast_select_fusion), channel_id=1, source_target_pairs={{15,16},{16,15},{47,48},{48,47},{79,80},{80,79},{111,112},{112,111... | collective-permute-start | bytes 98312 | tf_op jit(solution)/shard_map/ppermute | solution.py:34
  18.9 19.5 %collective-permute-start.2 = (bf16[8,2048]{1,0:T(8,128)(2,1)S(1)}, bf16[8,2048]{1,0:T(8,128)(2,1)S(1)}, u32[]{:S(2)}, u32[]{:S(2)}) collective-permute-start(bf16[8,2048]{1,0:T(8,128)(2,1)S(1)} %get-tuple-element.46), channel_id=1, source_target_pairs={{0,1},{1,2},{2,3},{3,4},{4,5},{5,6},{6,7},{7,8},{8,9},{9,10},{10,1... | collective-permute-start | bytes 98312 | tf_op jit(solution)/shard_map/ppermute | solution.py:33
  23.1 20.8 %collective-permute-start.3 = (bf16[8,2048]{1,0:T(8,128)(2,1)S(1)}, bf16[8,2048]{1,0:T(8,128)(2,1)S(1)}, u32[]{:S(2)}, u32[]{:S(2)}) collective-permute-start(bf16[8,2048]{1,0:T(8,128)(2,1)S(1)} %get-tuple-element.47), channel_id=1, source_target_pairs={{1,0},{2,1},{3,2},{4,3},{5,4},{6,5},{7,6},{8,7},{9,8},{10,9},{11,1... | collective-permute-start | bytes 98312 | tf_op jit(solution)/shard_map/ppermute | solution.py:33
  47.5 22.9 %collective-permute-start.4 = (f32[2,128,128]{2,1,0:T(8,128)S(1)}, f32[2,128,128]{2,1,0:T(8,128)S(1)}, u32[]{:S(2)}, u32[]{:S(2)}) collective-permute-start(f32[2,128,128]{2,1,0:T(8,128)S(1)} %select_subtract_fusion), channel_id=1, source_target_pairs={{0,16},{16,0},{1,17},{17,1},{2,18},{18,2},{3,19},{19,3},{4,20},{20... | collective-permute-start | bytes 393224 | tf_op jit(solution)/shard_map/ppermute | solution.py:366
  71.4 20.5 %all-to-all-start.1 = ((bf16[8,2,128,128]{3,2,1,0:T(8,128)(2,1)}), bf16[8,2,128,128]{3,2,1,0:T(8,128)(2,1)S(1)}, u32[]{:S(2)}, u32[]{:S(2)}) async-start(bf16[8,2,128,128]{3,2,1,0:T(8,128)(2,1)} %broadcast_in_dim.43), calls=%async_computation.1 | async-start | bytes 1048576 | tf_op jit(solution)/shard_map/all_to_all | solution.py:401
  75.0 5.3 %collective-permute-start.5 = (bf16[1,6,2048]{2,0,1:T(2,128)(2,1)S(1)}, bf16[1,6,2048]{2,0,1:T(2,128)(2,1)S(1)}, u32[]{:S(2)}, u32[]{:S(2)}) collective-permute-start(bf16[1,6,2048]{2,0,1:T(2,128)(2,1)S(1)} %get-tuple-element.44), channel_id=1, source_target_pairs={{0,32},{32,64},{64,96},{96,128},{128,160},{160,192},{192,224},{224... | collective-permute-start | bytes 73736 | tf_op jit(solution)/shard_map/ppermute | solution.py:43
  76.9 7.2 %collective-permute-start.6 = (bf16[1,6,2048]{2,0,1:T(2,128)(2,1)S(1)}, bf16[1,6,2048]{2,0,1:T(2,128)(2,1)S(1)}, u32[]{:S(2)}, u32[]{:S(2)}) collective-permute-start(bf16[1,6,2048]{2,0,1:T(2,128)(2,1)S(1)} %get-tuple-element.45), channel_id=1, source_target_pairs={{32,0},{64,32},{96,64},{128,96},{160,128},{192,160},{224,192},{256... | collective-permute-start | bytes 73736 | tf_op jit(solution)/shard_map/ppermute | solution.py:43
  91.9 7.7 %collective-permute-start.7 = (bf16[8,2,128,128]{3,2,1,0:T(8,128)(2,1)S(1)}, bf16[8,2,128,128]{3,2,1,0:T(8,128)(2,1)S(1)}, u32[]{:S(2)}, u32[]{:S(2)}) collective-permute-start(bf16[8,2,128,128]{3,2,1,0:T(8,128)(2,1)S(1)} %all-to-all-done.1.views), channel_id=1, source_target_pairs={{0,1},{1,0},{2,3},{3,2},{4,5},{5,4},{6,7},{7,6},{8,9},{9,8},{10,11... | collective-permute-start | bytes 1572872 | tf_op jit(solution)/shard_map/ppermute | solution.py:366
